TPU v7x, 32 devices: a whole 2x2x4 slice. The times are simulated.
32 devices in a mesh: ctx: 8 (over z, x), head: 4 (over y, core).
Axes of the slice: x: 2, y: 2, z: 4, core: 2. Of those that a mesh axis runs over, the one named last changes fastest.
Arguments:
- mixer_x: bfloat16 [1024, 16384], P('ctx', 'head'), may hold values from -6 to 6
- mixer_bc: bfloat16 [1024, 256], P('ctx'), may hold values from -6 to 6
- dt_raw: float32 [1024, 256], P('ctx', 'head'), may hold values from -4 to 4
- gate_z: bfloat16 [1024, 16384], P('ctx', 'head'), may hold values from -6 to 6
- conv_weight_x: float32 [4, 16384], P(None, 'head'), may hold values from -3 to 3
- conv_bias_x: float32 [16384], P('head'), may hold values from -3 to 3
- conv_weight_bc: float32 [4, 256], replicated, may hold values from -3 to 3
- conv_bias_bc: float32 [256], replicated, may hold values from -3 to 3
- a_log: float32 [256], P('head'), may hold values from -6 to 1
- dt_bias: float32 [256], P('head'), may hold values from -7 to -4
- skip_d: float32 [256], P('head'), may hold values from 0.5 to 2
- d_mixer: bfloat16 [1024, 16384], P('ctx', 'head'), may hold values from -6 to 6
- doc_lengths: int32 [8], replicated, may hold values from 1 to 512, 1024 in all
- att_queries: bfloat16 [1024, 8192], P('ctx', 'head'), may hold values from -144 to 144
- att_keys: bfloat16 [1024, 1024], P('ctx', 'head'), may hold values from -6 to 6
- att_values: bfloat16 [1024, 1024], P('ctx', 'head'), may hold values from -6 to 6
- d_attn: bfloat16 [1024, 8192], P('ctx', 'head'), may hold values from -6 to 6
Outputs:
- grad_mixer_x: bfloat16 [1024, 16384], P('ctx', 'head')
- grad_mixer_bc: bfloat16 [1024, 256], P('ctx')
- grad_dt_raw: float32 [1024, 256], P('ctx', 'head')
- grad_gate_z: bfloat16 [1024, 16384], P('ctx', 'head')
- grad_conv_weight_x: float32 [4, 16384], P(None, 'head')
- grad_conv_bias_x: float32 [16384], P('head')
- grad_conv_weight_bc: float32 [4, 256], replicated
- grad_conv_bias_bc: float32 [256], replicated
- grad_a_log: float32 [256], P('head')
- grad_dt_bias: float32 [256], P('head')
- grad_skip_d: float32 [256], P('head')
- grad_queries: bfloat16 [1024, 8192], P('ctx', 'head')
- grad_keys: bfloat16 [1024, 1024], P('ctx', 'head')
- grad_values: bfloat16 [1024, 1024], P('ctx', 'head')
Inputs may be any that keep to these rules, and one draw needn't show every extreme that they name: `doc_lengths`: lengths of 8 documents packed in order, summing to 1024; the longest is exactly 512.
All inputs are finite; a program needn't handle non-finite values.
Results may differ from a plain program's by a relative error of at most 0.0051.
Values may be sent and summed in bfloat16 or wider, within the bound.
No kernel may reach another device: no remote copies, remote signals or barrier semaphores. Data moves between devices by JAX's collectives and lax.ppermute only.
A program may use at most 192 MiB of HBM per device.

v0:
```python
from functools import partial
import math

import jax
import jax.numpy as jnp
from jax import lax
from jax.sharding import PartitionSpec as P

MP = 64
NS = 128
KC = 4
AH = 64
KVH = 8
HD = 128


FILL_SCORE = -1e30
HIGHEST = lax.Precision.HIGHEST


def shifted(value, axis, steps):
    count = lax.axis_size(axis)
    initial, last = (max(0, -steps), min(count, count - steps))
    return lax.ppermute(value, axis, [(source, source + steps) for source in range(initial, last)])


def entering(value, axis, combine, identity, reverse):
    size, place = (lax.axis_size(axis), lax.axis_index(axis))
    everything = jax.tree.map(lambda part: lax.all_gather(part, axis), value)
    start = jax.tree.map(
        lambda part, zero: jnp.broadcast_to(jnp.asarray(zero, part.dtype), part.shape),
        value,
        identity,
    )

    def turn(k, before):
        at = size - 1 - k if reverse else k
        reached = at > place if reverse else at < place
        new = combine(before, jax.tree.map(lambda part: part[at], everything))
        return jax.tree.map(lambda a, b: jnp.where(reached, a, b), new, before)

    return lax.fori_loop(0, size, turn, start)


def doc_index(positions, doc_lengths):
    ends = jnp.cumsum(doc_lengths)
    return jnp.sum((ends[None, :] <= positions[:, None]).astype(jnp.int32), axis=1)


def conv_silu(padded, weight, bias_row, seg_pad, row_count):
    seg_now = seg_pad[KC - 1 :]
    summed = jnp.broadcast_to(bias_row[None, :], (row_count, bias_row.shape[0]))
    for tap_index in range(KC):
        offset = KC - 1 - tap_index
        lagged = padded[offset : offset + row_count]
        same_doc = (seg_pad[offset : offset + row_count] == seg_now).astype(jnp.float32)
        summed = summed + weight[tap_index][None, :] * lagged * same_doc[:, None]
    return jax.nn.silu(summed)


def ssd_scan(inputs_x, steps_dt, decay_log, b_in, c_out, seg_now, seg_start):
    row_count, head_count, head_width = inputs_x.shape
    block_rows = min(128, row_count)
    block_count = row_count // block_rows

    def by_block(array):
        return array.reshape((block_count, block_rows) + array.shape[1:])

    causal = jnp.arange(block_rows)[:, None] >= jnp.arange(block_rows)[None, :]

    def advance(carried, pieces):
        running, seg_before = carried
        xblock, dtblock, ablock, bblock, cblock, sblock = pieces
        cum_log = jnp.cumsum(ablock, axis=0)
        heads_cum = cum_log.T
        allowed = causal & (sblock[:, None] == sblock[None, :])
        log_gaps = heads_cum[:, :, None] - heads_cum[:, None, :]
        within = jnp.exp(jnp.where(allowed[None], log_gaps, FILL_SCORE))
        c_dot_b = jnp.dot(cblock, bblock.T, precision=HIGHEST)
        weighted = dtblock[:, :, None] * xblock
        within_sum = jnp.einsum("hts,shp->thp", within * c_dot_b[None], weighted, precision=HIGHEST)
        entry_block = jnp.exp(cum_log) * (sblock == seg_before).astype(jnp.float32)[:, None]
        from_state = (
            jnp.einsum("tn,hpn->thp", cblock, running, precision=HIGHEST) * entry_block[:, :, None]
        )
        last_log = cum_log[-1]
        seg_last = sblock[-1]
        leaving = (
            jnp.exp(last_log[None, :] - cum_log) * (sblock == seg_last).astype(jnp.float32)[:, None]
        )
        kept_share = jnp.exp(last_log) * (seg_last == seg_before).astype(jnp.float32)
        added_state = jnp.einsum(
            "shp,sn->hpn", leaving[:, :, None] * weighted, bblock, precision=HIGHEST
        )
        return (
            (running * kept_share[:, None, None] + added_state, seg_last),
            within_sum + from_state,
        )

    start_state = (jnp.zeros((head_count, head_width, b_in.shape[1]), jnp.float32), seg_start)
    pieces = (
        by_block(inputs_x),
        by_block(steps_dt),
        by_block(decay_log),
        by_block(b_in),
        by_block(c_out),
        by_block(seg_now),
    )
    (last_state, seg_final), outputs = lax.scan(advance, start_state, pieces)
    return (outputs.reshape(row_count, head_count, head_width), last_state)


def mixer_front(
    raw_x,
    raw_bc,
    margin,
    dt_raw,
    weight_x,
    bias_x,
    weight_bc,
    bias_bc,
    a_log,
    dt_bias,
    skip_d,
    seg_pad,
    seg_start,
):
    row_count, channels = raw_x.shape
    seg_now = seg_pad[KC - 1 :]
    conv_x = conv_silu(
        jnp.concatenate([margin[:, :channels], raw_x], axis=0), weight_x, bias_x, seg_pad, row_count
    )
    conv_bc = conv_silu(
        jnp.concatenate([margin[:, channels:], raw_bc], axis=0),
        weight_bc,
        bias_bc,
        seg_pad,
        row_count,
    )
    b_in = conv_bc[:, :NS]
    c_out = conv_bc[:, NS:]
    steps_dt = jax.nn.softplus(dt_raw + dt_bias[None, :])
    decay_log = -steps_dt * jnp.exp(a_log)[None, :]
    inputs_x = conv_x.reshape(row_count, channels // MP, MP)
    within_sum, last_state = ssd_scan(
        inputs_x, steps_dt, decay_log, b_in, c_out, seg_now, seg_start
    )
    ungated = within_sum + skip_d[None, :, None] * inputs_x
    entry_decay = (
        jnp.exp(jnp.cumsum(decay_log, axis=0)) * (seg_now == seg_start).astype(jnp.float32)[:, None]
    )
    return (ungated, last_state, entry_decay[-1], c_out, entry_decay)


def mixer_gate(ungated, c_out, entry_decay, gate_value, incoming):
    from_before = (
        jnp.einsum("tn,hpn->thp", c_out, incoming, precision=HIGHEST) * entry_decay[:, :, None]
    )
    summed = (ungated + from_before).reshape(ungated.shape[0], -1)
    return summed * jax.nn.silu(gate_value)


def compose(earlier_part, later_part):
    return (
        earlier_part[0] * later_part[0],
        later_part[0][:, None, None] * earlier_part[1] + later_part[1],
    )


def mixer_grads(
    mixer_x,
    mixer_bc,
    dt_raw,
    gate_z,
    conv_weight_x,
    conv_bias_x,
    conv_weight_bc,
    conv_bias_bc,
    a_log,
    dt_bias,
    skip_d,
    d_mixer,
    doc_lengths,
):
    row_count, channels = mixer_x.shape
    first_pos = lax.axis_index("ctx") * row_count
    positions = first_pos + jnp.arange(-(KC - 1), row_count, dtype=jnp.int32)
    seg_pad = doc_index(positions, doc_lengths)
    seg_start = seg_pad[KC - 2]
    tail_rows = jnp.concatenate(
        [mixer_x[row_count - (KC - 1) :], mixer_bc[row_count - (KC - 1) :]], axis=1
    )
    margin = shifted(tail_rows, "ctx", 1).astype(jnp.float32)
    front = partial(mixer_front, seg_pad=seg_pad, seg_start=seg_start)
    front_out, front_pullback = jax.vjp(
        front,
        mixer_x.astype(jnp.float32),
        mixer_bc.astype(jnp.float32),
        margin,
        dt_raw,
        conv_weight_x,
        conv_bias_x,
        conv_weight_bc,
        conv_bias_bc,
        a_log,
        dt_bias,
        skip_d,
    )
    ungated, last_state, decay_total, c_out, entry_decay = front_out
    identity = (jnp.ones_like(decay_total), jnp.zeros_like(last_state))
    incoming = entering((decay_total, last_state), "ctx", compose, identity, False)[1]
    gated_out, gate_pullback = jax.vjp(
        mixer_gate, ungated, c_out, entry_decay, gate_z.astype(jnp.float32), incoming
    )
    grad_ungated, grad_cout, grad_entry, grad_gate, grad_incoming = gate_pullback(
        d_mixer.astype(jnp.float32)
    )
    from_later = entering((decay_total, grad_incoming), "ctx", compose, identity, True)[1]
    grad_decay = jnp.sum(from_later * incoming, axis=(1, 2))
    grad_parts = front_pullback((grad_ungated, from_later, grad_decay, grad_cout, grad_entry))
    bc_grad, bc_margin, weight_bc_grad, bias_bc_grad = lax.psum(
        (grad_parts[1], grad_parts[2][:, channels:], grad_parts[6], grad_parts[7]), "head"
    )
    margin_grad = jnp.concatenate([grad_parts[2][:, :channels], bc_margin], axis=1)
    from_next = shifted(margin_grad, "ctx", -1)
    lead_rows = row_count - (KC - 1)
    grad_x = grad_parts[0] + jnp.pad(from_next[:, :channels], ((lead_rows, 0), (0, 0)))
    grad_bc = bc_grad + jnp.pad(from_next[:, channels:], ((lead_rows, 0), (0, 0)))
    summed = lax.psum(
        (
            grad_parts[4],
            grad_parts[5],
            weight_bc_grad,
            bias_bc_grad,
            grad_parts[8],
            grad_parts[9],
            grad_parts[10],
        ),
        "ctx",
    )
    return (
        grad_x.astype(jnp.bfloat16),
        grad_bc.astype(jnp.bfloat16),
        grad_parts[3],
        grad_gate.astype(jnp.bfloat16),
    ) + tuple(summed)


def attention_grads(att_queries, att_keys, att_values, d_attn, doc_lengths):
    row_count = att_queries.shape[0]
    kv_count = att_keys.shape[1] // HD
    group_size = AH // KVH
    inv_root = 1.0 / math.sqrt(HD)
    all_keys, all_values = (
        lax.all_gather(att_keys, "ctx", axis=0, tiled=True),
        lax.all_gather(att_values, "ctx", axis=0, tiled=True),
    )
    token_count = all_keys.shape[0]
    span_rows = min(512, token_count)
    block_count = token_count // span_rows
    first_pos = lax.axis_index("ctx") * row_count
    query_pos = first_pos + jnp.arange(row_count, dtype=jnp.int32)
    query_seg = doc_index(query_pos, doc_lengths)
    key_pos = jnp.arange(token_count, dtype=jnp.int32)
    key_seg = doc_index(key_pos, doc_lengths)
    query_heads = att_queries.reshape(row_count, kv_count, group_size, HD)
    grad_heads = d_attn.reshape(row_count, kv_count, group_size, HD)
    blocked = (
        all_keys.reshape(block_count, span_rows, kv_count, HD),
        all_values.reshape(block_count, span_rows, kv_count, HD),
        key_pos.reshape(block_count, span_rows),
        key_seg.reshape(block_count, span_rows),
    )

    def masked_scores(key_block, pos_block, seg_block):
        raw_scores = (
            jnp.einsum("lgjd,kgd->lgjk", query_heads, key_block, preferred_element_type=jnp.float32)
            * inv_root
        )
        allowed = (pos_block[None, :] <= query_pos[:, None]) & (
            seg_block[None, :] == query_seg[:, None]
        )
        return jnp.where(allowed[:, None, None, :], raw_scores, FILL_SCORE)

    def forward_step(running, pieces):
        key_block, value_block, pos_block, seg_block = pieces
        run_max, run_sum, run_acc = running
        scores = masked_scores(key_block, pos_block, seg_block)
        new_max = jnp.maximum(run_max, jnp.max(scores, axis=-1))
        rescale = jnp.exp(run_max - new_max)
        weights = jnp.exp(scores - new_max[..., None])
        new_sum = run_sum * rescale + jnp.sum(weights, axis=-1)
        new_acc = run_acc * rescale[..., None] + jnp.einsum(
            "lgjk,kgd->lgjd", weights, value_block.astype(jnp.float32), precision=HIGHEST
        )
        return ((new_max, new_sum, new_acc), None)

    start_stats = (
        jnp.full((row_count, kv_count, group_size), FILL_SCORE, jnp.float32),
        jnp.zeros((row_count, kv_count, group_size), jnp.float32),
        jnp.zeros((row_count, kv_count, group_size, HD), jnp.float32),
    )
    (row_max, row_sum, row_acc), no_output = lax.scan(forward_step, start_stats, blocked)
    attended = row_acc / row_sum[..., None]
    row_delta = jnp.sum(grad_heads.astype(jnp.float32) * attended, axis=-1)

    def backward_step(grad_query, pieces):
        key_block, value_block, pos_block, seg_block = pieces
        scores = masked_scores(key_block, pos_block, seg_block)
        softmax = jnp.exp(scores - row_max[..., None]) / row_sum[..., None]
        grad_prob = jnp.einsum(
            "lgjd,kgd->lgjk", grad_heads, value_block, preferred_element_type=jnp.float32
        )
        grad_score = (softmax * (grad_prob - row_delta[..., None])).astype(jnp.bfloat16)
        updated = grad_query + jnp.einsum(
            "lgjk,kgd->lgjd", grad_score, key_block, preferred_element_type=jnp.float32
        )
        grad_key = jnp.einsum(
            "lgjk,lgjd->kgd", grad_score, query_heads, preferred_element_type=jnp.float32
        )
        grad_value = jnp.einsum(
            "lgjk,lgjd->kgd",
            softmax.astype(jnp.bfloat16),
            grad_heads,
            preferred_element_type=jnp.float32,
        )
        return (updated, (grad_key, grad_value))

    grad_query, key_terms = lax.scan(backward_step, jnp.zeros_like(attended), blocked)
    grad_queries = (
        (grad_query * inv_root).reshape(row_count, kv_count * group_size * HD).astype(jnp.bfloat16)
    )
    term_keys = key_terms[0].reshape(token_count, kv_count * HD) * inv_root
    term_values = key_terms[1].reshape(token_count, kv_count * HD)
    grad_keys, grad_values = (
        lax.psum_scatter(term_keys, "ctx", scatter_dimension=0, tiled=True),
        lax.psum_scatter(term_values, "ctx", scatter_dimension=0, tiled=True),
    )
    return (grad_queries, grad_keys.astype(jnp.bfloat16), grad_values.astype(jnp.bfloat16))


def body(
    mixer_x,
    mixer_bc,
    dt_raw,
    gate_z,
    conv_weight_x,
    conv_bias_x,
    conv_weight_bc,
    conv_bias_bc,
    a_log,
    dt_bias,
    skip_d,
    d_mixer,
    doc_lengths,
    att_queries,
    att_keys,
    att_values,
    d_attn,
):
    mixer_out = mixer_grads(
        mixer_x,
        mixer_bc,
        dt_raw,
        gate_z,
        conv_weight_x,
        conv_bias_x,
        conv_weight_bc,
        conv_bias_bc,
        a_log,
        dt_bias,
        skip_d,
        d_mixer,
        doc_lengths,
    )
    attention_out = attention_grads(att_queries, att_keys, att_values, d_attn, doc_lengths)
    return mixer_out + attention_out


def solution(mesh):
    placed = (
        P("ctx", "head"),
        P("ctx", None),
        P("ctx", "head"),
        P("ctx", "head"),
        P(None, "head"),
        P("head"),
        P(),
        P(),
        P("head"),
        P("head"),
        P("head"),
        P("ctx", "head"),
        P(),
        P("ctx", "head"),
        P("ctx", "head"),
        P("ctx", "head"),
        P("ctx", "head"),
    )
    return jax.shard_map(
        body,
        mesh=mesh,
        in_specs=placed,
        out_specs=(
            P("ctx", "head"),
            P("ctx", None),
            P("ctx", "head"),
            P("ctx", "head"),
            P(None, "head"),
            P("head"),
            P(),
            P(),
            P("head"),
            P("head"),
            P("head"),
            P("ctx", "head"),
            P("ctx", "head"),
            P("ctx", "head"),
        ),
        check_vma=False,
    )
```

profile of v0, /device:TPU:0, one launch (start us, length us, event | category | flops | bytes accessed | tf_op | source)
XLA Modules:
  0.0 896.9 jit_solution(16880902873905007535)
XLA Ops:
  8.4 33.2 %all_gather.27 = bf16[1024,256]{1,0:T(8,128)(2,1)S(1)} all-gather(bf16[128,256]{1,0:T(8,128)(2,1)} %param.39), channel_id=1, replica_groups=mesh['ctx'=8,'head'=4] {'ctx'}, dimensions={0}, use_global_device_ids=true | all-gather | bytes 589824 | tf_op jit(solution)/shard_map/all_gather | solution.py:255
  42.4 31.3 %all_gather.28 = bf16[1024,256]{1,0:T(8,128)(2,1)S(1)} all-gather(bf16[128,256]{1,0:T(8,128)(2,1)S(1)} %copy-done.40), channel_id=1, replica_groups=mesh['ctx'=8,'head'=4] {'ctx'}, dimensions={0}, use_global_device_ids=true | all-gather | bytes 589824 | tf_op jit(solution)/shard_map/all_gather | solution.py:256
  73.9 24.2 %while.40 = (s32[]{:T(128)}, f32[128,2,8]{0,2,1:T(8,128)S(1)}, f32[128,2,8]{0,2,1:T(8,128)S(1)}, f32[128,2,8,128]{0,3,2,1:T(8,128)}, s32[2,512]{1,0:T(2,128)S(1)...) while((s32[]{:T(128)}, f32[128,2,8]{0,2,1:T(8,128)S(1)}, ...), condition=%wide.region_49.50_spmd.clone, body=%wide.region_46.49_spmd.clone.sunk | while | flops 1890527360 | bytes 17184408 | solution.py:303
  74.1 2.7 fusion.199
  76.8 3.0 fusion.200
  80.2 5.6 fusion.202
  86.0 2.7 fusion.199
  88.7 3.0 fusion.200
  92.1 5.9 fusion.202
  100.0 22.0 %while.41 = (s32[]{:T(128)}, f32[128,2,8,128]{0,3,2,1:T(8,128)}, f32[2,512,2,128]{3,1,2,0:T(8,128)}, f32[2,512,2,128]{3,2,1,0:T(2,128)}, bf16[2,512,2,128]{3,1,2...) while((s32[]{:T(128)}, f32[128,2,8,128]{0,3,2,1:T(8,128)}, ...), condition=%wide.region_52.53_spmd.clone, body=%wide.region_51.52_spmd.clone.sunk | while | flops 1351286912 | bytes 76979112 | solution.py:329
  104.1 2.6 fusion.214
  114.9 2.9 fusion.214
  126.4 4.3 collective-permute-start
  140.8 5.4 multiply_reduce_fusion.1
  152.8 3.1 fusion.82
  157.9 3.2 fusion.80
  170.1 18.1 %all-gather.2 = f32[8,1,64]{2,1,0:T(1,128)S(1)} all-gather(f32[1,1,64]{2,1,0:T(1,128)S(1)} %bitcast.307), channel_id=1, replica_groups=mesh['ctx'=8,'head'=4] {'ctx'}, dimensions={0}, use_global_device_ids=true | all-gather | bytes 2304 | tf_op jit(solution)/shard_map/all_gather | solution.py:29
  190.5 5.2 fusion.103
  196.0 11.2 %fusion.47 = (f32[64,128]{1,0:T(8,128)}, f32[64,128]{1,0:T(8,128)}, f32[128,128]{1,0:T(8,128)S(1)}) fusion(f32[128,128]{1,0:T(8,128)S(1)} %fusion.137, f32[64,128]{1,0:T(8,128)S(1)} %copy-done.50, pred[128,128]{1,0:T(8,128)(4,1)S(1)} %fusion.134, f32[64,64,128]{2,1,0:T(8,128)S(1)} %bitcast.257, f32[128,64,64]{0,2,1:T(8,128)} %bitcast.261, ...), kind=kOutput, calls=%fused_computation.77 | convolution fusion | flops 815235072 | bytes 4472832 | tf_op jit(solution)/shard_map/transpose(jvp())/while/body/eval_jaxpr/hts,shp->thp/dot_general | solution.py:81
  208.8 48.6 %reduce-scatter.5.cloned.1.call-done = f32[128,256]{1,0:T(8,128)} async-done(((f32[1024,256]{1,0:T(8,128)}), f32[128,256]{1,0:T(8,128)}) %reduce-scatter.5.cloned.1.call-update) | async-done | bytes 131088 | tf_op jit(solution)/shard_map/reduce_scatter | solution.py:337
  258.9 226.8 %all-gather.8.cloned.1.call-done = f32[512,64,128]{2,1,0:T(8,128)} async-done(((f32[64,64,128]{2,1,0:T(8,128)}), f32[512,64,128]{2,1,0:T(8,128)}) %all-gather.8.cloned.1.call-update) | async-done | bytes 16777232 | tf_op jit(solution)/shard_map/all_gather | solution.py:29
  485.8 31.6 %while.19 = (s32[]{:T(128)}, f32[64,64,128]{2,1,0:T(8,128)}, s32[]{:T(128)}, f32[8,64]{1,0:T(8,128)S(1)}, f32[8,64,64,128]{3,2,1,0:T(8,128)}, /*index=5*/s32[]{:T(128)}, s32[]{:T(128)}) while((s32[]{:T(128)}, f32[64,64,128]{2,1,0:T(8,128)}, s32[]{:T(128)}, f32[8,64]{1,0:T(8,128)S(1)}, f32[8,64,64,128]{3,2,1,0:T(8,128)}, ...), condition=%wide.region_6.7_spmd.clone, body=%wide.region_5.6_spmd.clone.sunk | while | flops 2097156 | bytes 6292329 | solution.py:42
  485.8 3.3 fusion.196
  489.0 3.9 fusion.196
  492.9 4.7 fusion.196
  497.6 4.1 fusion.196
  501.7 3.9 fusion.196
  505.6 3.9 fusion.196
  509.5 3.9 fusion.196
  513.4 3.9 fusion.196
  517.4 195.9 %all-gather.6.cloned.1.call-done = f32[512,64,128]{2,1,0:T(8,128)} async-done(((f32[64,64,128]{2,1,0:T(8,128)}), f32[512,64,128]{2,1,0:T(8,128)}) %all-gather.6.cloned.1.call-update) | async-done | bytes 16777232 | tf_op jit(solution)/shard_map/all_gather | solution.py:29
  713.2 17.2 %while.18 = (s32[]{:T(128)}, f32[64,64,128]{2,1,0:T(8,128)S(1)}, s32[]{:T(128)}, f32[8,64]{1,0:T(8,128)S(1)}, f32[8,64,64,128]{3,2,1,0:T(8,128)}, /*index=5*/s32[]{:T(128)}, s32[]{:T(128)}, s32[]{:T(128)}, s32[]{:T(128)}) while((s32[]{:T(128)}, f32[64,64,128]{2,1,0:T(8,128)S(1)}, s32[]{:T(128)}, f32[8,64]{1,0:T(8,128)S(1)}, ...), condition=%wide.region_4.5_spmd.clone, body=%wide.region_3.4_spmd.clone.sunk | while | flops 2097160 | bytes 6292391 | solution.py:42
  715.4 2.1 fusion.195
  717.5 2.1 fusion.195
  719.6 2.1 fusion.195
  721.8 2.1 fusion.195
  723.9 2.1 fusion.195
  730.5 3.2 fusion.132
  734.8 3.2 fusion.128
  738.0 3.5 fusion.100
  741.6 3.6 fusion.96
  748.2 8.3 multiply_reduce_fusion.8
  758.6 8.3 fusion.60
  768.7 3.0 copy.189
  771.8 6.8 multiply_reduce_fusion.5
  785.0 6.1 all-reduce.25
  794.0 37.9 %all-reduce.24 = (f32[4096]{0:T(1024)}, f32[4,256]{1,0:T(4,128)}, f32[256]{0:T(256)}, f32[64]{0:T(128)}, f32[64]{0:T(128)}, /*index=5*/f32[64]{0:T(128)}) all-reduce(f32[4096]{0:T(1024)S(1)} %get-tuple-element.926, f32[4,256]{1,0:T(4,128)S(1)} %get-tuple-element.1018, ...), channel_id=1, replica_groups=mesh['ctx'=8,'head'=4] {'ctx'}, use_global_device_ids=true, to_apply=%region_27.28 | all-reduce | flops 5568 | bytes 44544 | tf_op jit(solution)/shard_map/psum | solution.py:229
  834.7 53.4 %all-reduce.31.cloned.1.call-done = f32[4,4096]{1,0:T(4,128)} async-done(((f32[4,4096]{1,0:T(4,128)}), f32[4,4096]{1,0:T(4,128)}) %all-reduce.31.cloned.1.call-update) | async-done | bytes 65552 | tf_op jit(solution)/shard_map/psum | solution.py:229
  (382 shorter events, 84.8 us)
Async XLA Ops:
  7.2 34.6 %copy-start.27 = (bf16[128,2048]{1,0:T(8,128)(2,1)S(1)}, bf16[128,2048]{1,0:T(8,128)(2,1)}, u32[]{:S(2)}) copy-start(bf16[128,2048]{1,0:T(8,128)(2,1)} %param.38) | copy-start | bytes 1572868
  7.2 200.0 %reduce-scatter.3.cloned.1.call-start = ((), (), s32[]{:S(2)}) async-start(), calls=%async_computation.4 | async-start | bytes 1179648 | tf_op jit(solution)/shard_map/reduce_scatter | solution.py:336
  73.8 24.2 %copy-start.28 = (bf16[128,2048]{1,0:T(8,128)(2,1)S(1)}, bf16[128,2048]{1,0:T(8,128)(2,1)}, u32[]{:S(2)}) copy-start(bf16[128,2048]{1,0:T(8,128)(2,1)} %param.41) | copy-start | bytes 1572868
  114.9 4.4 copy-start.1
  124.2 6.6 copy-start.23
  125.2 10.8 %copy-start.84 = (f32[4,256]{1,0:T(4,128)S(1)}, f32[4,256]{1,0:T(4,128)}, u32[]{:S(2)}) copy-start(f32[4,256]{1,0:T(4,128)} %param.31) | copy-start | bytes 12292
  125.2 11.4 %copy-start.43 = (f32[4,4096]{1,0:T(4,128)S(1)}, f32[4,4096]{1,0:T(4,128)}, u32[]{:S(2)}) copy-start(f32[4,4096]{1,0:T(4,128)} %param.29) | copy-start | bytes 196612
  125.2 12.1 %copy-start.47 = (f32[128,64]{0,1:T(8,128)S(1)}, f32[128,64]{0,1:T(8,128)}, u32[]{:S(2)}) copy-start(f32[128,64]{0,1:T(8,128)} %param.27) | copy-start | bytes 98308
  125.2 12.2 %copy-start.95 = (f32[64]{0:T(128)S(1)}, f32[64]{0:T(128)}, u32[]{:S(2)}) copy-start(f32[64]{0:T(128)} %param.33) | copy-start | bytes 772
  125.2 12.2 %copy-start.85 = (f32[64]{0:T(128)S(1)}, f32[64]{0:T(128)}, u32[]{:S(2)}) copy-start(f32[64]{0:T(128)} %param.34) | copy-start | bytes 772
  125.3 132.1 %reduce-scatter.5.cloned.1.call-start = ((), (), s32[]{:S(2)}) async-start(), calls=%async_computation.5 | async-start | bytes 1179648 | tf_op jit(solution)/shard_map/reduce_scatter | solution.py:337
  126.4 13.5 %collective-permute-start = (bf16[3,4352]{1,0:T(4,128)(2,1)}, bf16[3,4352]{1,0:T(4,128)(2,1)}, u32[]{:S(2)}, u32[]{:S(2)}) collective-permute-start(bf16[3,4352]{1,0:T(4,128)(2,1)} %pad_maximum_fusion.3), channel_id=1, source_target_pairs={{0,4},{4,8},{8,12},{12,16},{16,20},{20,24},{24,28},{1,5},{5,9},{9,... | collective-permute-start | bytes 78344 | tf_op jit(solution)/shard_map/ppermute | solution.py:24
  131.8 353.9 %all-gather.8.cloned.1.call-start = ((), (), s32[]{:S(2)}) async-start(), calls=%async_computation.7 | async-start | bytes 18874368 | tf_op jit(solution)/shard_map/all_gather | solution.py:29
  132.2 5.3 copy-start.64
  134.7 4.4 copy-start.75
  134.7 4.4 copy-start.77
  138.1 8.0 copy-start.26
  139.9 6.3 copy-start.10
  139.9 12.9 %copy-start.30 = (f32[128,64]{0,1:T(8,128)}, f32[128,64]{0,1:T(8,128)S(1)}, u32[]{:S(2)}) copy-start(f32[128,64]{0,1:T(8,128)S(1)} %copy.182) | copy-start | bytes 98308
  151.3 4.6 copy-start.13
  155.9 557.3 %all-gather.6.cloned.1.call-start = ((), (), s32[]{:S(2)}) async-start(), calls=%async_computation.6 | async-start | bytes 18874368 | tf_op jit(solution)/shard_map/all_gather | solution.py:29
  161.1 5.8 copy-start.7
  161.1 672.0 %all-reduce.29.cloned.1.call-start = ((), (), s32[]{:S(2)}) async-start(), calls=%async_computation.2 | async-start | bytes 262144 | tf_op jit(solution)/shard_map/psum | solution.py:221
  167.9 28.1 %copy-start.31 = (f32[128,64]{0,1:T(8,128)S(1)}, f32[128,64]{0,1:T(8,128)}, u32[]{:S(2)}) copy-start(f32[128,64]{0,1:T(8,128)} %copy-done.30) | copy-start | bytes 98308
  167.9 28.1 %copy-start.50 = (f32[64,128]{1,0:T(8,128)S(1)}, f32[64,128]{1,0:T(8,128)}, u32[]{:S(2)}) copy-start(f32[64,128]{1,0:T(8,128)} %copy.187) | copy-start | bytes 98308
  189.1 18.2 %copy-start.62 = (pred[128,128]{1,0:T(8,128)(4,1)}, pred[128,128]{1,0:T(8,128)(4,1)S(1)}, u32[]{:S(2)}) copy-start(pred[128,128]{1,0:T(8,128)(4,1)S(1)} %fusion.134) | copy-start | bytes 49156
  190.5 5.5 copy-start.4
  196.0 11.3 %copy-start.41 = (f32[128,128]{1,0:T(8,128)}, f32[128,128]{1,0:T(8,128)S(1)}, u32[]{:S(2)}) copy-start(f32[128,128]{1,0:T(8,128)S(1)} %fusion.137) | copy-start | bytes 196612
  741.6 5.2 copy-start.66
  741.6 5.1 copy-start.68
  741.6 5.1 copy-start.70
  741.6 5.1 copy-start.72
  748.2 8.3 copy-start.18
  771.8 6.9 copy-start.36
  771.8 6.9 copy-start.37
  771.8 6.9 copy-start.38
  780.6 4.3 copy-start.80
  780.6 4.3 copy-start.81
  780.6 4.3 copy-start.82
  780.7 4.3 copy-start.83
  780.7 4.3 copy-start.79
  780.7 11.7 %copy-start.25 = (f32[128,64]{1,0:T(8,128)S(1)}, f32[128,64]{1,0:T(8,128)}, u32[]{:S(2)}) copy-start(f32[128,64]{1,0:T(8,128)} %copy-done.24) | copy-start | bytes 98308
  780.7 11.7 %copy-start.86 = (f32[64]{0:T(128)S(1)}, f32[64]{0:T(128)}, u32[]{:S(2)}) copy-start(f32[64]{0:T(128)} %param.34) | copy-start | bytes 772
  780.7 11.7 %copy-start.88 = (f32[64]{0:T(128)S(1)}, f32[64]{0:T(128)}, u32[]{:S(2)}) copy-start(f32[64]{0:T(128)} %copy-done.87) | copy-start | bytes 772
  780.7 12.5 %copy-start.96 = (f32[64]{0:T(128)S(1)}, f32[64]{0:T(128)}, u32[]{:S(2)}) copy-start(f32[64]{0:T(128)} %param.33) | copy-start | bytes 772
  781.5 12.5 %copy-start.90 = (f32[64]{0:T(128)S(1)}, f32[64]{0:T(128)}, u32[]{:S(2)}) copy-start(f32[64]{0:T(128)} %reduce_sum.351) | copy-start | bytes 772
  784.9 103.3 %all-reduce.31.cloned.1.call-start = ((), (), s32[]{:S(2)}) async-start(), calls=%async_computation.3 | async-start | bytes 131072 | tf_op jit(solution)/shard_map/psum | solution.py:229
  791.1 40.8 %collective-permute-start.1 = (f32[3,4352]{1,0:T(4,128)S(1)}, f32[3,4352]{1,0:T(4,128)S(1)}, u32[]{:S(2)}, u32[]{:S(2)}) collective-permute-start(f32[3,4352]{1,0:T(4,128)S(1)} %pad_maximum_fusion.2), channel_id=1, source_target_pairs={{4,0},{8,4},{12,8},{16,12},{20,16},{24,20},{28,24},{5,1},{9,5},{13... | collective-permute-start | bytes 156680 | tf_op jit(solution)/shard_map/ppermute | solution.py:24
  (65 other events, 157.3 us)
Sparse Core Ops, SparseCore 0:
  125.4 65.3 reduce-scatter.2
  194.2 63.1 reduce-scatter.4
  259.5 226.2 all-gather.7
  487.7 225.4 all-gather.5
  785.0 29.9 all-reduce.28
  818.8 69.2 all-reduce.30
where the time goes:
time: 907 us; the launch traced here: 897 us
  waiting for transfers between devices  525 us (58%)
  blocking collectives  127 us (14%)
  other arithmetic  95.2 us (10%)
  matrix products  85.9 us (9%)
  local copies, waits for them, and re-layouts  40.1 us (4%)
  between operations  17.2 us (2%)
    all_gather x2, waiting for transfers between devices, entering(): everything = jax.tree.map(lambda part: lax.all_gather(part, axis), value)  423 us
    psum x1, waiting for transfers between devices, mixer_grads(): lax.psum((grad_parts[4], grad_parts[5], weight_bc_grad, bias_bc_grad, gra...  53.4 us
    reduce_scatter x1, waiting for transfers between devices, attention_grads(): lax.psum_scatter(term_values, 'ctx', scatter_dimension=0, tiled=True)  48.6 us
    select_n x16, other arithmetic, turn(): return jax.tree.map(lambda a, b: jnp.where(reached, a, b), new, before)  48.2 us
    psum x1, blocking collectives, mixer_grads(): lax.psum((grad_parts[4], grad_parts[5], weight_bc_grad, bias_bc_grad, gra...  37.9 us
    all_gather x1, blocking collectives, attention_grads(): lax.all_gather(att_keys, 'ctx', axis=0, tiled=True)  33.2 us
    all_gather x1, blocking collectives, attention_grads(): lax.all_gather(att_values, 'ctx', axis=0, tiled=True)  31.3 us
    dot_general x3, matrix products, advance(): jnp.einsum('hts,shp->thp', within * c_dot_b[None], weighted, precision=HI...  27.8 us
  transfers between devices with their start and end apart: 8, of which 4 were waited for; matrix products, arithmetic and copies ran while one was open for 10% of the time, Pallas kernels for 0%

commit v1 on v0

v1 whole, which is shorter than its diff:
```python
import math

import jax
import jax.numpy as jnp
from jax import lax
from jax.experimental import pallas as pl
from jax.experimental.pallas import tpu as pltpu
from jax.sharding import PartitionSpec as P


MP = 64
KC = 4
AH = 64
KVH = 8
HD = 128
RB = 128
FILL = -1e30
F32 = jnp.float32
BF16 = jnp.bfloat16
HIGHEST = lax.Precision.HIGHEST


def params(limit=56):
    return pltpu.CompilerParams(vmem_limit_bytes=limit * 1024 * 1024)


def shifted(value, axis, steps):
    count = lax.axis_size(axis)
    initial, last = (max(0, -steps), min(count, count - steps))
    return lax.ppermute(value, axis, [(source, source + steps) for source in range(initial, last)])


def crossed(value, axis, mask):
    count = lax.axis_size(axis)
    return lax.ppermute(value, axis, [(source, source ^ mask) for source in range(count)])


def dot(a, b, dims=((1,), (0,)), precision=None):
    return lax.dot_general(a, b, (dims, ((), ())), precision=precision, preferred_element_type=F32)


NN = ((1,), (0,))
NT = ((1,), (1,))
TN = ((0,), (0,))


def iota(shape, dim):
    return lax.broadcasted_iota(jnp.int32, shape, dim)


def doc_start(doc_ref, pos):
    end = jnp.int32(0)
    start = jnp.zeros_like(pos)
    for j in range(doc_ref.shape[0]):
        end = end + doc_ref[j]
        start = jnp.where(pos >= end, end, start)
    return start


def smem():
    return pl.BlockSpec(memory_space=pltpu.SMEM)


def vmem():
    return pl.BlockSpec(memory_space=pltpu.VMEM)


def attention_kernel(reach, idx_ref, doc_ref, q_ref, do_ref, *rest):
    nb = reach + 1
    kv_refs = rest[:nb]
    dq_ref = rest[nb]
    out_refs = rest[nb + 1 : 2 * nb + 1]
    k_ref, v_ref, kt_ref, mask_ref, qc_ref, dc_ref, p_ref, g_ref = rest[2 * nb + 1 :]
    group = AH // KVH
    kv_count = q_ref.shape[1] // (group * HD)
    inv_root = 1.0 / math.sqrt(HD)
    keys = nb * RB
    first = idx_ref[0] * RB
    q_pos = first + iota((8, RB), 1)
    q_start = doc_start(doc_ref, q_pos)[:1]
    k_pos = first - reach * RB + iota((keys, RB), 0)
    allowed = (k_pos <= q_pos[:1]) & (k_pos >= q_start)
    mask_ref[...] = jnp.where(allowed, 0.0, FILL)
    for kv in range(kv_count):
        for b in range(nb):
            k_ref[pl.ds(b * RB, RB), :] = kv_refs[b][:, pl.ds(kv * HD, HD)]
            v_ref[pl.ds(b * RB, RB), :] = kv_refs[b][:, pl.ds((kv_count + kv) * HD, HD)]
        kt_ref[...] = k_ref[...].astype(F32).T.astype(BF16)

        def head(h, carry):
            lanes = pl.ds(pl.multiple_of((kv * group + h) * HD, HD), HD)
            rows = pl.ds(pl.multiple_of(h * RB, RB), RB)
            q = q_ref[:, lanes]
            do = do_ref[:, lanes]
            qc_ref[rows, :] = q
            dc_ref[rows, :] = do
            scores = dot(k_ref[...], q, NT) * inv_root + mask_ref[...]
            top = jnp.max(scores, axis=0, keepdims=True)
            weights = jnp.exp(scores - top)
            softmax = weights * (1.0 / jnp.sum(weights, axis=0, keepdims=True))
            grad_prob = dot(v_ref[...], do, NT)
            delta = jnp.sum(softmax * grad_prob, axis=0, keepdims=True)
            grad_score = (softmax * (grad_prob - delta)).astype(BF16)
            p_ref[:, rows] = softmax.astype(BF16)
            g_ref[:, rows] = grad_score
            grad_q = dot(kt_ref[...], grad_score, NN) * inv_root
            dq_ref[:, lanes] = grad_q.T.astype(BF16)
            return carry

        lax.fori_loop(0, group, head, 0)
        grad_k = dot(g_ref[...], qc_ref[...], NN) * inv_root
        grad_v = dot(p_ref[...], dc_ref[...], NN)
        for b in range(nb):
            kind = out_refs[b].dtype
            rows = slice(b * RB, (b + 1) * RB)
            out_refs[b][:, pl.ds(kv * HD, HD)] = grad_k[rows].astype(kind)
            out_refs[b][:, pl.ds((kv_count + kv) * HD, HD)] = grad_v[rows].astype(kind)


def attention_call(idx, doc, queries, grads, blocks):
    nb = len(blocks)
    keys = nb * RB
    group = AH // KVH
    outs = [jax.ShapeDtypeStruct(queries.shape, BF16)]
    outs += [jax.ShapeDtypeStruct(blocks[0].shape, BF16)] * (nb - 1)
    outs += [jax.ShapeDtypeStruct(blocks[0].shape, F32)]
    return pl.pallas_call(
        lambda *refs: attention_kernel(nb - 1, *refs),
        out_shape=outs,
        in_specs=[smem(), smem()] + [vmem()] * (2 + nb),
        out_specs=[vmem()] * (1 + nb),
        scratch_shapes=[
            pltpu.VMEM((keys, HD), BF16),
            pltpu.VMEM((keys, HD), BF16),
            pltpu.VMEM((HD, keys), BF16),
            pltpu.VMEM((keys, RB), F32),
            pltpu.VMEM((group * RB, HD), BF16),
            pltpu.VMEM((group * RB, HD), BF16),
            pltpu.VMEM((keys, group * RB), BF16),
            pltpu.VMEM((keys, group * RB), BF16),
        ],
        compiler_params=params(),
        name="attention",
    )(idx, doc, queries, grads, *blocks)


def pack_kernel(n, idx_ref, x_ref, z_ref, d_ref, *outs):
    width = x_ref.shape[1] // n
    me = idx_ref[0]
    for m in range(n):
        lanes = pl.ds(pl.multiple_of((me ^ m) * width, 128), width)
        z = z_ref[:, lanes].astype(F32)
        grad = d_ref[:, lanes].astype(F32) * z * jax.nn.sigmoid(z)
        outs[m][:, :width] = x_ref[:, lanes]
        outs[m][:, width:] = grad.astype(BF16)


def pack_call(n, idx, mixer_x, gate_z, d_mixer):
    rows, channels = mixer_x.shape
    width = channels // n
    return pl.pallas_call(
        lambda *refs: pack_kernel(n, *refs),
        out_shape=[jax.ShapeDtypeStruct((rows, 2 * width), BF16)] * n,
        in_specs=[smem()] + [vmem()] * 3,
        out_specs=[vmem()] * n,
        compiler_params=params(),
        name="pack",
    )(idx, mixer_x, gate_z, d_mixer)


def unpack_kernel(n, hp, idx_ref, z_ref, d_ref, *refs):
    big = refs[:n]
    small = refs[n : 2 * n]
    gx_ref, gz_ref, gw_ref, ddt_ref, hv_ref = refs[2 * n :]
    width = z_ref.shape[1] // n
    pairs = width // 128
    me = idx_ref[0]
    for m in range(n):
        source = me ^ m
        lanes = pl.ds(pl.multiple_of(source * width, 128), width)
        gx_ref[:, lanes] = big[m][:, :width]
        z = z_ref[:, lanes].astype(F32)
        sig = jax.nn.sigmoid(z)
        y = big[m][:, width:].astype(F32)
        gz_ref[:, lanes] = (d_ref[:, lanes].astype(F32) * y * (sig * (1.0 + z * (1.0 - sig)))).astype(BF16)
        ddt_ref[pl.ds(pl.multiple_of(source * hp, 8), hp), :] = small[m][:hp, :]
        for p in range(pairs):
            part = pl.ds(pl.multiple_of(source * width + p * 128, 128), 128)
            gw_ref[:, part] = small[m][hp + 8 * p : hp + 8 * p + 8, :]
        at = hp + 8 * pairs + 16
        hv_ref[pl.ds(pl.multiple_of(source * hp, 8), hp), :128] = small[m][at : at + hp, :]
        hv_ref[pl.ds(pl.multiple_of(source * hp, 8), hp), 128:] = small[m][at + hp : at + 2 * hp, :]


def unpack_call(n, hp, idx, gate_z, d_mixer, big, small):
    rows, channels = gate_z.shape
    return pl.pallas_call(
        lambda *refs: unpack_kernel(n, hp, *refs),
        out_shape=[
            jax.ShapeDtypeStruct((rows, channels), BF16),
            jax.ShapeDtypeStruct((rows, channels), BF16),
            jax.ShapeDtypeStruct((8, channels), F32),
            jax.ShapeDtypeStruct((n * hp, 128), F32),
            jax.ShapeDtypeStruct((n * hp, 256), F32),
        ],
        in_specs=[smem()] + [vmem()] * (2 + 2 * n),
        out_specs=[vmem()] * 5,
        compiler_params=params(),
        name="unpack",
    )(idx, gate_z, d_mixer, *big, *small)


def by_sublane(value):
    return jnp.sum(value.reshape(value.shape[0] // 8, 8, value.shape[1]), axis=0)


def mixer_kernel(n, heads, hp, idx_ref, doc_ref, *refs):
    width = heads * MP
    pairs = width // 128
    wide = 2 - pairs % 2
    xd_in = refs[:n]
    bc_in = refs[n : 2 * n]
    dt_in = refs[2 * n : 3 * n]
    wx_ref, bx_ref, wbc_ref, bbc_ref, par_ref = refs[3 * n : 3 * n + 5]
    at = 3 * n + 5
    big_out = refs[at : at + n]
    bc_out = refs[at + n : at + 2 * n]
    small_out = refs[at + 2 * n : at + 3 * n]
    (
        xd_ref,
        od_ref,
        raw_ref,
        og_ref,
        off_ref,
        xs_ref,
        gp_ref,
        bb_ref,
        cc_ref,
        bt_ref,
        ct_ref,
        cb_ref,
        bias_ref,
        dcb_ref,
        db_ref,
        dc_ref,
        step_ref,
        cum_ref,
        sg_ref,
        z1_ref,
        z2_ref,
        sin_ref,
        yn_ref,
        dwi_ref,
        lv_ref,
        st_ref,
        xc_ref,
        ds_ref,
        ed_ref,
        k_ref,
        acc_ref,
    ) = refs[at + 3 * n :]
    me = idx_ref[0]
    tokens = n * RB
    lane = iota((RB, 128), 1)
    sub = iota((RB, 128), 0)
    low = lane < MP
    zero8 = jnp.zeros((8, 128), F32)

    def rows_of(c, extra=0):
        return pl.ds(pl.multiple_of(c * RB, RB), RB + extra)

    upper = (sub <= lane).astype(F32)
    e_log = jnp.exp(par_ref[0])
    for m in range(n):
        source = me ^ m
        rows = rows_of(source)
        xd_ref[rows, :] = xd_in[m][...]
        raw_ref[pl.ds(pl.multiple_of(source * RB + 8, 8), RB), :] = bc_in[m][...].astype(F32)
        logit = dt_in[m][...] + par_ref[1]
        tail = jnp.exp(-jnp.abs(logit))
        step = jnp.maximum(logit, 0.0) + jnp.log1p(tail)
        step_ref[source] = step
        sg_ref[source] = jax.nn.sigmoid(logit)
        cum_ref[source] = dot(-step * e_log, upper, NN, HIGHEST)
        z1_ref[source] = jnp.zeros((hp, 128), F32)
        z2_ref[source] = jnp.zeros((hp, 128), F32)
        dcb_ref[source] = jnp.zeros((RB, RB), F32)
        db_ref[source] = jnp.zeros((RB, 128), F32)
        dc_ref[source] = jnp.zeros((RB, 128), F32)
    raw_ref[:8, :] = jnp.zeros((8, 256), F32)
    for u in range(wide):
        xs_ref[u, :8, :] = zero8
        for j in range(KC - 1):
            gp_ref[u, j, tokens:, :] = zero8
    off_ref[tokens:, :] = jnp.zeros((8, 128), jnp.int32)

    def conv(c, src_ref, lanes, weight, bias):
        off = off_ref[rows_of(c), :]
        window = src_ref[rows_of(c, 8), lanes]
        lags = [window[8:]]
        for j in range(1, KC):
            lags.append(jnp.where(off >= j, window[8 - j : 8 + RB - j], 0.0))
        pre = bias
        for j in range(KC):
            pre = pre + weight[j : j + 1] * lags[j]
        return pre, lags

    def conv_back(c, grad, src_ref, lanes, weight, u):
        off = off_ref[rows_of(c), :]
        window = src_ref[rows_of(c, 8), lanes]
        back = weight[0:1] * grad
        sums = [by_sublane(grad * window[8:])]
        for j in range(1, KC):
            held_back = jnp.where(off >= j, grad, 0.0)
            sums.append(by_sublane(held_back * window[8 - j : 8 + RB - j]))
            gp_ref[u, j - 1, rows_of(c), :] = held_back
            back = back + weight[j : j + 1] * gp_ref[u, j - 1, rows_of(c, 8), :][j : j + RB]
        sums.append(by_sublane(grad))
        return back, sums

    def silu_parts(pre):
        sig = jax.nn.sigmoid(pre)
        return pre * sig, sig * (1.0 + pre * (1.0 - sig))

    wbc = wbc_ref[...]
    bbc = bbc_ref[...]

    def prepare(c, carry):
        pos = c * RB + sub
        off = pos - doc_start(doc_ref, pos)
        off_ref[rows_of(c), :] = off
        allowed = (lane <= sub) & (sub - lane <= off)
        bias_ref[c] = jnp.where(allowed, 0.0, FILL)
        pre_b, unused = conv(c, raw_ref, slice(0, 128), wbc[:, :128], bbc[:, :128])
        pre_c, unused = conv(c, raw_ref, slice(128, 256), wbc[:, 128:], bbc[:, 128:])
        b_in = silu_parts(pre_b)[0]
        c_out = silu_parts(pre_c)[0]
        b_low, c_low = b_in.astype(BF16), c_out.astype(BF16)
        bb_ref[rows_of(c), :] = b_low
        cc_ref[rows_of(c), :] = c_low
        bt_ref[c] = b_in.T.astype(BF16)
        ct_ref[c] = c_out.T.astype(BF16)
        cb_ref[c] = dot(c_low, b_low, NT)
        return carry

    lax.fori_loop(0, n, prepare, 0)

    def streams(block, carry):
        ids = [block * wide + u for u in range(wide)]
        each = range(wide)
        lanes = [pl.ds(pl.multiple_of(p * 128, 128), 128) for p in ids]
        lanes_d = [pl.ds(pl.multiple_of(width + p * 128, 128), 128) for p in ids]
        held = [pl.ds(pl.multiple_of(me * width + p * 128, 128), 128) for p in ids]
        weight = [wx_ref[:, h] for h in held]
        bias = [bx_ref[:, h] for h in held]
        skip = [
            jnp.where(low[:1], par_ref[2, pl.ds(2 * p, 1), :], par_ref[2, pl.ds(2 * p + 1, 1), :]) for p in ids
        ]
        pick = [
            jnp.where(iota((hp, 128), 0) == 2 * p + iota((hp, 128), 1) // MP, 1.0, 0.0).astype(BF16) for p in ids
        ]

        def load(c, unused):
            for u in each:
                xs_ref[u, pl.ds(pl.multiple_of(c * RB + 8, 8), RB), :] = xd_ref[rows_of(c), lanes[u]].astype(F32)
            return unused

        lax.fori_loop(0, n, load, 0)

        def forward_one(u, c, state):
            p = ids[u]
            rows = rows_of(c)
            off = off_ref[rows, :]
            pre, _ = conv(c, xs_ref.at[u], slice(None), weight[u], bias[u])
            x, slope = silu_parts(pre)
            xc_ref[u, rows, :] = x
            ds_ref[u, rows, :] = slope
            row0 = cum_ref[c, pl.ds(2 * p, 1), :]
            row1 = cum_ref[c, pl.ds(2 * p + 1, 1), :]
            col0 = jnp.broadcast_to(row0, (128, RB)).T
            col1 = jnp.broadcast_to(row1, (128, RB)).T
            step0 = step_ref[c, pl.ds(2 * p, 1), :]
            step1 = step_ref[c, pl.ds(2 * p + 1, 1), :]
            step = jnp.where(sub < MP, step0, step1).T
            st_ref[u, rows, :] = step
            cum = jnp.where(low, col0, col1)
            mask = bias_ref[c]
            cb = cb_ref[c]
            decay0 = jnp.exp(col0 - row0 + mask)
            decay1 = jnp.exp(col1 - row1 + mask)
            mix0 = (decay0 * cb).astype(BF16)
            mix1 = (decay1 * cb).astype(BF16)
            value = step * x
            grad = xd_ref[rows, lanes_d[u]].astype(F32)
            value_low = value.astype(BF16)
            value_two = jnp.concatenate(
                [jnp.where(low, value, 0.0).astype(BF16), jnp.where(low, 0.0, value).astype(BF16)], axis=0
            )
            grad_two = jnp.concatenate(
                [jnp.where(low, grad, 0.0).astype(BF16), jnp.where(low, 0.0, grad).astype(BF16)], axis=0
            )
            inner = dot(jnp.concatenate([mix0, mix1], axis=1), value_two, NN)
            dwi_ref[u, rows, :] = dot(jnp.concatenate([mix0, mix1], axis=0), grad_two, TN)
            grad_mix = dot(grad_two, value_low, NT)
            added = decay0 * grad_mix[:RB] + decay1 * grad_mix[RB:]
            enter = jnp.where(off > sub, jnp.exp(cum), 0.0)
            last = cum[RB - 1 :]
            off_last = off[RB - 1 :]
            leave = jnp.where(sub >= RB - 1 - off_last, jnp.exp(last - cum), 0.0)
            keep = jnp.where(off_last >= RB, jnp.exp(last), 0.0)
            lv_ref[u, rows, :] = leave
            k_ref[u, c] = jnp.broadcast_to(keep, (8, 128))
            sin_ref[u, c] = state
            state_low = state.astype(BF16)
            total = inner + enter * dot(cc_ref[rows, :], state_low, NN)
            yn_ref[u, rows, :] = total
            od_ref[rows, lanes_d[u]] = (total + skip[u] * x).astype(BF16)
            entered = (enter * grad).astype(BF16)
            ed_ref[u, rows, :] = entered
            new_state = keep * state + dot(bt_ref[c], (leave * value).astype(BF16), NN)
            return new_state, added, dot(entered, state_low, NT)

        def forward(c, states):
            found = [forward_one(u, c, states[u]) for u in each]
            dcb_ref[c] += sum(f[1] for f in found)
            dc_ref[c] += sum(f[2] for f in found)
            return tuple(f[0] for f in found)

        nothing = tuple(jnp.zeros((128, 128), F32) for u in each)
        final = lax.fori_loop(0, n, forward, nothing)
        for u in each:
            sin_ref[u, n] = final[u]
            for j in range(KC + 2):
                acc_ref[u, j] = zero8

        def backward_one(u, c, later):
            rows = rows_of(c)
            later_low = later.astype(BF16)
            leave = lv_ref[u, rows, :]
            x = xc_ref[u, rows, :]
            step = st_ref[u, rows, :]
            grad = xd_ref[rows, lanes_d[u]].astype(F32)
            value = step * x
            grad_value = dwi_ref[u, rows, :] + leave * dot(bb_ref[rows, :], later_low, NN)
            z1 = grad * yn_ref[u, rows, :] - value.astype(BF16).astype(F32) * grad_value
            carried = jnp.sum(later_low.astype(F32) * sin_ref[u, c + 1], axis=0, keepdims=True)
            z1 = jnp.concatenate([z1[: RB - 8], z1[RB - 8 :] + jnp.where(sub[RB - 8 :] == RB - 1, carried, 0.0)], axis=0)
            z1_high = z1.astype(BF16)
            z1_rest = (z1 - z1_high.astype(F32)).astype(BF16)
            rates = dot(pick[u], z1_high, NT) + dot(pick[u], z1_rest, NT)
            steps = dot(pick[u], (x * grad_value).astype(BF16), NT)
            grad_b = dot((leave * value).astype(BF16), later_low, NT)
            grad_x = (step * grad_value + skip[u] * grad) * ds_ref[u, rows, :]
            back, sums = conv_back(c, grad_x, xs_ref.at[u], slice(None), weight[u], u)
            od_ref[rows, lanes[u]] = back.astype(BF16)
            sums.append(by_sublane(grad * x))
            for j in range(KC + 2):
                acc_ref[u, j] += sums[j]
            new_later = k_ref[u, c][:1] * later + dot(ct_ref[c], ed_ref[u, rows, :], NN)
            return new_later, rates, steps, grad_b

        def backward(k, laters):
            c = n - 1 - k
            found = [backward_one(u, c, laters[u]) for u in each]
            z1_ref[c] += sum(f[1] for f in found)
            z2_ref[c] += sum(f[2] for f in found)
            db_ref[c] += sum(f[3] for f in found)
            return tuple(f[0] for f in found)

        lax.fori_loop(0, n, backward, nothing)
        for u in each:
            found = [jnp.sum(acc_ref[u, j], axis=0, keepdims=True) for j in range(KC + 2)]
            found.append(jnp.zeros((8 - KC - 2, 128), F32))
            at_row = pl.multiple_of(hp + 8 * ids[u], 8)
            small_out[0][pl.ds(at_row, 8), :] = jnp.concatenate(found, axis=0)
        return carry

    lax.fori_loop(0, pairs // wide, streams, 0)

    for side in range(2):
        lanes = slice(128 * side, 128 * side + 128)
        weight = wbc[:, lanes]
        bias = bbc[:, lanes]
        for j in range(KC + 1):
            acc_ref[0, j] = zero8

        def finish(k, carry):
            c = n - 1 - k
            rows = rows_of(c)
            mixed = dcb_ref[c].astype(BF16)
            if side == 0:
                grad = db_ref[c] + dot(mixed, cc_ref[rows, :], TN)
            else:
                grad = dc_ref[c] + dot(mixed, bb_ref[rows, :], NN)
            pre, _ = conv(c, raw_ref, lanes, weight, bias)
            back, sums = conv_back(c, grad * silu_parts(pre)[1], raw_ref, lanes, weight, 0)
            og_ref[rows, lanes] = back.astype(BF16)
            for j in range(KC + 1):
                acc_ref[0, j] += sums[j]
            return carry

        lax.fori_loop(0, n, finish, 0)
        found = [jnp.sum(acc_ref[0, j], axis=0, keepdims=True) for j in range(KC + 1)]
        found.append(jnp.zeros((8 - KC - 1, 128), F32))
        first = hp + 8 * pairs + 8 * side
        small_out[0][first : first + 8, :] = jnp.concatenate(found, axis=0)

    later_sum = (sub >= lane).astype(F32)
    sum_log = jnp.zeros((hp, 128), F32)
    sum_step = jnp.zeros((hp, 128), F32)
    for m in range(n):
        c = me ^ m
        rate_grad = dot(z1_ref[c], later_sum, NN, HIGHEST)
        step_grad = z2_ref[c] - e_log * rate_grad
        logit_grad = step_grad * sg_ref[c]
        sum_log = sum_log - step_ref[c] * e_log * rate_grad
        sum_step = sum_step + logit_grad
        small_out[m][:hp, :] = logit_grad
        big_out[m][...] = od_ref[rows_of(c), :]
        bc_out[m][...] = og_ref[rows_of(c), :]
    first = hp + 8 * pairs + 16
    small_out[0][first : first + hp, :] = sum_log
    small_out[0][first + hp : first + 2 * hp, :] = sum_step
    for m in range(1, n):
        small_out[m][hp:, :] = small_out[0][hp:, :]


def mixer_call(n, heads, hp, idx, doc, big, raw, steps, weight_x, bias_x, weight_bc, bias_bc, head_params):
    width = heads * MP
    pairs = width // 128
    wide = 2 - pairs % 2
    tokens = n * RB
    small_rows = 3 * hp + 8 * pairs + 16
    square = pltpu.VMEM((n, RB, RB), F32)
    square_low = pltpu.VMEM((n, RB, RB), BF16)
    flat = pltpu.VMEM((wide, tokens, 128), F32)
    flat_low = pltpu.VMEM((tokens, 128), BF16)
    per_head = pltpu.VMEM((n, hp, 128), F32)
    return pl.pallas_call(
        lambda *refs: mixer_kernel(n, heads, hp, *refs),
        out_shape=[jax.ShapeDtypeStruct((RB, 2 * width), BF16)] * n
        + [jax.ShapeDtypeStruct((RB, 256), BF16)] * n
        + [jax.ShapeDtypeStruct((small_rows, 128), F32)] * n,
        in_specs=[smem(), smem()] + [vmem()] * (3 * n + 5),
        out_specs=[vmem()] * (3 * n),
        scratch_shapes=[
            pltpu.VMEM((tokens, 2 * width), BF16),
            pltpu.VMEM((tokens, 2 * width), BF16),
            pltpu.VMEM((tokens + 8, 256), F32),
            pltpu.VMEM((tokens, 256), BF16),
            pltpu.VMEM((tokens + 8, 128), jnp.int32),
            pltpu.VMEM((wide, tokens + 8, 128), F32),
            pltpu.VMEM((wide, KC - 1, tokens + 8, 128), F32),
            flat_low,
            flat_low,
            square_low,
            square_low,
            square,
            square,
            square,
            square,
            square,
            per_head,
            per_head,
            per_head,
            per_head,
            per_head,
            pltpu.VMEM((wide, n + 1, 128, 128), F32),
            flat,
            flat,
            flat,
            flat,
            flat,
            flat,
            pltpu.VMEM((wide, tokens, 128), BF16),
            pltpu.VMEM((wide, n, 8, 128), F32),
            pltpu.VMEM((wide, KC + 2, 8, 128), F32),
        ],
        compiler_params=params(),
        name="mixer",
    )(idx, doc, *big, *raw, *steps, weight_x, bias_x, weight_bc, bias_bc, head_params)


def program(
    mixer_x,
    mixer_bc,
    dt_raw,
    gate_z,
    conv_weight_x,
    conv_bias_x,
    conv_weight_bc,
    conv_bias_bc,
    a_log,
    dt_bias,
    skip_d,
    d_mixer,
    doc_lengths,
    att_queries,
    att_keys,
    att_values,
    d_attn,
):
    n = lax.axis_size("ctx")
    place = lax.axis_index("ctx")
    idx = jnp.reshape(place, (1,)).astype(jnp.int32)
    rows, channels = mixer_x.shape
    all_heads = channels // MP
    heads = all_heads // n
    hp = max(8, heads)
    reach = max(1, n // 2)

    packed = pack_call(n, idx, mixer_x, gate_z, d_mixer)
    big = [packed[0]] + [crossed(packed[m], "ctx", m) for m in range(1, n)]

    own = jnp.concatenate([att_keys, att_values], axis=1)
    logits = jnp.transpose(dt_raw).reshape(n, heads, rows)
    logits = jnp.pad(logits, ((0, 0), (0, hp - heads), (0, 0)))
    own, raw_own, logits, _ = lax.optimization_barrier((own, mixer_bc, logits, packed[0]))
    blocks = [shifted(own, "ctx", d) for d in range(reach, 0, -1)] + [own]
    raw = [raw_own] + [crossed(raw_own, "ctx", m) for m in range(1, n)]
    steps = [lax.dynamic_index_in_dim(logits, place ^ m, 0, keepdims=False) for m in range(n)]
    steps = [steps[0]] + [crossed(steps[m], "ctx", m) for m in range(1, n)]

    attended = attention_call(idx, doc_lengths, att_queries, d_attn, blocks)
    grad_queries = attended[0]
    grad_kv = attended[-1]
    for d in range(1, reach + 1):
        grad_kv = grad_kv + shifted(attended[1 + reach - d], "ctx", -d).astype(F32)
    kv_width = att_keys.shape[1]
    grad_keys = grad_kv[:, :kv_width].astype(BF16)
    grad_values = grad_kv[:, kv_width:].astype(BF16)

    head_params = jnp.stack([a_log, dt_bias, skip_d])
    head_params = lax.dynamic_slice_in_dim(head_params, place * heads, heads, 1)
    head_params = jnp.pad(head_params, ((0, 0), (0, hp - heads)))
    head_params = jnp.broadcast_to(head_params[:, :, None], (3, hp, 128))
    results = mixer_call(
        n,
        heads,
        hp,
        idx,
        doc_lengths,
        big,
        raw,
        steps,
        conv_weight_x,
        conv_bias_x[None],
        conv_weight_bc,
        conv_bias_bc[None],
        head_params,
    )
    bc_parts = [results[n]] + [crossed(results[n + m], "ctx", m) for m in range(1, n)]
    small = [results[2 * n]] + [crossed(results[2 * n + m], "ctx", m) for m in range(1, n)]
    big = [results[0]] + [crossed(results[m], "ctx", m) for m in range(1, n)]

    pairs = heads * MP // 128
    first = hp + 8 * pairs
    bc_sum = bc_parts[0].astype(F32)
    tap_sum = small[0][first : first + 16]
    for m in range(1, n):
        bc_sum = bc_sum + bc_parts[m].astype(F32)
        tap_sum = tap_sum + small[m][first : first + 16]
    tap_sum = jnp.concatenate([tap_sum[:8], tap_sum[8:]], axis=1)
    both = jnp.concatenate([bc_sum, tap_sum], axis=0)
    for m in range(1, lax.axis_size("head")):
        arrived = crossed(both, "head", m)
        total = arrived if m == 1 else total + arrived
    both = both + total
    grad_bc = both[:rows].astype(BF16)
    grad_weight_bc = both[rows : rows + KC]
    grad_bias_bc = both[rows + KC]

    grad_x, grad_z, taps, logit_rows, head_sums = unpack_call(n, hp, idx, gate_z, d_mixer, big, small)
    logit_rows = logit_rows.reshape(n, hp, rows)[:, :heads].reshape(all_heads, rows)
    head_sums = head_sums.reshape(n, hp, 2, 128)[:, :heads].sum(axis=-1).reshape(all_heads, 2)
    return (
        grad_x,
        grad_bc,
        jnp.transpose(logit_rows),
        grad_z,
        taps[:KC],
        taps[KC],
        grad_weight_bc,
        grad_bias_bc,
        head_sums[:, 0],
        head_sums[:, 1],
        taps[KC + 1].reshape(all_heads, MP).sum(axis=1),
        grad_queries,
        grad_keys,
        grad_values,
    )


def solution(mesh):
    placed = (
        P("ctx", "head"),
        P("ctx", None),
        P("ctx", "head"),
        P("ctx", "head"),
        P(None, "head"),
        P("head"),
        P(),
        P(),
        P("head"),
        P("head"),
        P("head"),
        P("ctx", "head"),
        P(),
        P("ctx", "head"),
        P("ctx", "head"),
        P("ctx", "head"),
        P("ctx", "head"),
    )
    return jax.shard_map(
        program,
        mesh=mesh,
        in_specs=placed,
        out_specs=(
            P("ctx", "head"),
            P("ctx", None),
            P("ctx", "head"),
            P("ctx", "head"),
            P(None, "head"),
            P("head"),
            P(),
            P(),
            P("head"),
            P("head"),
            P("head"),
            P("ctx", "head"),
            P("ctx", "head"),
            P("ctx", "head"),
        ),
        check_vma=False,
    )
```

time: 907 us -> 263 us (0.29)
  the two profiles are of different devices: /device:TPU:0 before, /device:TPU:16 now
where the time goes in v1:
time: 263 us; the launch traced here: 262 us
  starting transfers between devices  101 us (38%)
  waiting for transfers between devices  93 us (35%)
  Pallas kernels  54.7 us (21%)
  local copies, waits for them, and re-layouts  9.24 us (4%)
    ppermute x45, waiting for transfers between devices, crossed(): lax.ppermute(value, axis, [(source, source ^ mask) for source in range(co...  93 us
    ppermute x45, starting transfers between devices, crossed(): lax.ppermute(value, axis, [(source, source ^ mask) for source in range(co...  60.4 us
    ppermute x8, starting transfers between devices, shifted(): lax.ppermute(value, axis, [(source, source + steps) for source in range(i...  40.8 us
    pallas_call x1, Pallas kernels, mixer_call(): pl.pallas_call(lambda *refs: mixer_kernel(n, heads, hp, *refs), out_shape...  29.5 us
    pallas_call x1, Pallas kernels, attention_call(): pl.pallas_call(lambda *refs: attention_kernel(nb - 1, *refs), out_shape=o...  17.4 us
  transfers between devices with their start and end apart: 53, of which 20 were waited for; matrix products, arithmetic and copies ran while one was open for 2% of the time, Pallas kernels for 18%

profile of v1, /device:TPU:16, one launch (start us, length us, event | category | flops | bytes accessed | tf_op | source)
XLA Modules:
  0.0 262.1 jit_solution(7692357570546234553)
XLA Ops:
  1.6 3.5 %pack.1 = (bf16[128,1024]{1,0:T(8,128)(2,1)}, bf16[128,1024]{1,0:T(8,128)(2,1)}, bf16[128,1024]{1,0:T(8,128)(2,1)}, bf16[128,1024]{1,0:T(8,128)(2,1)}, bf16[128,...) custom-call(s32[1]{0:T(128)} %bitcast.refs_0_, ...), custom_call_target="tpu_custom_call" | custom-call | tf_op jit(solution)/shard_map/pack/pallas_call | solution.py:161
  5.1 1.6 collective-permute-start.7
  6.6 1.6 collective-permute-start.8
  11.3 6.1 %collective-permute-done.14.refs_19_ = f32[8,128]{1,0:T(8,128)S(1)} collective-permute-done((f32[8,128]{1,0:T(8,128)S(1)}, f32[8,128]{1,0:T(8,128)S(1)}, u32[]{:S(2)}, u32[]{:S(2)}) %collective-permute-start.14) | collective-permute-done | bytes 4128 | tf_op jit(solution)/shard_map/ppermute | solution.py:35
  18.1 2.9 %collective-permute-done.15.refs_20_ = f32[8,128]{1,0:T(8,128)S(1)} collective-permute-done((f32[8,128]{1,0:T(8,128)S(1)}, f32[8,128]{1,0:T(8,128)S(1)}, u32[]{:S(2)}, u32[]{:S(2)}) %collective-permute-start.15) | collective-permute-done | bytes 4128 | tf_op jit(solution)/shard_map/ppermute | solution.py:35
  22.2 3.3 %collective-permute-done.16.refs_21_ = f32[8,128]{1,0:T(8,128)S(1)} collective-permute-done((f32[8,128]{1,0:T(8,128)S(1)}, f32[8,128]{1,0:T(8,128)S(1)}, u32[]{:S(2)}, u32[]{:S(2)}) %collective-permute-start.16) | collective-permute-done | bytes 4128 | tf_op jit(solution)/shard_map/ppermute | solution.py:35
  25.9 4.2 %collective-permute-done.17.refs_22_ = f32[8,128]{1,0:T(8,128)S(1)} collective-permute-done((f32[8,128]{1,0:T(8,128)S(1)}, f32[8,128]{1,0:T(8,128)S(1)}, u32[]{:S(2)}, u32[]{:S(2)}) %collective-permute-start.17) | collective-permute-done | bytes 4128 | tf_op jit(solution)/shard_map/ppermute | solution.py:35
  30.4 5.0 %collective-permute-done.18.refs_23_ = f32[8,128]{1,0:T(8,128)S(1)} collective-permute-done((f32[8,128]{1,0:T(8,128)S(1)}, f32[8,128]{1,0:T(8,128)S(1)}, u32[]{:S(2)}, u32[]{:S(2)}) %collective-permute-start.18) | collective-permute-done | bytes 4128 | tf_op jit(solution)/shard_map/ppermute | solution.py:35
  35.4 3.6 %collective-permute-done.19.refs_24_ = f32[8,128]{1,0:T(8,128)S(1)} collective-permute-done((f32[8,128]{1,0:T(8,128)S(1)}, f32[8,128]{1,0:T(8,128)S(1)}, u32[]{:S(2)}, u32[]{:S(2)}) %collective-permute-start.19) | collective-permute-done | bytes 4128 | tf_op jit(solution)/shard_map/ppermute | solution.py:35
  39.1 4.5 %collective-permute-done.20.refs_25_ = f32[8,128]{1,0:T(8,128)S(1)} collective-permute-done((f32[8,128]{1,0:T(8,128)S(1)}, f32[8,128]{1,0:T(8,128)S(1)}, u32[]{:S(2)}, u32[]{:S(2)}) %collective-permute-start.20) | collective-permute-done | bytes 4128 | tf_op jit(solution)/shard_map/ppermute | solution.py:35
  43.6 4.3 %collective-permute-start.1 = (bf16[128,1024]{1,0:T(8,128)(2,1)}, bf16[128,1024]{1,0:T(8,128)(2,1)S(1)}, u32[]{:S(2)}, u32[]{:S(2)}) collective-permute-start(bf16[128,1024]{1,0:T(8,128)(2,1)} %get-tuple-element.62), channel_id=1, source_target_pairs={{0,8},{4,12},{8,0},{12,4},{16,24},{20,28},{24,16},{28,20},{1,9},{5... | collective-permute-start | bytes 786440 | tf_op jit(solution)/shard_map/ppermute | solution.py:35
  48.0 3.4 %collective-permute-start.11 = (bf16[128,256]{1,0:T(8,128)(2,1)S(1)}, bf16[128,256]{1,0:T(8,128)(2,1)S(1)}, u32[]{:S(2)}, u32[]{:S(2)}) collective-permute-start(bf16[128,256]{1,0:T(8,128)(2,1)S(1)} %copy-done.20), channel_id=1, source_target_pairs={{0,20},{4,16},{8,28},{12,24},{16,4},{20,0},{24,12},{28,8},{1,21},{... | collective-permute-start | bytes 196616 | tf_op jit(solution)/shard_map/ppermute | solution.py:35
  51.9 3.2 %collective-permute-done.10.refs_14_ = bf16[128,256]{1,0:T(8,128)(2,1)S(1)} collective-permute-done((bf16[128,256]{1,0:T(8,128)(2,1)S(1)}, bf16[128,256]{1,0:T(8,128)(2,1)S(1)}, u32[]{:S(2)}, u32[]{:S(2)}) %collective-permute-start.10) | collective-permute-done | bytes 65568 | tf_op jit(solution)/shard_map/ppermute | solution.py:35
  55.1 2.1 collective-permute-start.12
  57.5 2.0 collective-permute-start.13
  59.5 2.0 collective-permute-done.12.refs_16_
  61.5 4.9 %collective-permute-start.3 = (bf16[128,1024]{1,0:T(8,128)(2,1)}, bf16[128,1024]{1,0:T(8,128)(2,1)S(1)}, u32[]{:S(2)}, u32[]{:S(2)}) collective-permute-start(bf16[128,1024]{1,0:T(8,128)(2,1)} %get-tuple-element.64), channel_id=1, source_target_pairs={{0,16},{4,20},{8,24},{12,28},{16,0},{20,4},{24,8},{28,12},{1,17},{... | collective-permute-start | bytes 786440 | tf_op jit(solution)/shard_map/ppermute | solution.py:35
  66.5 6.5 %collective-permute-done.13.refs_17_ = bf16[128,256]{1,0:T(8,128)(2,1)S(1)} collective-permute-done((bf16[128,256]{1,0:T(8,128)(2,1)S(1)}, bf16[128,256]{1,0:T(8,128)(2,1)S(1)}, u32[]{:S(2)}, u32[]{:S(2)}) %collective-permute-start.13) | collective-permute-done | bytes 65568 | tf_op jit(solution)/shard_map/ppermute | solution.py:35
  73.0 1.5 collective-permute-start.4
  74.5 1.5 collective-permute-start.5
  76.1 2.1 collective-permute-start.6
  80.2 17.2 %collective-permute-start.46 = (bf16[128,512]{1,0:T(8,128)(2,1)S(1)}, bf16[128,512]{1,0:T(8,128)(2,1)S(1)}, u32[]{:S(2)}, u32[]{:S(2)}) collective-permute-start(bf16[128,512]{1,0:T(8,128)(2,1)S(1)} %pad_maximum_fusion.refs_8_), channel_id=1, source_target_pairs={{0,12},{4,16},{8,20},{12,24},{16,28},{1,13},{5,17},{9,21},{13,25},... | collective-permute-start | bytes 393224 | tf_op jit(solution)/shard_map/ppermute | solution.py:30
  97.5 5.6 %collective-permute-start.47 = (bf16[128,512]{1,0:T(8,128)(2,1)S(1)}, bf16[128,512]{1,0:T(8,128)(2,1)S(1)}, u32[]{:S(2)}, u32[]{:S(2)}) collective-permute-start(bf16[128,512]{1,0:T(8,128)(2,1)S(1)} %pad_maximum_fusion.refs_8_), channel_id=1, source_target_pairs={{0,8},{4,12},{8,16},{12,20},{16,24},{20,28},{1,9},{5,13},{9,17},{1... | collective-permute-start | bytes 393224 | tf_op jit(solution)/shard_map/ppermute | solution.py:30
  103.1 4.7 %collective-permute-start.48 = (bf16[128,512]{1,0:T(8,128)(2,1)S(1)}, bf16[128,512]{1,0:T(8,128)(2,1)S(1)}, u32[]{:S(2)}, u32[]{:S(2)}) collective-permute-start(bf16[128,512]{1,0:T(8,128)(2,1)S(1)} %pad_maximum_fusion.refs_8_), channel_id=1, source_target_pairs={{0,4},{4,8},{8,12},{12,16},{16,20},{20,24},{24,28},{1,5},{5,9},{9,... | collective-permute-start | bytes 393224 | tf_op jit(solution)/shard_map/ppermute | solution.py:30
  107.9 3.1 %collective-permute-done.6.refs_9_ = bf16[128,1024]{1,0:T(8,128)(2,1)S(1)} collective-permute-done((bf16[128,1024]{1,0:T(8,128)(2,1)}, bf16[128,1024]{1,0:T(8,128)(2,1)S(1)}, u32[]{:S(2)}, u32[]{:S(2)}) %collective-permute-start.6) | collective-permute-done | bytes 262176 | tf_op jit(solution)/shard_map/ppermute | solution.py:35
  111.7 29.5 %mixer.1 = (bf16[128,1024]{1,0:T(8,128)(2,1)}, bf16[128,1024]{1,0:T(8,128)(2,1)}, bf16[128,1024]{1,0:T(8,128)(2,1)}, bf16[128,1024]{1,0:T(8,128)(2,1)}, bf16[128...) custom-call(s32[1]{0:T(128)} %bitcast.refs_0_, ...), custom_call_target="tpu_custom_call" | custom-call | tf_op jit(solution)/shard_map/mixer/pallas_call | solution.py:539
  141.4 3.4 %collective-permute-start.30 = (f32[72,128]{1,0:T(8,128)}, f32[72,128]{1,0:T(8,128)S(1)}, u32[]{:S(2)}, u32[]{:S(2)}) collective-permute-start(f32[72,128]{1,0:T(8,128)} %get-tuple-element.81), channel_id=1, source_target_pairs={{0,12},{4,8},{8,4},{12,0},{16,28},{20,24},{24,20},{28,16},{1,13},{... | collective-permute-start | bytes 110600 | tf_op jit(solution)/shard_map/ppermute | solution.py:35
  144.8 2.4 collective-permute-start.32
  147.4 3.3 %collective-permute-start.34 = (f32[72,128]{1,0:T(8,128)}, f32[72,128]{1,0:T(8,128)S(1)}, u32[]{:S(2)}, u32[]{:S(2)}) collective-permute-start(f32[72,128]{1,0:T(8,128)} %get-tuple-element.85), channel_id=1, source_target_pairs={{0,28},{4,24},{8,20},{12,16},{16,12},{20,8},{24,4},{28,0},{1,29},{... | collective-permute-start | bytes 110600 | tf_op jit(solution)/shard_map/ppermute | solution.py:35
  150.8 17.4 %attention.1 = (bf16[128,2048]{1,0:T(8,128)(2,1)}, bf16[128,512]{1,0:T(8,128)(2,1)}, bf16[128,512]{1,0:T(8,128)(2,1)}, bf16[128,512]{1,0:T(8,128)(2,1)}, bf16[128,512]{1,0:T(8,128)(2,1)}, /*index=5*/f32[128,512]{1,0:T(8,128)}) custom-call(s32[1]{0:T(128)} %bitcast.refs_0_, s32[8]{0:T(128)} %refs_1_.7, bf16[128,2048]{1,0:T(8,128)(2,1)} %refs_2_.5, ...), custom_call_target="tpu_custom_call" | custom-call | tf_op jit(solution)/shard_map/attention/pallas_call | solution.py:127
  170.0 5.1 %collective-permute-start.39 = (bf16[128,256]{1,0:T(8,128)(2,1)S(1)}, bf16[128,256]{1,0:T(8,128)(2,1)S(1)}, u32[]{:S(2)}, u32[]{:S(2)}) collective-permute-start(bf16[128,256]{1,0:T(8,128)(2,1)S(1)} %copy-done.59), channel_id=1, source_target_pairs={{0,20},{4,16},{8,28},{12,24},{16,4},{20,0},{24,12},{28,8},{1,21},{... | collective-permute-start | bytes 196616 | tf_op jit(solution)/shard_map/ppermute | solution.py:35
  175.2 3.0 %collective-permute-start.37 = (bf16[128,256]{1,0:T(8,128)(2,1)S(1)}, bf16[128,256]{1,0:T(8,128)(2,1)S(1)}, u32[]{:S(2)}, u32[]{:S(2)}) collective-permute-start(bf16[128,256]{1,0:T(8,128)(2,1)S(1)} %copy-done.57), channel_id=1, source_target_pairs={{0,12},{4,8},{8,4},{12,0},{16,28},{20,24},{24,20},{28,16},{1,13},{... | collective-permute-start | bytes 196616 | tf_op jit(solution)/shard_map/ppermute | solution.py:35
  179.0 1.5 collective-permute-start.35
  181.0 4.8 %collective-permute-start.52 = (bf16[128,512]{1,0:T(8,128)(2,1)}, bf16[128,512]{1,0:T(8,128)(2,1)S(1)}, u32[]{:S(2)}, u32[]{:S(2)}) collective-permute-start(bf16[128,512]{1,0:T(8,128)(2,1)} %get-tuple-element.105), channel_id=1, source_target_pairs={{16,0},{20,4},{24,8},{28,12},{17,1},{21,5},{25,9},{29,13},{18,2},{... | collective-permute-start | bytes 393224 | tf_op jit(solution)/shard_map/ppermute | solution.py:30
  185.8 2.7 %collective-permute-start.51 = (bf16[128,512]{1,0:T(8,128)(2,1)}, bf16[128,512]{1,0:T(8,128)(2,1)S(1)}, u32[]{:S(2)}, u32[]{:S(2)}) collective-permute-start(bf16[128,512]{1,0:T(8,128)(2,1)} %get-tuple-element.104), channel_id=1, source_target_pairs={{12,0},{16,4},{20,8},{24,12},{28,16},{13,1},{17,5},{21,9},{25,13},... | collective-permute-start | bytes 393224 | tf_op jit(solution)/shard_map/ppermute | solution.py:30
  188.5 1.9 collective-permute-start.50
  190.5 2.6 collective-permute-start.49
  194.6 2.1 collective-permute-start.22
  196.8 1.6 collective-permute-start.42
  199.2 3.5 %collective-permute-done.44 = f32[136,256]{1,0:T(8,128)S(1)} collective-permute-done((f32[136,256]{1,0:T(8,128)S(1)}, f32[136,256]{1,0:T(8,128)S(1)}, u32[]{:S(2)}, u32[]{:S(2)}) %collective-permute-start.44) | collective-permute-done | bytes 139296 | tf_op jit(solution)/shard_map/ppermute | solution.py:35
  202.8 2.9 %collective-permute-done.43 = f32[136,256]{1,0:T(8,128)S(1)} collective-permute-done((f32[136,256]{1,0:T(8,128)S(1)}, f32[136,256]{1,0:T(8,128)S(1)}, u32[]{:S(2)}, u32[]{:S(2)}) %collective-permute-start.43) | collective-permute-done | bytes 139296 | tf_op jit(solution)/shard_map/ppermute | solution.py:35
  212.8 2.4 collective-permute-done.24.refs_7_
  215.2 22.4 %collective-permute-done.25.refs_8_ = bf16[128,1024]{1,0:T(8,128)(2,1)S(1)} collective-permute-done((bf16[128,1024]{1,0:T(8,128)(2,1)S(1)}, bf16[128,1024]{1,0:T(8,128)(2,1)S(1)}, u32[]{:S(2)}, u32[]{:S(2)}) %collective-permute-start.25) | collective-permute-done | bytes 262176 | tf_op jit(solution)/shard_map/ppermute | solution.py:35
  237.7 8.8 %collective-permute-done.26.refs_9_ = bf16[128,1024]{1,0:T(8,128)(2,1)S(1)} collective-permute-done((bf16[128,1024]{1,0:T(8,128)(2,1)S(1)}, bf16[128,1024]{1,0:T(8,128)(2,1)S(1)}, u32[]{:S(2)}, u32[]{:S(2)}) %collective-permute-start.26) | collective-permute-done | bytes 262176 | tf_op jit(solution)/shard_map/ppermute | solution.py:35
  246.5 6.0 %collective-permute-done.27.refs_10_ = bf16[128,1024]{1,0:T(8,128)(2,1)S(1)} collective-permute-done((bf16[128,1024]{1,0:T(8,128)(2,1)S(1)}, bf16[128,1024]{1,0:T(8,128)(2,1)S(1)}, u32[]{:S(2)}, u32[]{:S(2)}) %collective-permute-start.27) | collective-permute-done | bytes 262176 | tf_op jit(solution)/shard_map/ppermute | solution.py:35
  253.2 4.3 %unpack.1 = (bf16[128,4096]{1,0:T(8,128)(2,1)}, bf16[128,4096]{1,0:T(8,128)(2,1)}, f32[8,4096]{1,0:T(8,128)}, f32[64,128]{1,0:T(8,128)}, f32[64,256]{1,0:T(8,128)}) custom-call(s32[1]{0:T(128)} %bitcast.refs_0_, bf16[128,4096]{1,0:T(8,128)(2,1)} %refs_1_.6, bf16[128,4096]{1,0:T(8,128)(2,1)} %refs_2_.4, bf16[128,1024]{1,0:T(8,128)(2,1)} %get-tuple-element.70.refs_3_, ...), custom_call_target="tpu_custom_call" | custom-call | tf_op jit(solution)/shard_map/unpack/pallas_call | solution.py:197
  257.5 1.5 slice.74
  259.1 1.6 slice_reduce_fusion
  (209 shorter events, 25.2 us)
Async XLA Ops:
  5.1 42.9 %collective-permute-start.7 = (bf16[128,256]{1,0:T(8,128)(2,1)S(1)}, bf16[128,256]{1,0:T(8,128)(2,1)S(1)}, u32[]{:S(2)}, u32[]{:S(2)}) collective-permute-start(bf16[128,256]{1,0:T(8,128)(2,1)S(1)} %copy-done.20), channel_id=1, source_target_pairs={{0,4},{4,0},{8,12},{12,8},{16,20},{20,16},{24,28},{28,24},{1,5},{5... | collective-permute-start | bytes 196616 | tf_op jit(solution)/shard_map/ppermute | solution.py:35
  6.6 41.3 %collective-permute-start.8 = (bf16[128,256]{1,0:T(8,128)(2,1)S(1)}, bf16[128,256]{1,0:T(8,128)(2,1)S(1)}, u32[]{:S(2)}, u32[]{:S(2)}) collective-permute-start(bf16[128,256]{1,0:T(8,128)(2,1)S(1)} %copy-done.20), channel_id=1, source_target_pairs={{0,8},{4,12},{8,0},{12,4},{16,24},{20,28},{24,16},{28,20},{1,9},{5... | collective-permute-start | bytes 196616 | tf_op jit(solution)/shard_map/ppermute | solution.py:35
  8.2 66.3 %collective-permute-start = (bf16[128,1024]{1,0:T(8,128)(2,1)}, bf16[128,1024]{1,0:T(8,128)(2,1)S(1)}, u32[]{:S(2)}, u32[]{:S(2)}) collective-permute-start(bf16[128,1024]{1,0:T(8,128)(2,1)} %get-tuple-element.61), channel_id=1, source_target_pairs={{0,4},{4,0},{8,12},{12,8},{16,20},{20,16},{24,28},{28,24},{1,5},{5... | collective-permute-start | bytes 786440 | tf_op jit(solution)/shard_map/ppermute | solution.py:35
  9.3 8.1 %collective-permute-start.14 = (f32[8,128]{1,0:T(8,128)S(1)}, f32[8,128]{1,0:T(8,128)S(1)}, u32[]{:S(2)}, u32[]{:S(2)}) collective-permute-start(f32[8,128]{1,0:T(8,128)S(1)} %get-tuple-element.116), channel_id=1, source_target_pairs={{0,4},{4,0},{8,12},{12,8},{16,20},{20,16},{24,28},{28,24},{1,5},{5... | collective-permute-start | bytes 12296 | tf_op jit(solution)/shard_map/ppermute | solution.py:35
  10.8 40.5 %collective-permute-start.9 = (bf16[128,256]{1,0:T(8,128)(2,1)S(1)}, bf16[128,256]{1,0:T(8,128)(2,1)S(1)}, u32[]{:S(2)}, u32[]{:S(2)}) collective-permute-start(bf16[128,256]{1,0:T(8,128)(2,1)S(1)} %copy-done.20), channel_id=1, source_target_pairs={{0,12},{4,8},{8,4},{12,0},{16,28},{20,24},{24,20},{28,16},{1,13},{... | collective-permute-start | bytes 196616 | tf_op jit(solution)/shard_map/ppermute | solution.py:35
  30.0 5.4 %collective-permute-start.18 = (f32[8,128]{1,0:T(8,128)S(1)}, f32[8,128]{1,0:T(8,128)S(1)}, u32[]{:S(2)}, u32[]{:S(2)}) collective-permute-start(f32[8,128]{1,0:T(8,128)S(1)} %get-tuple-element.112), channel_id=1, source_target_pairs={{0,20},{4,16},{8,28},{12,24},{16,4},{20,0},{24,12},{28,8},{1,21},{... | collective-permute-start | bytes 12296 | tf_op jit(solution)/shard_map/ppermute | solution.py:35
  43.6 32.5 %collective-permute-start.1 = (bf16[128,1024]{1,0:T(8,128)(2,1)}, bf16[128,1024]{1,0:T(8,128)(2,1)S(1)}, u32[]{:S(2)}, u32[]{:S(2)}) collective-permute-start(bf16[128,1024]{1,0:T(8,128)(2,1)} %get-tuple-element.62), channel_id=1, source_target_pairs={{0,8},{4,12},{8,0},{12,4},{16,24},{20,28},{24,16},{28,20},{1,9},{5... | collective-permute-start | bytes 786440 | tf_op jit(solution)/shard_map/ppermute | solution.py:35
  47.9 7.2 %collective-permute-start.10 = (bf16[128,256]{1,0:T(8,128)(2,1)S(1)}, bf16[128,256]{1,0:T(8,128)(2,1)S(1)}, u32[]{:S(2)}, u32[]{:S(2)}) collective-permute-start(bf16[128,256]{1,0:T(8,128)(2,1)S(1)} %copy-done.20), channel_id=1, source_target_pairs={{0,16},{4,20},{8,24},{12,28},{16,0},{20,4},{24,8},{28,12},{1,17},{... | collective-permute-start | bytes 196616 | tf_op jit(solution)/shard_map/ppermute | solution.py:35
  48.0 9.6 %collective-permute-start.11 = (bf16[128,256]{1,0:T(8,128)(2,1)S(1)}, bf16[128,256]{1,0:T(8,128)(2,1)S(1)}, u32[]{:S(2)}, u32[]{:S(2)}) collective-permute-start(bf16[128,256]{1,0:T(8,128)(2,1)S(1)} %copy-done.20), channel_id=1, source_target_pairs={{0,20},{4,16},{8,28},{12,24},{16,4},{20,0},{24,12},{28,8},{1,21},{... | collective-permute-start | bytes 196616 | tf_op jit(solution)/shard_map/ppermute | solution.py:35
  51.4 26.8 %collective-permute-start.2 = (bf16[128,1024]{1,0:T(8,128)(2,1)}, bf16[128,1024]{1,0:T(8,128)(2,1)S(1)}, u32[]{:S(2)}, u32[]{:S(2)}) collective-permute-start(bf16[128,1024]{1,0:T(8,128)(2,1)} %get-tuple-element.63), channel_id=1, source_target_pairs={{0,12},{4,8},{8,4},{12,0},{16,28},{20,24},{24,20},{28,16},{1,13},{... | collective-permute-start | bytes 786440 | tf_op jit(solution)/shard_map/ppermute | solution.py:35
  55.1 6.4 %collective-permute-start.12 = (bf16[128,256]{1,0:T(8,128)(2,1)S(1)}, bf16[128,256]{1,0:T(8,128)(2,1)S(1)}, u32[]{:S(2)}, u32[]{:S(2)}) collective-permute-start(bf16[128,256]{1,0:T(8,128)(2,1)S(1)} %copy-done.20), channel_id=1, source_target_pairs={{0,24},{4,28},{8,16},{12,20},{16,8},{20,12},{24,0},{28,4},{1,25},{... | collective-permute-start | bytes 196616 | tf_op jit(solution)/shard_map/ppermute | solution.py:35
  57.5 15.5 %collective-permute-start.13 = (bf16[128,256]{1,0:T(8,128)(2,1)S(1)}, bf16[128,256]{1,0:T(8,128)(2,1)S(1)}, u32[]{:S(2)}, u32[]{:S(2)}) collective-permute-start(bf16[128,256]{1,0:T(8,128)(2,1)S(1)} %copy-done.20), channel_id=1, source_target_pairs={{0,28},{4,24},{8,20},{12,16},{16,12},{20,8},{24,4},{28,0},{1,29},{... | collective-permute-start | bytes 196616 | tf_op jit(solution)/shard_map/ppermute | solution.py:35
  61.5 18.7 %collective-permute-start.3 = (bf16[128,1024]{1,0:T(8,128)(2,1)}, bf16[128,1024]{1,0:T(8,128)(2,1)S(1)}, u32[]{:S(2)}, u32[]{:S(2)}) collective-permute-start(bf16[128,1024]{1,0:T(8,128)(2,1)} %get-tuple-element.64), channel_id=1, source_target_pairs={{0,16},{4,20},{8,24},{12,28},{16,0},{20,4},{24,8},{28,12},{1,17},{... | collective-permute-start | bytes 786440 | tf_op jit(solution)/shard_map/ppermute | solution.py:35
  73.0 24.4 %collective-permute-start.4 = (bf16[128,1024]{1,0:T(8,128)(2,1)}, bf16[128,1024]{1,0:T(8,128)(2,1)S(1)}, u32[]{:S(2)}, u32[]{:S(2)}) collective-permute-start(bf16[128,1024]{1,0:T(8,128)(2,1)} %get-tuple-element.65), channel_id=1, source_target_pairs={{0,20},{4,16},{8,28},{12,24},{16,4},{20,0},{24,12},{28,8},{1,21},{... | collective-permute-start | bytes 786440 | tf_op jit(solution)/shard_map/ppermute | solution.py:35
  74.5 28.5 %collective-permute-start.5 = (bf16[128,1024]{1,0:T(8,128)(2,1)}, bf16[128,1024]{1,0:T(8,128)(2,1)S(1)}, u32[]{:S(2)}, u32[]{:S(2)}) collective-permute-start(bf16[128,1024]{1,0:T(8,128)(2,1)} %get-tuple-element.66), channel_id=1, source_target_pairs={{0,24},{4,28},{8,16},{12,20},{16,8},{20,12},{24,0},{28,4},{1,25},{... | collective-permute-start | bytes 786440 | tf_op jit(solution)/shard_map/ppermute | solution.py:35
  76.1 34.9 %collective-permute-start.6 = (bf16[128,1024]{1,0:T(8,128)(2,1)}, bf16[128,1024]{1,0:T(8,128)(2,1)S(1)}, u32[]{:S(2)}, u32[]{:S(2)}) collective-permute-start(bf16[128,1024]{1,0:T(8,128)(2,1)} %get-tuple-element.67), channel_id=1, source_target_pairs={{0,28},{4,24},{8,20},{12,16},{16,12},{20,8},{24,4},{28,0},{1,29},{... | collective-permute-start | bytes 786440 | tf_op jit(solution)/shard_map/ppermute | solution.py:35
  78.2 63.1 %collective-permute-start.45 = (bf16[128,512]{1,0:T(8,128)(2,1)S(1)}, bf16[128,512]{1,0:T(8,128)(2,1)S(1)}, u32[]{:S(2)}, u32[]{:S(2)}) collective-permute-start(bf16[128,512]{1,0:T(8,128)(2,1)S(1)} %pad_maximum_fusion.refs_8_), channel_id=1, source_target_pairs={{0,16},{4,20},{8,24},{12,28},{1,17},{5,21},{9,25},{13,29},{2,18},{... | collective-permute-start | bytes 393224 | tf_op jit(solution)/shard_map/ppermute | solution.py:30
  80.2 61.2 %collective-permute-start.46 = (bf16[128,512]{1,0:T(8,128)(2,1)S(1)}, bf16[128,512]{1,0:T(8,128)(2,1)S(1)}, u32[]{:S(2)}, u32[]{:S(2)}) collective-permute-start(bf16[128,512]{1,0:T(8,128)(2,1)S(1)} %pad_maximum_fusion.refs_8_), channel_id=1, source_target_pairs={{0,12},{4,16},{8,20},{12,24},{16,28},{1,13},{5,17},{9,21},{13,25},... | collective-permute-start | bytes 393224 | tf_op jit(solution)/shard_map/ppermute | solution.py:30
  97.5 47.3 %collective-permute-start.47 = (bf16[128,512]{1,0:T(8,128)(2,1)S(1)}, bf16[128,512]{1,0:T(8,128)(2,1)S(1)}, u32[]{:S(2)}, u32[]{:S(2)}) collective-permute-start(bf16[128,512]{1,0:T(8,128)(2,1)S(1)} %pad_maximum_fusion.refs_8_), channel_id=1, source_target_pairs={{0,8},{4,12},{8,16},{12,20},{16,24},{20,28},{1,9},{5,13},{9,17},{1... | collective-permute-start | bytes 393224 | tf_op jit(solution)/shard_map/ppermute | solution.py:30
  103.1 41.7 %collective-permute-start.48 = (bf16[128,512]{1,0:T(8,128)(2,1)S(1)}, bf16[128,512]{1,0:T(8,128)(2,1)S(1)}, u32[]{:S(2)}, u32[]{:S(2)}) collective-permute-start(bf16[128,512]{1,0:T(8,128)(2,1)S(1)} %pad_maximum_fusion.refs_8_), channel_id=1, source_target_pairs={{0,4},{4,8},{8,12},{12,16},{16,20},{20,24},{24,28},{1,5},{5,9},{9,... | collective-permute-start | bytes 393224 | tf_op jit(solution)/shard_map/ppermute | solution.py:30
  141.2 6.0 %collective-permute-start.28 = (f32[72,128]{1,0:T(8,128)}, f32[72,128]{1,0:T(8,128)S(1)}, u32[]{:S(2)}, u32[]{:S(2)}) collective-permute-start(f32[72,128]{1,0:T(8,128)} %get-tuple-element.79), channel_id=1, source_target_pairs={{0,4},{4,0},{8,12},{12,8},{16,20},{20,16},{24,28},{28,24},{1,5},{5... | collective-permute-start | bytes 110600 | tf_op jit(solution)/shard_map/ppermute | solution.py:35
  141.3 6.1 %collective-permute-start.29 = (f32[72,128]{1,0:T(8,128)}, f32[72,128]{1,0:T(8,128)S(1)}, u32[]{:S(2)}, u32[]{:S(2)}) collective-permute-start(f32[72,128]{1,0:T(8,128)} %get-tuple-element.80), channel_id=1, source_target_pairs={{0,8},{4,12},{8,0},{12,4},{16,24},{20,28},{24,16},{28,20},{1,9},{5... | collective-permute-start | bytes 110600 | tf_op jit(solution)/shard_map/ppermute | solution.py:35
  141.4 26.8 %collective-permute-start.30 = (f32[72,128]{1,0:T(8,128)}, f32[72,128]{1,0:T(8,128)S(1)}, u32[]{:S(2)}, u32[]{:S(2)}) collective-permute-start(f32[72,128]{1,0:T(8,128)} %get-tuple-element.81), channel_id=1, source_target_pairs={{0,12},{4,8},{8,4},{12,0},{16,28},{20,24},{24,20},{28,16},{1,13},{... | collective-permute-start | bytes 110600 | tf_op jit(solution)/shard_map/ppermute | solution.py:35
  144.8 23.7 %collective-permute-start.31 = (f32[72,128]{1,0:T(8,128)}, f32[72,128]{1,0:T(8,128)S(1)}, u32[]{:S(2)}, u32[]{:S(2)}) collective-permute-start(f32[72,128]{1,0:T(8,128)} %get-tuple-element.82), channel_id=1, source_target_pairs={{0,16},{4,20},{8,24},{12,28},{16,0},{20,4},{24,8},{28,12},{1,17},{... | collective-permute-start | bytes 110600 | tf_op jit(solution)/shard_map/ppermute | solution.py:35
  144.8 25.1 %collective-permute-start.32 = (f32[72,128]{1,0:T(8,128)}, f32[72,128]{1,0:T(8,128)S(1)}, u32[]{:S(2)}, u32[]{:S(2)}) collective-permute-start(f32[72,128]{1,0:T(8,128)} %get-tuple-element.83), channel_id=1, source_target_pairs={{0,20},{4,16},{8,28},{12,24},{16,4},{20,0},{24,12},{28,8},{1,21},{... | collective-permute-start | bytes 110600 | tf_op jit(solution)/shard_map/ppermute | solution.py:35
  147.3 27.8 %collective-permute-start.33 = (f32[72,128]{1,0:T(8,128)}, f32[72,128]{1,0:T(8,128)S(1)}, u32[]{:S(2)}, u32[]{:S(2)}) collective-permute-start(f32[72,128]{1,0:T(8,128)} %get-tuple-element.84), channel_id=1, source_target_pairs={{0,24},{4,28},{8,16},{12,20},{16,8},{20,12},{24,0},{28,4},{1,25},{... | collective-permute-start | bytes 110600 | tf_op jit(solution)/shard_map/ppermute | solution.py:35
  147.4 27.7 %collective-permute-start.34 = (f32[72,128]{1,0:T(8,128)}, f32[72,128]{1,0:T(8,128)S(1)}, u32[]{:S(2)}, u32[]{:S(2)}) collective-permute-start(f32[72,128]{1,0:T(8,128)} %get-tuple-element.85), channel_id=1, source_target_pairs={{0,28},{4,24},{8,20},{12,16},{16,12},{20,8},{24,4},{28,0},{1,29},{... | collective-permute-start | bytes 110600 | tf_op jit(solution)/shard_map/ppermute | solution.py:35
  168.2 10.6 %collective-permute-start.41 = (bf16[128,256]{1,0:T(8,128)(2,1)S(1)}, bf16[128,256]{1,0:T(8,128)(2,1)S(1)}, u32[]{:S(2)}, u32[]{:S(2)}) collective-permute-start(bf16[128,256]{1,0:T(8,128)(2,1)S(1)} %copy-done.61), channel_id=1, source_target_pairs={{0,28},{4,24},{8,20},{12,16},{16,12},{20,8},{24,4},{28,0},{1,29},{... | collective-permute-start | bytes 196616 | tf_op jit(solution)/shard_map/ppermute | solution.py:35
  168.5 10.5 %collective-permute-start.40 = (bf16[128,256]{1,0:T(8,128)(2,1)S(1)}, bf16[128,256]{1,0:T(8,128)(2,1)S(1)}, u32[]{:S(2)}, u32[]{:S(2)}) collective-permute-start(bf16[128,256]{1,0:T(8,128)(2,1)S(1)} %copy-done.60), channel_id=1, source_target_pairs={{0,24},{4,28},{8,16},{12,20},{16,8},{20,12},{24,0},{28,4},{1,25},{... | collective-permute-start | bytes 196616 | tf_op jit(solution)/shard_map/ppermute | solution.py:35
  170.0 11.0 %collective-permute-start.39 = (bf16[128,256]{1,0:T(8,128)(2,1)S(1)}, bf16[128,256]{1,0:T(8,128)(2,1)S(1)}, u32[]{:S(2)}, u32[]{:S(2)}) collective-permute-start(bf16[128,256]{1,0:T(8,128)(2,1)S(1)} %copy-done.59), channel_id=1, source_target_pairs={{0,20},{4,16},{8,28},{12,24},{16,4},{20,0},{24,12},{28,8},{1,21},{... | collective-permute-start | bytes 196616 | tf_op jit(solution)/shard_map/ppermute | solution.py:35
  175.1 10.8 %collective-permute-start.38 = (bf16[128,256]{1,0:T(8,128)(2,1)S(1)}, bf16[128,256]{1,0:T(8,128)(2,1)S(1)}, u32[]{:S(2)}, u32[]{:S(2)}) collective-permute-start(bf16[128,256]{1,0:T(8,128)(2,1)S(1)} %copy-done.58), channel_id=1, source_target_pairs={{0,16},{4,20},{8,24},{12,28},{16,0},{20,4},{24,8},{28,12},{1,17},{... | collective-permute-start | bytes 196616 | tf_op jit(solution)/shard_map/ppermute | solution.py:35
  175.2 13.4 %collective-permute-start.37 = (bf16[128,256]{1,0:T(8,128)(2,1)S(1)}, bf16[128,256]{1,0:T(8,128)(2,1)S(1)}, u32[]{:S(2)}, u32[]{:S(2)}) collective-permute-start(bf16[128,256]{1,0:T(8,128)(2,1)S(1)} %copy-done.57), channel_id=1, source_target_pairs={{0,12},{4,8},{8,4},{12,0},{16,28},{20,24},{24,20},{28,16},{1,13},{... | collective-permute-start | bytes 196616 | tf_op jit(solution)/shard_map/ppermute | solution.py:35
  178.9 11.6 %collective-permute-start.36 = (bf16[128,256]{1,0:T(8,128)(2,1)S(1)}, bf16[128,256]{1,0:T(8,128)(2,1)S(1)}, u32[]{:S(2)}, u32[]{:S(2)}) collective-permute-start(bf16[128,256]{1,0:T(8,128)(2,1)S(1)} %copy-done.56), channel_id=1, source_target_pairs={{0,8},{4,12},{8,0},{12,4},{16,24},{20,28},{24,16},{28,20},{1,9},{5... | collective-permute-start | bytes 196616 | tf_op jit(solution)/shard_map/ppermute | solution.py:35
  179.0 14.1 %collective-permute-start.35 = (bf16[128,256]{1,0:T(8,128)(2,1)S(1)}, bf16[128,256]{1,0:T(8,128)(2,1)S(1)}, u32[]{:S(2)}, u32[]{:S(2)}) collective-permute-start(bf16[128,256]{1,0:T(8,128)(2,1)S(1)} %copy-done.55), channel_id=1, source_target_pairs={{0,4},{4,0},{8,12},{12,8},{16,20},{20,16},{24,28},{28,24},{1,5},{5... | collective-permute-start | bytes 196616 | tf_op jit(solution)/shard_map/ppermute | solution.py:35
  181.0 13.7 %collective-permute-start.52 = (bf16[128,512]{1,0:T(8,128)(2,1)}, bf16[128,512]{1,0:T(8,128)(2,1)S(1)}, u32[]{:S(2)}, u32[]{:S(2)}) collective-permute-start(bf16[128,512]{1,0:T(8,128)(2,1)} %get-tuple-element.105), channel_id=1, source_target_pairs={{16,0},{20,4},{24,8},{28,12},{17,1},{21,5},{25,9},{29,13},{18,2},{... | collective-permute-start | bytes 393224 | tf_op jit(solution)/shard_map/ppermute | solution.py:30
  185.8 10.9 %collective-permute-start.51 = (bf16[128,512]{1,0:T(8,128)(2,1)}, bf16[128,512]{1,0:T(8,128)(2,1)S(1)}, u32[]{:S(2)}, u32[]{:S(2)}) collective-permute-start(bf16[128,512]{1,0:T(8,128)(2,1)} %get-tuple-element.104), channel_id=1, source_target_pairs={{12,0},{16,4},{20,8},{24,12},{28,16},{13,1},{17,5},{21,9},{25,13},... | collective-permute-start | bytes 393224 | tf_op jit(solution)/shard_map/ppermute | solution.py:30
  188.5 8.3 %collective-permute-start.50 = (bf16[128,512]{1,0:T(8,128)(2,1)}, bf16[128,512]{1,0:T(8,128)(2,1)S(1)}, u32[]{:S(2)}, u32[]{:S(2)}) collective-permute-start(bf16[128,512]{1,0:T(8,128)(2,1)} %get-tuple-element.103), channel_id=1, source_target_pairs={{8,0},{12,4},{16,8},{20,12},{24,16},{28,20},{9,1},{13,5},{17,9},{2... | collective-permute-start | bytes 393224 | tf_op jit(solution)/shard_map/ppermute | solution.py:30
  190.5 8.0 %collective-permute-start.49 = (bf16[128,512]{1,0:T(8,128)(2,1)}, bf16[128,512]{1,0:T(8,128)(2,1)S(1)}, u32[]{:S(2)}, u32[]{:S(2)}) collective-permute-start(bf16[128,512]{1,0:T(8,128)(2,1)} %get-tuple-element.102), channel_id=1, source_target_pairs={{4,0},{8,4},{12,8},{16,12},{20,16},{24,20},{28,24},{5,1},{9,5},{13... | collective-permute-start | bytes 393224 | tf_op jit(solution)/shard_map/ppermute | solution.py:30
  193.1 13.5 %collective-permute-start.21 = (bf16[128,1024]{1,0:T(8,128)(2,1)S(1)}, bf16[128,1024]{1,0:T(8,128)(2,1)S(1)}, u32[]{:S(2)}, u32[]{:S(2)}) collective-permute-start(bf16[128,1024]{1,0:T(8,128)(2,1)S(1)} %copy-done.54), channel_id=1, source_target_pairs={{0,4},{4,0},{8,12},{12,8},{16,20},{20,16},{24,28},{28,24},{1,5},{5... | collective-permute-start | bytes 786440 | tf_op jit(solution)/shard_map/ppermute | solution.py:35
  194.6 12.8 %collective-permute-start.22 = (bf16[128,1024]{1,0:T(8,128)(2,1)S(1)}, bf16[128,1024]{1,0:T(8,128)(2,1)S(1)}, u32[]{:S(2)}, u32[]{:S(2)}) collective-permute-start(bf16[128,1024]{1,0:T(8,128)(2,1)S(1)} %copy-done.53), channel_id=1, source_target_pairs={{0,8},{4,12},{8,0},{12,4},{16,24},{20,28},{24,16},{28,20},{1,9},{5... | collective-permute-start | bytes 786440 | tf_op jit(solution)/shard_map/ppermute | solution.py:35
  196.8 6.0 %collective-permute-start.44 = (f32[136,256]{1,0:T(8,128)S(1)}, f32[136,256]{1,0:T(8,128)S(1)}, u32[]{:S(2)}, u32[]{:S(2)}) collective-permute-start(f32[136,256]{1,0:T(8,128)S(1)} %maximum_maximum_fusion), channel_id=1, source_target_pairs={{0,3},{1,2},{2,1},{3,0},{4,7},{5,6},{6,5},{7,4},{8,11},{9,10},{10,... | collective-permute-start | bytes 417800 | tf_op jit(solution)/shard_map/ppermute | solution.py:35
  196.8 6.0 %collective-permute-start.42 = (f32[136,256]{1,0:T(8,128)S(1)}, f32[136,256]{1,0:T(8,128)S(1)}, u32[]{:S(2)}, u32[]{:S(2)}) collective-permute-start(f32[136,256]{1,0:T(8,128)S(1)} %maximum_maximum_fusion), channel_id=1, source_target_pairs={{0,1},{1,0},{2,3},{3,2},{4,5},{5,4},{6,7},{7,6},{8,9},{9,8},{10,11... | collective-permute-start | bytes 417800 | tf_op jit(solution)/shard_map/ppermute | solution.py:35
  198.5 7.3 %collective-permute-start.43 = (f32[136,256]{1,0:T(8,128)S(1)}, f32[136,256]{1,0:T(8,128)S(1)}, u32[]{:S(2)}, u32[]{:S(2)}) collective-permute-start(f32[136,256]{1,0:T(8,128)S(1)} %maximum_maximum_fusion), channel_id=1, source_target_pairs={{0,2},{1,3},{2,0},{3,1},{4,6},{5,7},{6,4},{7,5},{8,10},{9,11},{10,... | collective-permute-start | bytes 417800 | tf_op jit(solution)/shard_map/ppermute | solution.py:35
  202.7 10.1 %collective-permute-start.23 = (bf16[128,1024]{1,0:T(8,128)(2,1)S(1)}, bf16[128,1024]{1,0:T(8,128)(2,1)S(1)}, u32[]{:S(2)}, u32[]{:S(2)}) collective-permute-start(bf16[128,1024]{1,0:T(8,128)(2,1)S(1)} %copy-done.52), channel_id=1, source_target_pairs={{0,12},{4,8},{8,4},{12,0},{16,28},{20,24},{24,20},{28,16},{1,13},{... | collective-permute-start | bytes 786440 | tf_op jit(solution)/shard_map/ppermute | solution.py:35
  202.8 12.4 %collective-permute-start.24 = (bf16[128,1024]{1,0:T(8,128)(2,1)S(1)}, bf16[128,1024]{1,0:T(8,128)(2,1)S(1)}, u32[]{:S(2)}, u32[]{:S(2)}) collective-permute-start(bf16[128,1024]{1,0:T(8,128)(2,1)S(1)} %copy-done.51), channel_id=1, source_target_pairs={{0,16},{4,20},{8,24},{12,28},{16,0},{20,4},{24,8},{28,12},{1,17},{... | collective-permute-start | bytes 786440 | tf_op jit(solution)/shard_map/ppermute | solution.py:35
  205.8 31.9 %collective-permute-start.25 = (bf16[128,1024]{1,0:T(8,128)(2,1)S(1)}, bf16[128,1024]{1,0:T(8,128)(2,1)S(1)}, u32[]{:S(2)}, u32[]{:S(2)}) collective-permute-start(bf16[128,1024]{1,0:T(8,128)(2,1)S(1)} %copy-done.50), channel_id=1, source_target_pairs={{0,20},{4,16},{8,28},{12,24},{16,4},{20,0},{24,12},{28,8},{1,21},{... | collective-permute-start | bytes 786440 | tf_op jit(solution)/shard_map/ppermute | solution.py:35
  206.6 39.9 %collective-permute-start.26 = (bf16[128,1024]{1,0:T(8,128)(2,1)S(1)}, bf16[128,1024]{1,0:T(8,128)(2,1)S(1)}, u32[]{:S(2)}, u32[]{:S(2)}) collective-permute-start(bf16[128,1024]{1,0:T(8,128)(2,1)S(1)} %copy-done.49), channel_id=1, source_target_pairs={{0,24},{4,28},{8,16},{12,20},{16,8},{20,12},{24,0},{28,4},{1,25},{... | collective-permute-start | bytes 786440 | tf_op jit(solution)/shard_map/ppermute | solution.py:35
  207.4 45.1 %collective-permute-start.27 = (bf16[128,1024]{1,0:T(8,128)(2,1)S(1)}, bf16[128,1024]{1,0:T(8,128)(2,1)S(1)}, u32[]{:S(2)}, u32[]{:S(2)}) collective-permute-start(bf16[128,1024]{1,0:T(8,128)(2,1)S(1)} %copy-done.48), channel_id=1, source_target_pairs={{0,28},{4,24},{8,20},{12,16},{16,12},{20,8},{24,4},{28,0},{1,29},{... | collective-permute-start | bytes 786440 | tf_op jit(solution)/shard_map/ppermute | solution.py:35
  (67 other events, 1524.4 us)

commit v2 on v1

v2 whole, which is shorter than its diff:
```python
import math

import jax
import jax.numpy as jnp
from jax import lax
from jax.experimental import pallas as pl
from jax.experimental.pallas import tpu as pltpu
from jax.sharding import PartitionSpec as P


MP = 64
KC = 4
AH = 64
KVH = 8
HD = 128
RB = 128
FILL = -1e30
F32 = jnp.float32
BF16 = jnp.bfloat16
HIGHEST = lax.Precision.HIGHEST


def params(limit=56):
    return pltpu.CompilerParams(vmem_limit_bytes=limit * 1024 * 1024)


def shifted(value, axis, steps):
    count = lax.axis_size(axis)
    initial, last = (max(0, -steps), min(count, count - steps))
    return lax.ppermute(value, axis, [(source, source + steps) for source in range(initial, last)])


def crossed(value, axis, mask):
    count = lax.axis_size(axis)
    return lax.ppermute(value, axis, [(source, source ^ mask) for source in range(count)])


def dot(a, b, dims=((1,), (0,)), precision=None):
    return lax.dot_general(a, b, (dims, ((), ())), precision=precision, preferred_element_type=F32)


NN = ((1,), (0,))
NT = ((1,), (1,))
TN = ((0,), (0,))


def iota(shape, dim):
    return lax.broadcasted_iota(jnp.int32, shape, dim)


def doc_start(doc_ref, pos):
    end = jnp.int32(0)
    start = jnp.zeros_like(pos)
    for j in range(doc_ref.shape[0]):
        end = end + doc_ref[j]
        start = jnp.where(pos >= end, end, start)
    return start


def smem():
    return pl.BlockSpec(memory_space=pltpu.SMEM)


def vmem():
    return pl.BlockSpec(memory_space=pltpu.VMEM)


def attention_kernel(reach, idx_ref, doc_ref, q_ref, do_ref, *rest):
    nb = reach + 1
    kv_refs = rest[:nb]
    dq_ref = rest[nb]
    out_refs = rest[nb + 1 : 2 * nb + 1]
    k_ref, v_ref, kt_ref, mask_ref, qc_ref, dc_ref, p_ref, g_ref = rest[2 * nb + 1 :]
    group = AH // KVH
    kv_count = q_ref.shape[1] // (group * HD)
    inv_root = 1.0 / math.sqrt(HD)
    keys = nb * RB
    first = idx_ref[1] * RB
    q_pos = first + iota((8, RB), 1)
    q_start = doc_start(doc_ref, q_pos)[:1]
    k_pos = first - reach * RB + iota((keys, RB), 0)
    allowed = (k_pos <= q_pos[:1]) & (k_pos >= q_start)
    mask_ref[...] = jnp.where(allowed, 0.0, FILL)
    for kv in range(kv_count):
        for b in range(nb):
            k_ref[pl.ds(b * RB, RB), :] = kv_refs[b][:RB, pl.ds(kv * HD, HD)]
            v_ref[pl.ds(b * RB, RB), :] = kv_refs[b][:RB, pl.ds((kv_count + kv) * HD, HD)]
        kt_ref[...] = k_ref[...].astype(F32).T.astype(BF16)

        def one(h):
            lanes = pl.ds(pl.multiple_of((kv * group + h) * HD, HD), HD)
            rows = pl.ds(pl.multiple_of(h * RB, RB), RB)
            q = q_ref[:, lanes]
            do = do_ref[:, lanes]
            qc_ref[rows, :] = q
            dc_ref[rows, :] = do
            scores = dot(k_ref[...], q, NT) * inv_root + mask_ref[...]
            top = jnp.max(scores, axis=0, keepdims=True)
            weights = jnp.exp(scores - top)
            softmax = weights * (1.0 / jnp.sum(weights, axis=0, keepdims=True))
            grad_prob = dot(v_ref[...], do, NT)
            delta = jnp.sum(softmax * grad_prob, axis=0, keepdims=True)
            grad_score = (softmax * (grad_prob - delta)).astype(BF16)
            p_ref[:, rows] = softmax.astype(BF16)
            g_ref[:, rows] = grad_score
            grad_q = dot(kt_ref[...], grad_score, NN) * inv_root
            dq_ref[:, lanes] = grad_q.T.astype(BF16)

        def head(h, carry):
            one(2 * h)
            one(2 * h + 1)
            return carry

        lax.fori_loop(0, group // 2, head, 0)
        grad_k = dot(g_ref[...], qc_ref[...], NN) * inv_root
        grad_v = dot(p_ref[...], dc_ref[...], NN)
        for b in range(nb):
            kind = out_refs[b].dtype
            rows = slice(b * RB, (b + 1) * RB)
            out_refs[b][:, pl.ds(kv * HD, HD)] = grad_k[rows].astype(kind)
            out_refs[b][:, pl.ds((kv_count + kv) * HD, HD)] = grad_v[rows].astype(kind)


def attention_call(idx, doc, queries, grads, blocks):
    nb = len(blocks)
    keys = nb * RB
    group = AH // KVH
    outs = [jax.ShapeDtypeStruct(queries.shape, BF16)]
    outs += [jax.ShapeDtypeStruct(blocks[-1].shape, BF16)] * (nb - 1)
    outs += [jax.ShapeDtypeStruct(blocks[-1].shape, F32)]
    return pl.pallas_call(
        lambda *refs: attention_kernel(nb - 1, *refs),
        out_shape=outs,
        in_specs=[smem(), smem()] + [vmem()] * (2 + nb),
        out_specs=[vmem()] * (1 + nb),
        scratch_shapes=[
            pltpu.VMEM((keys, HD), BF16),
            pltpu.VMEM((keys, HD), BF16),
            pltpu.VMEM((HD, keys), BF16),
            pltpu.VMEM((keys, RB), F32),
            pltpu.VMEM((group * RB, HD), BF16),
            pltpu.VMEM((group * RB, HD), BF16),
            pltpu.VMEM((keys, group * RB), BF16),
            pltpu.VMEM((keys, group * RB), BF16),
        ],
        compiler_params=params(),
        name="attention",
    )(idx, doc, queries, grads, *blocks)


def pack_kernel(n, heads, idx_ref, x_ref, z_ref, d_ref, raw_ref, step_ref, *outs):
    width = heads * MP
    me = idx_ref[0]
    lane = iota((x_ref.shape[0], 128), 1)
    for m in range(n):
        dest = me ^ m
        lanes = pl.ds(pl.multiple_of(dest * width, 128), width)
        z = z_ref[:, lanes].astype(F32)
        grad = d_ref[:, lanes].astype(F32) * z * jax.nn.sigmoid(z)
        outs[m][:, :width] = x_ref[:, lanes]
        outs[m][:, width : 2 * width] = grad.astype(BF16)
        outs[m][:, 2 * width : 2 * width + 256] = raw_ref[...]
        logit = pltpu.roll(step_ref[...], (128 - dest * heads) % 128, 1)
        high = logit.astype(BF16).astype(F32)
        middle = (logit - high).astype(BF16).astype(F32)
        rest = logit - high - middle
        parts = jnp.where(lane < heads, high, pltpu.roll(middle, heads, 1))
        parts = jnp.where(lane < 2 * heads, parts, pltpu.roll(rest, 2 * heads, 1))
        outs[m][:, 2 * width + 256 :] = parts.astype(BF16)


def pack_call(n, heads, idx, mixer_x, gate_z, d_mixer, raw, steps):
    rows = mixer_x.shape[0]
    return pl.pallas_call(
        lambda *refs: pack_kernel(n, heads, *refs),
        out_shape=[jax.ShapeDtypeStruct((rows, 2 * heads * MP + 384), BF16)] * n,
        in_specs=[smem()] + [vmem()] * 5,
        out_specs=[vmem()] * n,
        compiler_params=params(),
        name="pack",
    )(idx, mixer_x, gate_z, d_mixer, raw, steps)


def keys_kernel(n, k_ref, v_ref, x_ref, raw_ref, own_ref, *outs):
    kv_width = k_ref.shape[1]
    width = x_ref.shape[1] // n
    half = width // 2
    own_ref[:, :kv_width] = k_ref[...]
    own_ref[:, kv_width:] = v_ref[...]
    for d in range(n):
        outs[d][:RB, :kv_width] = k_ref[...]
        outs[d][:RB, kv_width:] = v_ref[...]
        outs[d][RB : RB + 16, :] = x_ref[:, d * width : d * width + half]
        outs[d][RB + 16 : RB + 32, :] = x_ref[:, d * width + half : (d + 1) * width]
        outs[d][RB + 32 :, :256] = raw_ref[...]
        if 2 * kv_width > 256:
            outs[d][RB + 32 :, 256:] = jnp.zeros((16, 2 * kv_width - 256), BF16)


def keys_call(n, att_keys, att_values, mixer_x, mixer_bc):
    rows, kv_width = att_keys.shape
    last = rows // 16 - 1
    return pl.pallas_call(
        lambda *refs: keys_kernel(n, *refs),
        grid=(1,),
        out_shape=[jax.ShapeDtypeStruct((rows, 2 * kv_width), BF16)]
        + [jax.ShapeDtypeStruct((rows + 48, 2 * kv_width), BF16)] * n,
        in_specs=[
            pl.BlockSpec((rows, kv_width), lambda i: (0, 0)),
            pl.BlockSpec((rows, kv_width), lambda i: (0, 0)),
            pl.BlockSpec((16, mixer_x.shape[1]), lambda i: (last, 0)),
            pl.BlockSpec((16, 256), lambda i: (last, 0)),
        ],
        out_specs=[pl.BlockSpec((rows, 2 * kv_width), lambda i: (0, 0))]
        + [pl.BlockSpec((rows + 48, 2 * kv_width), lambda i: (0, 0))] * n,
        compiler_params=params(),
        name="keys",
    )(att_keys, att_values, mixer_x, mixer_bc)


def edges_kernel(n, hp, pairs, idx_ref, *refs):
    edges = refs[:n]
    logit_ref, margin_ref, share_ref, rows_ref = refs[n:]
    width = pairs * 128
    me = idx_ref[0]
    margin = jnp.zeros((16, 128), F32)
    total = jnp.zeros((16, 128), F32)
    first = hp + 8 * pairs + 16
    heads_at = first + 8 * pairs + 16
    for m in range(n):
        source = me ^ m
        held = pl.ds(pl.multiple_of(source * hp, 8), hp)
        rows_ref[0, held, :] = edges[m][:hp, :]
        for k in range(3):
            rows_ref[1 + k, held, :] = edges[m][heads_at + k * hp : heads_at + (k + 1) * hp, :]
        for p in range(pairs):
            part = pl.ds(pl.multiple_of(source * width + p * 128, 128), 128)
            margin_ref[:, part] = edges[m][hp + 8 * p : hp + 8 * p + 8, :]
            share_ref[:, part] = edges[m][first + 8 * p : first + 8 * p + 8, :]
        margin = margin + edges[m][hp + 8 * pairs : first, :]
        total = total + edges[m][first + 8 * pairs : heads_at, :]
    at = n * width
    margin_ref[:, at : at + 128] = margin[:8]
    margin_ref[:, at + 128 :] = margin[8:]
    share_ref[:, at : at + 128] = total[:8]
    share_ref[:, at + 128 : at + 256] = total[8:]
    ones = jnp.ones((8, 128), F32)
    for k in range(3):
        lanes = slice(at + 256 + k * n * hp, at + 256 + (k + 1) * n * hp)
        share_ref[:, lanes] = dot(ones, rows_ref[1 + k], NT, HIGHEST)
    logit_ref[...] = rows_ref[0].T


def edges_call(n, hp, pairs, idx, edges):
    return pl.pallas_call(
        lambda *refs: edges_kernel(n, hp, pairs, *refs),
        out_shape=[
            jax.ShapeDtypeStruct((RB, n * hp), F32),
            jax.ShapeDtypeStruct((8, n * pairs * 128 + 256), F32),
            jax.ShapeDtypeStruct((8, n * pairs * 128 + 256 + 3 * n * hp), F32),
        ],
        in_specs=[smem()] + [vmem()] * n,
        out_specs=[vmem()] * 3,
        scratch_shapes=[pltpu.VMEM((4, n * hp, 128), F32)],
        compiler_params=params(),
        name="edges",
    )(idx, *edges)


def unpack_kernel(n, hp, idx_ref, z_ref, d_ref, margin_ref, share_ref, *refs):
    big = refs[:n]
    gx_ref, gz_ref, taps_ref, bias_ref, heads_ref = refs[n:]
    channels = z_ref.shape[1]
    width = channels // n
    me = idx_ref[0]
    use = jnp.where(me == n - 1, 1.0, 0.0)
    for m in range(n):
        source = me ^ m
        lanes = pl.ds(pl.multiple_of(source * width, 128), width)
        gx_ref[: RB - 16, lanes] = big[m][: RB - 16, :width]
        end = big[m][RB - 16 :, :width].astype(F32)
        end = jnp.concatenate([end[:8], end[8:] + use * margin_ref[:, lanes]], axis=0)
        gx_ref[RB - 16 :, lanes] = end.astype(BF16)
        z = z_ref[:, lanes].astype(F32)
        sig = jax.nn.sigmoid(z)
        y = big[m][:, width:].astype(F32)
        gz_ref[:, lanes] = (d_ref[:, lanes].astype(F32) * y * (sig * (1.0 + z * (1.0 - sig)))).astype(BF16)
    taps_ref[...] = share_ref[:KC, :channels]
    bias_ref[...] = share_ref[KC : KC + 1, :channels]
    for k in range(3):
        at = channels + 256 + k * n * hp
        heads_ref[k : k + 1, :] = share_ref[:1, at : at + n * hp]


def unpack_call(n, hp, idx, gate_z, d_mixer, margin, share, big):
    rows, channels = gate_z.shape
    return pl.pallas_call(
        lambda *refs: unpack_kernel(n, hp, *refs),
        out_shape=[
            jax.ShapeDtypeStruct((rows, channels), BF16),
            jax.ShapeDtypeStruct((rows, channels), BF16),
            jax.ShapeDtypeStruct((KC, channels), F32),
            jax.ShapeDtypeStruct((1, channels), F32),
            jax.ShapeDtypeStruct((3, n * hp), F32),
        ],
        in_specs=[smem()] + [vmem()] * (4 + n),
        out_specs=[vmem()] * 5,
        compiler_params=params(),
        name="unpack",
    )(idx, gate_z, d_mixer, margin, share, *big)


def by_sublane(value):
    return jnp.sum(value.reshape(value.shape[0] // 8, 8, value.shape[1]), axis=0)


class Shared:
    def __init__(self, n, heads, hp, idx_ref, doc_ref, ins, scratch, full):
        self.n = n
        self.me = me = idx_ref[0]
        first = (idx_ref[1] - me) * RB
        xd_in = ins[:n]
        tails = ins[n : 2 * n]
        self.wx_ref, self.bx_ref, wbc_ref, bbc_ref, par_ref = ins[2 * n :]
        self.par_ref = par_ref
        width = heads * MP
        self.tail_ref, self.xd_ref, self.raw_ref, self.off_ref, self.xs_ref = scratch[:5]
        self.bb_ref, self.cc_ref, self.bt_ref, self.ct_ref, self.step_ref, self.cum_ref = scratch[5:11]
        if full:
            self.cb_ref, self.bias_ref, self.sg_ref = scratch[11:14]
        self.lane = lane = iota((RB, 128), 1)
        self.sub = sub = iota((RB, 128), 0)
        self.low = lane < MP
        upper = (sub <= lane).astype(F32)
        self.e_log = e_log = jnp.exp(par_ref[0])
        for m in range(n):
            source = me ^ m
            self.tail_ref[m, :, : width // 2] = tails[m][RB : RB + 16, :]
            self.tail_ref[m, :, width // 2 : width] = tails[m][RB + 16 : RB + 32, :]
            self.tail_ref[m, :, width:] = tails[m][RB + 32 : RB + 48, :256]
            self.xd_ref[self.rows(source), :] = xd_in[m][:, : 2 * width]
            raw = xd_in[m][:, 2 * width : 2 * width + 256]
            self.raw_ref[pl.ds(pl.multiple_of(source * RB + 8, 8), RB), :] = raw.astype(F32)
            parts = xd_in[m][:, 2 * width + 256 :].astype(F32).T
            logit = parts[:hp] + parts[hp : 2 * hp] + parts[2 * hp : 3 * hp]
            logit = logit + par_ref[1]
            step = jnp.maximum(logit, 0.0) + jnp.log1p(jnp.exp(-jnp.abs(logit)))
            self.step_ref[source] = step
            if full:
                self.sg_ref[source] = jax.nn.sigmoid(logit)
            self.cum_ref[source] = dot(-step * e_log, upper, NN, HIGHEST)
        self.raw_ref[:8, :] = self.tail_ref[me, :, width:].astype(F32)[8:]
        self.wbc = wbc = wbc_ref[...]
        self.bbc = bbc = bbc_ref[...]

        def prepare(c, carry):
            pos = first + c * RB + sub
            off = pos - doc_start(doc_ref, pos)
            self.off_ref[self.rows(c), :] = off
            pre_b = self.conv(c, self.raw_ref, slice(0, 128), wbc[:, :128], bbc[:, :128])
            pre_c = self.conv(c, self.raw_ref, slice(128, 256), wbc[:, 128:], bbc[:, 128:])
            b_in = pre_b * jax.nn.sigmoid(pre_b)
            c_out = pre_c * jax.nn.sigmoid(pre_c)
            self.bt_ref[c] = b_in.T.astype(BF16)
            self.ct_ref[c] = c_out.T.astype(BF16)
            if full:
                allowed = (lane <= sub) & (sub - lane <= off)
                self.bias_ref[c] = jnp.where(allowed, 0.0, FILL)
                b_low, c_low = b_in.astype(BF16), c_out.astype(BF16)
                self.bb_ref[self.rows(c), :] = b_low
                self.cc_ref[self.rows(c), :] = c_low
                self.cb_ref[c] = dot(c_low, b_low, NT)
            return carry

        lax.fori_loop(0, n, prepare, 0)

    def rows(self, c, extra=0):
        return pl.ds(pl.multiple_of(c * RB, RB), RB + extra)

    def conv(self, c, src_ref, lanes, weight, bias):
        off = self.off_ref[self.rows(c), :]
        window = src_ref[self.rows(c, 8), lanes]
        pre = bias + weight[0:1] * window[8:]
        for j in range(1, KC):
            pre = pre + weight[j : j + 1] * jnp.where(off >= j, window[8 - j : 8 + RB - j], 0.0)
        return pre

    def load(self, u, lanes):
        self.xs_ref[u, :8, :] = self.tail_ref[self.me, :, lanes].astype(F32)[8:]

        def one(c, unused):
            rows = pl.ds(pl.multiple_of(c * RB + 8, 8), RB)
            self.xs_ref[u, rows, :] = self.xd_ref[self.rows(c), lanes].astype(F32)
            return unused

        lax.fori_loop(0, self.n, one, 0)

    def decays(self, last_off, off, cum):
        last = cum[RB - 1 :]
        enter = jnp.where(off > self.sub, jnp.exp(cum), 0.0)
        leave = jnp.where(self.sub >= RB - 1 - last_off, jnp.exp(last - cum), 0.0)
        keep = jnp.where(last_off >= RB, jnp.exp(last), 0.0)
        return enter, leave, keep

    def pair_rows(self, ref, c, p):
        return ref[c, pl.ds(2 * p, 1), :], ref[c, pl.ds(2 * p + 1, 1), :]


def shared_scratch(n, heads, hp, wide, full):
    width = heads * MP
    tokens = n * RB
    found = [
        pltpu.VMEM((n, 16, width + 256), BF16),
        pltpu.VMEM((tokens, 2 * width), BF16),
        pltpu.VMEM((tokens + 8, 256), F32),
        pltpu.VMEM((tokens, 128), jnp.int32),
        pltpu.VMEM((wide, tokens + 8, 128), F32),
        pltpu.VMEM((tokens, 128), BF16),
        pltpu.VMEM((tokens, 128), BF16),
        pltpu.VMEM((n, 128, RB), BF16),
        pltpu.VMEM((n, 128, RB), BF16),
        pltpu.VMEM((n, hp, 128), F32),
        pltpu.VMEM((n, hp, 128), F32),
    ]
    if full:
        found += [
            pltpu.VMEM((n, RB, RB), F32),
            pltpu.VMEM((n, RB, RB), F32),
            pltpu.VMEM((n, hp, 128), F32),
        ]
    return found


def totals_kernel(n, heads, hp, wide, idx_ref, doc_ref, *refs):
    pairs = heads * MP // 128
    width = heads * MP
    ins = refs[: 2 * n + 5]
    state_ref, grad_ref, keep_ref = refs[2 * n + 5 : 2 * n + 8]
    sh = Shared(n, heads, hp, idx_ref, doc_ref, ins, refs[2 * n + 8 :], False)

    def streams(block, carry):
        ids = [block * wide + u for u in range(wide)]
        held = [pl.ds(pl.multiple_of(sh.me * width + p * 128, 128), 128) for p in ids]
        weight = [sh.wx_ref[:, h] for h in held]
        bias = [sh.bx_ref[:, h] for h in held]
        for u in range(wide):
            sh.load(u, pl.ds(pl.multiple_of(ids[u] * 128, 128), 128))

        def one(u, c, state, grads, kept):
            p = ids[u]
            off = sh.off_ref[sh.rows(c), :]
            pre = sh.conv(c, sh.xs_ref.at[u], slice(None), weight[u], bias[u])
            x = pre * jax.nn.sigmoid(pre)
            row0, row1 = sh.pair_rows(sh.cum_ref, c, p)
            step0, step1 = sh.pair_rows(sh.step_ref, c, p)
            cum = jnp.where(sh.sub < MP, row0, row1).T
            step = jnp.where(sh.sub < MP, step0, step1).T
            enter, leave, keep = sh.decays(off[RB - 1 :], off, cum)
            grad = sh.xd_ref[sh.rows(c), pl.ds(pl.multiple_of(width + p * 128, 128), 128)].astype(F32)
            state = keep * state + dot(sh.bt_ref[c], (leave * (step * x)).astype(BF16), NN)
            grads = grads + kept * dot(sh.ct_ref[c], (enter * grad).astype(BF16), NN)
            return state, grads, kept * keep

        def chunk(c, held):
            return tuple(one(u, c, *held[u]) for u in range(wide))

        zero = jnp.zeros((128, 128), F32)
        found = lax.fori_loop(0, n, chunk, tuple((zero, zero, jnp.ones((1, 128), F32)) for _ in range(wide)))
        for u in range(wide):
            state_ref[ids[u]] = found[u][0].astype(BF16)
            grad_ref[ids[u]] = found[u][1].astype(BF16)
            keep_ref[ids[u]] = jnp.broadcast_to(found[u][2], (8, 128))
        return carry

    lax.fori_loop(0, pairs // wide, streams, 0)


def totals_call(n, heads, hp, idx, doc, ins):
    pairs = heads * MP // 128
    wide = 2 - pairs % 2
    return pl.pallas_call(
        lambda *refs: totals_kernel(n, heads, hp, wide, *refs),
        out_shape=[
            jax.ShapeDtypeStruct((pairs, 128, 128), BF16),
            jax.ShapeDtypeStruct((pairs, 128, 128), BF16),
            jax.ShapeDtypeStruct((pairs, 8, 128), F32),
        ],
        in_specs=[smem(), smem()] + [vmem()] * len(ins),
        out_specs=[vmem()] * 3,
        scratch_shapes=shared_scratch(n, heads, hp, wide, False),
        compiler_params=params(),
        name="totals",
    )(idx, doc, *ins)


def mixer_kernel(n, heads, hp, wide, idx_ref, doc_ref, *refs):
    width = heads * MP
    pairs = width // 128
    ins = refs[: 2 * n + 5]
    first_ref, later_ref = refs[2 * n + 5 : 2 * n + 7]
    at = 2 * n + 7
    big_out = refs[at : at + n]
    bc_out = refs[at + n : at + 2 * n]
    edge_out = refs[at + 2 * n : at + 3 * n]
    at = at + 3 * n
    (
        od_ref,
        og_ref,
        gp_ref,
        dcb_ref,
        db_ref,
        dc_ref,
        z1_ref,
        z2_ref,
        sin_ref,
        yn_ref,
        dwi_ref,
        lv_ref,
        st_ref,
        xc_ref,
        ds_ref,
        ed_ref,
        k_ref,
        acc_ref,
        skip_ref,
    ) = refs[at : at + 19]
    sh = Shared(n, heads, hp, idx_ref, doc_ref, ins, refs[at + 19 :], True)
    me, lane, sub, low = sh.me, sh.lane, sh.sub, sh.low
    par_ref, wx_ref, bx_ref, xd_ref, off_ref = sh.par_ref, sh.wx_ref, sh.bx_ref, sh.xd_ref, sh.off_ref
    raw_ref, xs_ref, cum_ref, step_ref = sh.raw_ref, sh.xs_ref, sh.cum_ref, sh.step_ref
    bb_ref, cc_ref, bt_ref, ct_ref = sh.bb_ref, sh.cc_ref, sh.bt_ref, sh.ct_ref
    cb_ref, bias_ref, sg_ref = sh.cb_ref, sh.bias_ref, sh.sg_ref
    wbc, bbc, e_log, conv, rows_of = sh.wbc, sh.bbc, sh.e_log, sh.conv, sh.rows
    tokens = n * RB
    sums_at = hp + 8 * pairs + 16
    zero8 = jnp.zeros((8, 128), F32)
    for c in range(n):
        z1_ref[c] = jnp.zeros((hp, 128), F32)
        z2_ref[c] = jnp.zeros((hp, 128), F32)
        dcb_ref[c] = jnp.zeros((RB, RB), F32)
        db_ref[c] = jnp.zeros((RB, 128), F32)
        dc_ref[c] = jnp.zeros((RB, 128), F32)
    skip_ref[...] = jnp.zeros((hp, 128), F32)
    for u in range(wide):
        for j in range(KC - 1):
            gp_ref[u, j, tokens:, :] = zero8

    def conv_back(c, grad, src_ref, lanes, weight, u):
        off = off_ref[rows_of(c), :]
        window = src_ref[rows_of(c, 8), lanes]
        back = weight[0:1] * grad
        sums = [by_sublane(grad * window[8:])]
        for j in range(1, KC):
            held_back = jnp.where(off >= j, grad, 0.0)
            sums.append(by_sublane(held_back * window[8 - j : 8 + RB - j]))
            gp_ref[u, j - 1, rows_of(c), :] = held_back
            back = back + weight[j : j + 1] * gp_ref[u, j - 1, rows_of(c, 8), :][j : j + RB]
        sums.append(by_sublane(grad))
        return back, sums

    def silu_parts(pre):
        sig = jax.nn.sigmoid(pre)
        return pre * sig, sig * (1.0 + pre * (1.0 - sig))

    def margin_of(weight, u):
        total = zero8
        for j in range(1, KC):
            turned = pltpu.roll(gp_ref[u, j - 1, :8, :], 8 - j, 0)
            total = total + weight[j : j + 1] * jnp.where(sub[:8] >= 8 - j, turned, 0.0)
        return total

    def streams(block, carry):
        ids = [block * wide + u for u in range(wide)]
        each = range(wide)
        lanes = [pl.ds(pl.multiple_of(p * 128, 128), 128) for p in ids]
        lanes_d = [pl.ds(pl.multiple_of(width + p * 128, 128), 128) for p in ids]
        held = [pl.ds(pl.multiple_of(me * width + p * 128, 128), 128) for p in ids]
        weight = [wx_ref[:, h] for h in held]
        bias = [bx_ref[:, h] for h in held]
        skip = [
            jnp.where(low[:1], par_ref[2, pl.ds(2 * p, 1), :], par_ref[2, pl.ds(2 * p + 1, 1), :]) for p in ids
        ]
        pick = [
            jnp.where(iota((hp, 128), 0) == 2 * p + iota((hp, 128), 1) // MP, 1.0, 0.0).astype(BF16) for p in ids
        ]

        for u in each:
            sh.load(u, lanes[u])

        def forward_one(u, c, state):
            p = ids[u]
            rows = rows_of(c)
            off = off_ref[rows, :]
            pre = conv(c, xs_ref.at[u], slice(None), weight[u], bias[u])
            x, slope = silu_parts(pre)
            xc_ref[u, rows, :] = x
            ds_ref[u, rows, :] = slope
            row0 = cum_ref[c, pl.ds(2 * p, 1), :]
            row1 = cum_ref[c, pl.ds(2 * p + 1, 1), :]
            col0 = jnp.broadcast_to(row0, (128, RB)).T
            col1 = jnp.broadcast_to(row1, (128, RB)).T
            step0 = step_ref[c, pl.ds(2 * p, 1), :]
            step1 = step_ref[c, pl.ds(2 * p + 1, 1), :]
            step = jnp.where(sub < MP, step0, step1).T
            st_ref[u, rows, :] = step
            cum = jnp.where(low, col0, col1)
            mask = bias_ref[c]
            cb = cb_ref[c]
            decay0 = jnp.exp(col0 - row0 + mask)
            decay1 = jnp.exp(col1 - row1 + mask)
            mix0 = (decay0 * cb).astype(BF16)
            mix1 = (decay1 * cb).astype(BF16)
            value = step * x
            grad = xd_ref[rows, lanes_d[u]].astype(F32)
            value_low = value.astype(BF16)
            value_two = jnp.concatenate(
                [jnp.where(low, value, 0.0).astype(BF16), jnp.where(low, 0.0, value).astype(BF16)], axis=0
            )
            grad_two = jnp.concatenate(
                [jnp.where(low, grad, 0.0).astype(BF16), jnp.where(low, 0.0, grad).astype(BF16)], axis=0
            )
            inner = dot(jnp.concatenate([mix0, mix1], axis=1), value_two, NN)
            dwi_ref[u, rows, :] = dot(jnp.concatenate([mix0, mix1], axis=0), grad_two, TN)
            grad_mix = dot(grad_two, value_low, NT)
            added = decay0 * grad_mix[:RB] + decay1 * grad_mix[RB:]
            enter, leave, keep = sh.decays(off[RB - 1 :], off, cum)
            lv_ref[u, rows, :] = leave
            k_ref[u, c] = jnp.broadcast_to(keep, (8, 128))
            sin_ref[u, c] = state
            state_low = state.astype(BF16)
            total = inner + enter * dot(cc_ref[rows, :], state_low, NN)
            yn_ref[u, rows, :] = total
            od_ref[rows, lanes_d[u]] = (total + skip[u] * x).astype(BF16)
            entered = (enter * grad).astype(BF16)
            ed_ref[u, rows, :] = entered
            new_state = keep * state + dot(bt_ref[c], (leave * value).astype(BF16), NN)
            return new_state, added, dot(entered, state_low, NT)

        def forward(c, states):
            found = [forward_one(u, c, states[u]) for u in each]
            dcb_ref[c] += sum(f[1] for f in found)
            dc_ref[c] += sum(f[2] for f in found)
            return tuple(f[0] for f in found)

        final = lax.fori_loop(0, n, forward, tuple(first_ref[p].astype(F32) for p in ids))
        for u in each:
            sin_ref[u, n] = final[u]
            for j in range(KC + 2):
                acc_ref[u, j] = zero8

        def backward_one(u, c, later):
            rows = rows_of(c)
            later_low = later.astype(BF16)
            leave = lv_ref[u, rows, :]
            x = xc_ref[u, rows, :]
            step = st_ref[u, rows, :]
            grad = xd_ref[rows, lanes_d[u]].astype(F32)
            value = step * x
            grad_value = dwi_ref[u, rows, :] + leave * dot(bb_ref[rows, :], later_low, NN)
            z1 = grad * yn_ref[u, rows, :] - value.astype(BF16).astype(F32) * grad_value
            carried = jnp.sum(later_low.astype(F32) * sin_ref[u, c + 1], axis=0, keepdims=True)
            z1 = jnp.concatenate([z1[: RB - 8], z1[RB - 8 :] + jnp.where(sub[RB - 8 :] == RB - 1, carried, 0.0)], axis=0)
            z1_high = z1.astype(BF16)
            z1_rest = (z1 - z1_high.astype(F32)).astype(BF16)
            rates = dot(pick[u], z1_high, NT) + dot(pick[u], z1_rest, NT)
            steps = dot(pick[u], (x * grad_value).astype(BF16), NT)
            grad_b = dot((leave * value).astype(BF16), later_low, NT)
            grad_x = (step * grad_value + skip[u] * grad) * ds_ref[u, rows, :]
            back, sums = conv_back(c, grad_x, xs_ref.at[u], slice(None), weight[u], u)
            od_ref[rows, lanes[u]] = back.astype(BF16)
            sums.append(by_sublane(grad * x))
            for j in range(KC + 2):
                acc_ref[u, j] += sums[j]
            new_later = k_ref[u, c][:1] * later + dot(ct_ref[c], ed_ref[u, rows, :], NN)
            return new_later, rates, steps, grad_b

        def backward(k, laters):
            c = n - 1 - k
            found = [backward_one(u, c, laters[u]) for u in each]
            z1_ref[c] += sum(f[1] for f in found)
            z2_ref[c] += sum(f[2] for f in found)
            db_ref[c] += sum(f[3] for f in found)
            return tuple(f[0] for f in found)

        lax.fori_loop(0, n, backward, tuple(later_ref[p].astype(F32) for p in ids))
        for u in each:
            found = [jnp.sum(acc_ref[u, j], axis=0, keepdims=True) for j in range(KC + 2)]
            skip_ref[...] += pick[u].astype(F32) * found[KC + 1]
            found = found[: KC + 1] + [jnp.zeros((8 - KC - 1, 128), F32)]
            edge_out[0][pl.ds(pl.multiple_of(sums_at + 8 * ids[u], 8), 8), :] = jnp.concatenate(found, axis=0)
            edge_out[0][pl.ds(pl.multiple_of(hp + 8 * ids[u], 8), 8), :] = margin_of(weight[u], u)
        return carry

    lax.fori_loop(0, pairs // wide, streams, 0)

    for side in range(2):
        lanes = slice(128 * side, 128 * side + 128)
        weight = wbc[:, lanes]
        bias = bbc[:, lanes]
        for j in range(KC + 1):
            acc_ref[0, j] = zero8

        def finish(k, carry):
            c = n - 1 - k
            rows = rows_of(c)
            mixed = dcb_ref[c].astype(BF16)
            if side == 0:
                grad = db_ref[c] + dot(mixed, cc_ref[rows, :], TN)
            else:
                grad = dc_ref[c] + dot(mixed, bb_ref[rows, :], NN)
            pre = conv(c, raw_ref, lanes, weight, bias)
            back, sums = conv_back(c, grad * silu_parts(pre)[1], raw_ref, lanes, weight, 0)
            og_ref[rows, lanes] = back.astype(BF16)
            for j in range(KC + 1):
                acc_ref[0, j] += sums[j]
            return carry

        lax.fori_loop(0, n, finish, 0)
        found = [jnp.sum(acc_ref[0, j], axis=0, keepdims=True) for j in range(KC + 1)]
        found.append(jnp.zeros((8 - KC - 1, 128), F32))
        at_row = 8 * pairs + 8 * side
        edge_out[0][sums_at + at_row : sums_at + at_row + 8, :] = jnp.concatenate(found, axis=0)
        edge_out[0][hp + at_row : hp + at_row + 8, :] = margin_of(weight, 0)

    later_sum = (sub >= lane).astype(F32)
    sum_log = jnp.zeros((hp, 128), F32)
    sum_step = jnp.zeros((hp, 128), F32)
    for m in range(n):
        c = me ^ m
        rate_grad = dot(z1_ref[c], later_sum, NN, HIGHEST)
        step_grad = z2_ref[c] - e_log * rate_grad
        logit_grad = step_grad * sg_ref[c]
        sum_log = sum_log - step_ref[c] * e_log * rate_grad
        sum_step = sum_step + logit_grad
        edge_out[m][:hp, :] = logit_grad
        big_out[m][...] = od_ref[rows_of(c), :]
        bc_out[m][...] = og_ref[rows_of(c), :]
    at_row = sums_at + 8 * pairs + 16
    edge_out[0][at_row : at_row + hp, :] = sum_log
    edge_out[0][at_row + hp : at_row + 2 * hp, :] = sum_step
    edge_out[0][at_row + 2 * hp : at_row + 3 * hp, :] = skip_ref[...]
    for m in range(1, n):
        edge_out[m][hp:, :] = edge_out[0][hp:, :]


def mixer_call(n, heads, hp, idx, doc, ins, first, later):
    width = heads * MP
    pairs = width // 128
    wide = 2 - pairs % 2
    tokens = n * RB
    square = pltpu.VMEM((n, RB, RB), F32)
    flat = pltpu.VMEM((wide, tokens, 128), F32)
    per_head = pltpu.VMEM((n, hp, 128), F32)
    return pl.pallas_call(
        lambda *refs: mixer_kernel(n, heads, hp, wide, *refs),
        out_shape=[jax.ShapeDtypeStruct((RB, 2 * width), BF16)] * n
        + [jax.ShapeDtypeStruct((RB, 256), BF16)] * n
        + [jax.ShapeDtypeStruct((4 * hp + 16 * pairs + 32, 128), F32)] * n,
        in_specs=[smem(), smem()] + [vmem()] * (len(ins) + 2),
        out_specs=[vmem()] * (3 * n),
        scratch_shapes=[
            pltpu.VMEM((tokens, 2 * width), BF16),
            pltpu.VMEM((tokens, 256), BF16),
            pltpu.VMEM((wide, KC - 1, tokens + 8, 128), F32),
            square,
            square,
            square,
            per_head,
            per_head,
            pltpu.VMEM((wide, n + 1, 128, 128), F32),
            flat,
            flat,
            flat,
            flat,
            flat,
            flat,
            pltpu.VMEM((wide, tokens, 128), BF16),
            pltpu.VMEM((wide, n, 8, 128), F32),
            pltpu.VMEM((wide, KC + 2, 8, 128), F32),
            pltpu.VMEM((hp, 128), F32),
        ]
        + shared_scratch(n, heads, hp, wide, True),
        compiler_params=params(),
        name="mixer",
    )(idx, doc, *ins, first, later)


def program(
    mixer_x,
    mixer_bc,
    dt_raw,
    gate_z,
    conv_weight_x,
    conv_bias_x,
    conv_weight_bc,
    conv_bias_bc,
    a_log,
    dt_bias,
    skip_d,
    d_mixer,
    doc_lengths,
    att_queries,
    att_keys,
    att_values,
    d_attn,
):
    n = lax.axis_size("ctx")
    group = min(4, n)
    place = lax.axis_index("ctx")
    inside = place % group
    idx = jnp.stack([inside, place]).astype(jnp.int32)
    rows, channels = mixer_x.shape
    all_heads = channels // MP
    heads = all_heads // group
    hp = heads
    width = heads * MP
    pairs = width // 128
    reach = max(1, n // 2)

    sent = keys_call(group, att_keys, att_values, mixer_x, mixer_bc)
    own = sent[0]
    reached = [shifted(sent[d] if d <= group else own, "ctx", d) for d in range(1, max(reach, group) + 1)]
    tails = reached[:group]
    blocks = reached[:reach][::-1] + [own]

    logits = jnp.pad(dt_raw, ((0, 0), (0, 128 - all_heads)))
    packed = pack_call(group, heads, idx, mixer_x, gate_z, d_mixer, mixer_bc, logits)
    big = [packed[0]] + [crossed(packed[m], "ctx", m) for m in range(1, group)]

    head_params = jnp.stack([a_log, dt_bias, skip_d])
    head_params = lax.dynamic_slice_in_dim(head_params, inside * heads, heads, 1)
    head_params = jnp.broadcast_to(head_params[:, :, None], (3, hp, 128))
    ins = (
        big
        + tails
        + [conv_weight_x, conv_bias_x[None], conv_weight_bc, conv_bias_bc[None], head_params]
    )
    state, grad_state, keep = totals_call(group, heads, hp, idx, doc_lengths, ins)
    back_state, back_keep = grad_state, keep
    covered = 1
    while covered < n // group // 2:
        step_by = covered * group
        state = (state.astype(F32) + keep[:, :1] * shifted(state, "ctx", step_by).astype(F32)).astype(BF16)
        back_state = (
            back_state.astype(F32) + back_keep[:, :1] * shifted(back_state, "ctx", -step_by).astype(F32)
        ).astype(BF16)
        keep = keep * shifted(keep, "ctx", step_by)
        back_keep = back_keep * shifted(back_keep, "ctx", -step_by)
        covered = 2 * covered
    first = shifted(state, "ctx", group)
    later = shifted(back_state, "ctx", -group)

    attended = attention_call(idx, doc_lengths, att_queries, d_attn, blocks)
    grad_queries = attended[0]
    grad_kv = attended[-1]
    arrived = [shifted(attended[1 + reach - d], "ctx", -d) for d in range(1, reach + 1)]
    for part in arrived:
        grad_kv = grad_kv + part.astype(F32)
    kv_width = att_keys.shape[1]
    grad_keys = grad_kv[:, :kv_width].astype(BF16)
    grad_values = grad_kv[:, kv_width:].astype(BF16)

    results = mixer_call(group, heads, hp, idx, doc_lengths, ins, first, later)
    edges = [results[2 * group]] + [crossed(results[2 * group + m], "ctx", m) for m in range(1, group)]
    bc_parts = [results[group]] + [crossed(results[group + m], "ctx", m) for m in range(1, group)]
    big = [results[0]] + [crossed(results[m], "ctx", m) for m in range(1, group)]

    grad_logits, margin, share = edges_call(group, hp, pairs, idx, edges)
    margin = shifted(margin, "ctx", -1)
    mask = group
    while mask < n:
        share = share + crossed(share, "ctx", mask)
        mask = 2 * mask

    bc_sum = bc_parts[0].astype(F32)
    for m in range(1, group):
        bc_sum = bc_sum + bc_parts[m].astype(F32)
    bc_margin = jnp.where(inside == group - 1, margin[:, channels:], 0.0)
    bc_sum = jnp.concatenate([bc_sum[: rows - 8], bc_sum[rows - 8 :] + bc_margin], axis=0)
    both = jnp.concatenate([bc_sum, share[:, channels : channels + 256]], axis=0)
    total = both
    for m in range(1, lax.axis_size("head")):
        total = total + crossed(both, "head", m)
    grad_bc = total[:rows].astype(BF16)
    grad_weight_bc = total[rows : rows + KC]
    grad_bias_bc = total[rows + KC]

    grad_x, grad_z, taps, bias_sum, head_sums = unpack_call(group, hp, idx, gate_z, d_mixer, margin, share, big)
    return (
        grad_x,
        grad_bc,
        grad_logits,
        grad_z,
        taps,
        bias_sum[0],
        grad_weight_bc,
        grad_bias_bc,
        head_sums[0],
        head_sums[1],
        head_sums[2],
        grad_queries,
        grad_keys,
        grad_values,
    )


def solution(mesh):
    placed = (
        P("ctx", "head"),
        P("ctx", None),
        P("ctx", "head"),
        P("ctx", "head"),
        P(None, "head"),
        P("head"),
        P(),
        P(),
        P("head"),
        P("head"),
        P("head"),
        P("ctx", "head"),
        P(),
        P("ctx", "head"),
        P("ctx", "head"),
        P("ctx", "head"),
        P("ctx", "head"),
    )
    return jax.shard_map(
        program,
        mesh=mesh,
        in_specs=placed,
        out_specs=(
            P("ctx", "head"),
            P("ctx", None),
            P("ctx", "head"),
            P("ctx", "head"),
            P(None, "head"),
            P("head"),
            P(),
            P(),
            P("head"),
            P("head"),
            P("head"),
            P("ctx", "head"),
            P("ctx", "head"),
            P("ctx", "head"),
        ),
        check_vma=False,
    )
```

time: 263 us -> 198 us (0.75)
  the two profiles are of different devices: /device:TPU:16 before, /device:TPU:0 now
where the time goes in v2:
time: 198 us; the launch traced here: 197 us
  starting transfers between devices  69.7 us (35%)
  Pallas kernels  64.9 us (33%)
  waiting for transfers between devices  50.6 us (26%)
  local copies, waits for them, and re-layouts  10.1 us (5%)
    ppermute x16, starting transfers between devices, crossed(): lax.ppermute(value, axis, [(source, source ^ mask) for source in range(co...  39.4 us
    ppermute x11, waiting for transfers between devices, shifted(): lax.ppermute(value, axis, [(source, source + steps) for source in range(i...  37.2 us
    ppermute x11, starting transfers between devices, shifted(): lax.ppermute(value, axis, [(source, source + steps) for source in range(i...  30.3 us
    pallas_call x1, Pallas kernels, mixer_call(): pl.pallas_call(lambda *refs: mixer_kernel(n, heads, hp, wide, *refs), out...  26.6 us
    pallas_call x1, Pallas kernels, attention_call(): pl.pallas_call(lambda *refs: attention_kernel(nb - 1, *refs), out_shape=o...  15.4 us
    ppermute x16, waiting for transfers between devices, crossed(): lax.ppermute(value, axis, [(source, source ^ mask) for source in range(co...  13.5 us
    pallas_call x1, Pallas kernels, totals_call(): pl.pallas_call(lambda *refs: totals_kernel(n, heads, hp, wide, *refs), ou...  10.3 us
    unnamed x58, local copies, waits for them, and re-layouts  4.86 us
  transfers between devices with their start and end apart: 27, of which 9 were waited for; matrix products, arithmetic and copies ran while one was open for 2% of the time, Pallas kernels for 10%

profile of v2, /device:TPU:0, one launch (start us, length us, event | category | flops | bytes accessed | tf_op | source)
XLA Modules:
  0.0 197.3 jit_solution(6458173923093607256)
XLA Ops:
  0.7 0.8 copy.31
  2.1 0.6 pad.4.refs_5_
  2.7 3.7 %pack.1 = (bf16[128,2432]{1,0:T(8,128)(2,1)}, bf16[128,2432]{1,0:T(8,128)(2,1)}, bf16[128,2432]{1,0:T(8,128)(2,1)}, bf16[128,2432]{1,0:T(8,128)(2,1)}) custom-call(s32[2]{0:T(128)} %pad_add_fusion.refs_0_, bf16[128,4096]{1,0:T(8,128)(2,1)} %refs_2_.5, bf16[128,4096]{1,0:T(8,128)(2,1)} %refs_1_.10, bf16[128,4096]{1,0:T(8,128)(2,1)} %refs_2_.6, ...), custom_call_target="tpu_custom_call" | custom-call | tf_op jit(solution)/shard_map/pack/pallas_call | solution.py:174
  6.5 3.0 %collective-permute-start = (bf16[128,2432]{1,0:T(8,128)(2,1)}, bf16[128,2432]{1,0:T(8,128)(2,1)S(1)}, u32[]{:S(2)}, u32[]{:S(2)}) collective-permute-start(bf16[128,2432]{1,0:T(8,128)(2,1)} %get-tuple-element.52), channel_id=1, source_target_pairs={{0,4},{4,0},{8,12},{12,8},{16,20},{20,16},{24,28},{28,24},{1,5},{5... | collective-permute-start | bytes 1867784 | tf_op jit(solution)/shard_map/ppermute | solution.py:35
  9.5 1.6 collective-permute-start.1
  11.0 1.9 keys.1
  13.0 3.8 %collective-permute-start.3 = (bf16[176,512]{1,0:T(8,128)(2,1)}, bf16[176,512]{1,0:T(8,128)(2,1)S(1)}, u32[]{:S(2)}, u32[]{:S(2)}) collective-permute-start(bf16[176,512]{1,0:T(8,128)(2,1)} %get-tuple-element.55), channel_id=1, source_target_pairs={{0,4},{4,8},{8,12},{12,16},{16,20},{20,24},{24,28},{1,5},{5,9},{9,... | collective-permute-start | bytes 540680 | tf_op jit(solution)/shard_map/ppermute | solution.py:30
  16.8 3.5 %collective-permute-start.4 = (bf16[176,512]{1,0:T(8,128)(2,1)}, bf16[176,512]{1,0:T(8,128)(2,1)S(1)}, u32[]{:S(2)}, u32[]{:S(2)}) collective-permute-start(bf16[176,512]{1,0:T(8,128)(2,1)} %get-tuple-element.56), channel_id=1, source_target_pairs={{0,8},{4,12},{8,16},{12,20},{16,24},{20,28},{1,9},{5,13},{9,17},{1... | collective-permute-start | bytes 540680 | tf_op jit(solution)/shard_map/ppermute | solution.py:30
  20.3 20.0 %collective-permute-done.3.refs_6_.refs_7_ = bf16[176,512]{1,0:T(8,128)(2,1)S(1)} collective-permute-done((bf16[176,512]{1,0:T(8,128)(2,1)}, bf16[176,512]{1,0:T(8,128)(2,1)S(1)}, u32[]{:S(2)}, u32[]{:S(2)}) %collective-permute-start.3) | collective-permute-done | bytes 180256 | tf_op jit(solution)/shard_map/ppermute | solution.py:30
  40.3 5.3 %collective-permute-start.5 = (bf16[176,512]{1,0:T(8,128)(2,1)}, bf16[176,512]{1,0:T(8,128)(2,1)S(1)}, u32[]{:S(2)}, u32[]{:S(2)}) collective-permute-start(bf16[176,512]{1,0:T(8,128)(2,1)} %get-tuple-element.57), channel_id=1, source_target_pairs={{0,12},{4,16},{8,20},{12,24},{16,28},{1,13},{5,17},{9,21},{13,25},... | collective-permute-start | bytes 540680 | tf_op jit(solution)/shard_map/ppermute | solution.py:30
  45.6 4.5 %collective-permute-start.6 = (bf16[176,512]{1,0:T(8,128)(2,1)}, bf16[176,512]{1,0:T(8,128)(2,1)S(1)}, u32[]{:S(2)}, u32[]{:S(2)}) collective-permute-start(bf16[176,512]{1,0:T(8,128)(2,1)} %get-tuple-element.58), channel_id=1, source_target_pairs={{0,16},{4,20},{8,24},{12,28},{1,17},{5,21},{9,25},{13,29},{2,18},{... | collective-permute-start | bytes 540680 | tf_op jit(solution)/shard_map/ppermute | solution.py:30
  50.1 0.6 copy-done.21
  50.9 2.5 %collective-permute-done.6.refs_9_.refs_4_ = bf16[176,512]{1,0:T(8,128)(2,1)S(1)} collective-permute-done((bf16[176,512]{1,0:T(8,128)(2,1)}, bf16[176,512]{1,0:T(8,128)(2,1)S(1)}, u32[]{:S(2)}, u32[]{:S(2)}) %collective-permute-start.6) | collective-permute-done | bytes 180256 | tf_op jit(solution)/shard_map/ppermute | solution.py:30
  53.4 0.8 broadcast_in_dim.18.refs_14_
  54.7 10.3 %totals.1 = (bf16[8,128,128]{2,1,0:T(8,128)(2,1)}, bf16[8,128,128]{2,1,0:T(8,128)(2,1)}, f32[8,8,128]{2,1,0:T(8,128)}) custom-call(s32[2]{0:T(128)} %pad_add_fusion.refs_0_, s32[8]{0:T(128)} %refs_1_.11, bf16[128,2432]{1,0:T(8,128)(2,1)} %get-tuple-element.51.refs_2_, bf16[128,2432]{1,0:T(8,128)(2,1)} %copy-done, bf16[128,2432]{1,0:T(8,128)(2,1)} %copy-done.1, ...), custom_call_target="tpu_custom_call" | custom-call | tf_op jit(solution)/shard_map/totals/pallas_call | solution.py:481
  65.0 5.2 %collective-permute-start.7 = (bf16[8,128,128]{2,1,0:T(8,128)(2,1)}, bf16[8,128,128]{2,1,0:T(8,128)(2,1)S(1)}, u32[]{:S(2)}, u32[]{:S(2)}) collective-permute-start(bf16[8,128,128]{2,1,0:T(8,128)(2,1)} %get-tuple-element.59), channel_id=1, source_target_pairs={{0,16},{4,20},{8,24},{12,28},{1,17},{5,21},{9,25},{13,29},{2,18},{... | collective-permute-start | bytes 786440 | tf_op jit(solution)/shard_map/ppermute | solution.py:30
  70.2 1.3 collective-permute-start.8
  71.5 2.9 %collective-permute-done.7.refs_15_ = bf16[8,128,128]{2,1,0:T(8,128)(2,1)S(1)} collective-permute-done((bf16[8,128,128]{2,1,0:T(8,128)(2,1)}, bf16[8,128,128]{2,1,0:T(8,128)(2,1)S(1)}, u32[]{:S(2)}, u32[]{:S(2)}) %collective-permute-start.7) | collective-permute-done | bytes 262176 | tf_op jit(solution)/shard_map/ppermute | solution.py:30
  74.3 5.2 %collective-permute-done.8.refs_16_ = bf16[8,128,128]{2,1,0:T(8,128)(2,1)S(1)} collective-permute-done((bf16[8,128,128]{2,1,0:T(8,128)(2,1)}, bf16[8,128,128]{2,1,0:T(8,128)(2,1)S(1)}, u32[]{:S(2)}, u32[]{:S(2)}) %collective-permute-start.8) | collective-permute-done | bytes 262176 | tf_op jit(solution)/shard_map/ppermute | solution.py:30
  79.6 0.7 copy-done.13
  80.3 26.6 %mixer.1 = (bf16[128,2048]{1,0:T(8,128)(2,1)}, bf16[128,2048]{1,0:T(8,128)(2,1)}, bf16[128,2048]{1,0:T(8,128)(2,1)}, bf16[128,2048]{1,0:T(8,128)(2,1)}, bf16[128...) custom-call(s32[2]{0:T(128)} %pad_add_fusion.refs_0_, ...), custom_call_target="tpu_custom_call" | custom-call | tf_op jit(solution)/shard_map/mixer/pallas_call | solution.py:754
  106.8 3.3 %collective-permute-start.9 = (f32[224,128]{1,0:T(8,128)}, f32[224,128]{1,0:T(8,128)S(1)}, u32[]{:S(2)}, u32[]{:S(2)}) collective-permute-start(f32[224,128]{1,0:T(8,128)} %get-tuple-element.62), channel_id=1, source_target_pairs={{0,4},{4,0},{8,12},{12,8},{16,20},{20,16},{24,28},{28,24},{1,5},{5... | collective-permute-start | bytes 344072 | tf_op jit(solution)/shard_map/ppermute | solution.py:35
  110.1 7.8 %collective-permute-start.10 = (f32[224,128]{1,0:T(8,128)}, f32[224,128]{1,0:T(8,128)S(1)}, u32[]{:S(2)}, u32[]{:S(2)}) collective-permute-start(f32[224,128]{1,0:T(8,128)} %get-tuple-element.63), channel_id=1, source_target_pairs={{0,8},{4,12},{8,0},{12,4},{16,24},{20,28},{24,16},{28,20},{1,9},{5... | collective-permute-start | bytes 344072 | tf_op jit(solution)/shard_map/ppermute | solution.py:35
  117.9 2.9 %collective-permute-start.19 = (bf16[128,256]{1,0:T(8,128)(2,1)}, bf16[128,256]{1,0:T(8,128)(2,1)S(1)}, u32[]{:S(2)}, u32[]{:S(2)}) collective-permute-start(bf16[128,256]{1,0:T(8,128)(2,1)} %get-tuple-element.75), channel_id=1, source_target_pairs={{0,12},{4,8},{8,4},{12,0},{16,28},{20,24},{24,20},{28,16},{1,13},{... | collective-permute-start | bytes 196616 | tf_op jit(solution)/shard_map/ppermute | solution.py:35
  121.5 15.4 %attention.1 = (bf16[128,2048]{1,0:T(8,128)(2,1)}, bf16[128,512]{1,0:T(8,128)(2,1)}, bf16[128,512]{1,0:T(8,128)(2,1)}, bf16[128,512]{1,0:T(8,128)(2,1)}, bf16[128,512]{1,0:T(8,128)(2,1)}, /*index=5*/f32[128,512]{1,0:T(8,128)}) custom-call(s32[2]{0:T(128)} %pad_add_fusion.refs_0_, s32[8]{0:T(128)} %refs_1_.11, bf16[128,2048]{1,0:T(8,128)(2,1)} %refs_2_.7, ...), custom_call_target="tpu_custom_call" | custom-call | tf_op jit(solution)/shard_map/attention/pallas_call | solution.py:131
  136.9 1.4 collective-permute-start.26
  138.4 1.3 collective-permute-start.25
  139.7 2.2 %edges.1 = (f32[128,64]{1,0:T(8,128)}, f32[8,4352]{1,0:T(8,128)}, f32[8,4544]{1,0:T(8,128)}) custom-call(s32[2]{0:T(128)} %pad_add_fusion.refs_0_, f32[224,128]{1,0:T(8,128)} %get-tuple-element.61.refs_1_, f32[224,128]{1,0:T(8,128)} %copy-done.16, f32[224,128]{1,0:T(8,128)} %copy-done.17, f32[224,128]{1,0:T(8,128)} %copy-done.18), custom_call_target="tpu_custom_call" | custom-call | tf_op jit(solution)/shard_map/edges/pallas_call | solution.py:255
  141.9 1.3 collective-permute-start.24
  143.3 1.3 collective-permute-start.23
  144.6 1.5 collective-permute-start.12
  146.1 6.6 %collective-permute-done.12.refs_3_ = f32[8,4352]{1,0:T(8,128)S(1)} collective-permute-done((f32[8,4352]{1,0:T(8,128)}, f32[8,4352]{1,0:T(8,128)S(1)}, u32[]{:S(2)}, u32[]{:S(2)}) %collective-permute-start.12) | collective-permute-done | bytes 139296 | tf_op jit(solution)/shard_map/ppermute | solution.py:30
  152.7 10.2 %collective-permute-start.13 = (f32[8,4544]{1,0:T(8,128)S(1)}, f32[8,4544]{1,0:T(8,128)S(1)}, u32[]{:S(2)}, u32[]{:S(2)}) collective-permute-start(f32[8,4544]{1,0:T(8,128)S(1)} %copy-done.15), channel_id=1, source_target_pairs={{0,16},{4,20},{8,24},{12,28},{16,0},{20,4},{24,8},{28,12},{1,17},{... | collective-permute-start | bytes 436232 | tf_op jit(solution)/shard_map/ppermute | solution.py:35
  162.9 3.4 %collective-permute-done.13 = f32[8,4544]{1,0:T(8,128)S(1)} collective-permute-done((f32[8,4544]{1,0:T(8,128)S(1)}, f32[8,4544]{1,0:T(8,128)S(1)}, u32[]{:S(2)}, u32[]{:S(2)}) %collective-permute-start.13) | collective-permute-done | bytes 145440 | tf_op jit(solution)/shard_map/ppermute | solution.py:35
  166.4 0.7 collective-permute-start.14
  167.1 0.6 copy-done.7
  167.8 7.4 %collective-permute-start.15 = (bf16[128,2048]{1,0:T(8,128)(2,1)S(1)}, bf16[128,2048]{1,0:T(8,128)(2,1)S(1)}, u32[]{:S(2)}, u32[]{:S(2)}) collective-permute-start(bf16[128,2048]{1,0:T(8,128)(2,1)S(1)} %copy-done.25), channel_id=1, source_target_pairs={{0,8},{4,12},{8,0},{12,4},{16,24},{20,28},{24,16},{28,20},{1,9},{5... | collective-permute-start | bytes 1572872 | tf_op jit(solution)/shard_map/ppermute | solution.py:35
  175.4 1.6 collective-permute-start.21
  177.0 4.2 %collective-permute-done.22 = f32[136,256]{1,0:T(8,128)S(1)} collective-permute-done((f32[136,256]{1,0:T(8,128)S(1)}, f32[136,256]{1,0:T(8,128)S(1)}, u32[]{:S(2)}, u32[]{:S(2)}) %collective-permute-start.22) | collective-permute-done | bytes 139296 | tf_op jit(solution)/shard_map/ppermute | solution.py:35
  181.4 0.7 fusion.1
  182.1 0.7 copy.32
  182.8 1.4 collective-permute-done.21
  184.2 0.6 slice.68
  184.9 0.6 slice.56
  186.1 4.4 %collective-permute-done.16.refs_8_ = bf16[128,2048]{1,0:T(8,128)(2,1)S(1)} collective-permute-done((bf16[128,2048]{1,0:T(8,128)(2,1)S(1)}, bf16[128,2048]{1,0:T(8,128)(2,1)S(1)}, u32[]{:S(2)}, u32[]{:S(2)}) %collective-permute-start.16) | collective-permute-done | bytes 524320 | tf_op jit(solution)/shard_map/ppermute | solution.py:35
  190.5 0.8 copy-done.10
  191.2 4.8 %unpack.1 = (bf16[128,4096]{1,0:T(8,128)(2,1)}, bf16[128,4096]{1,0:T(8,128)(2,1)}, f32[4,4096]{1,0:T(4,128)}, f32[1,4096]{1,0:T(1,128)}, f32[3,64]{1,0:T(4,128)}) custom-call(s32[2]{0:T(128)} %pad_add_fusion.refs_0_, bf16[128,4096]{1,0:T(8,128)(2,1)} %refs_1_.10, bf16[128,4096]{1,0:T(8,128)(2,1)} %refs_2_.6, f32[8,4352]{1,0:T(8,128)} %copy-done.14, ...), custom_call_target="tpu_custom_call" | custom-call | tf_op jit(solution)/shard_map/unpack/pallas_call | solution.py:297
  196.0 1.3 slice_bitcast_fusion
  (89 shorter events, 3.0 us)
Async XLA Ops:
  6.5 46.9 %collective-permute-start = (bf16[128,2432]{1,0:T(8,128)(2,1)}, bf16[128,2432]{1,0:T(8,128)(2,1)S(1)}, u32[]{:S(2)}, u32[]{:S(2)}) collective-permute-start(bf16[128,2432]{1,0:T(8,128)(2,1)} %get-tuple-element.52), channel_id=1, source_target_pairs={{0,4},{4,0},{8,12},{12,8},{16,20},{20,16},{24,28},{28,24},{1,5},{5... | collective-permute-start | bytes 1867784 | tf_op jit(solution)/shard_map/ppermute | solution.py:35
  9.5 43.9 %collective-permute-start.1 = (bf16[128,2432]{1,0:T(8,128)(2,1)}, bf16[128,2432]{1,0:T(8,128)(2,1)S(1)}, u32[]{:S(2)}, u32[]{:S(2)}) collective-permute-start(bf16[128,2432]{1,0:T(8,128)(2,1)} %get-tuple-element.53), channel_id=1, source_target_pairs={{0,8},{4,12},{8,0},{12,4},{16,24},{20,28},{24,16},{28,20},{1,9},{5... | collective-permute-start | bytes 1867784 | tf_op jit(solution)/shard_map/ppermute | solution.py:35
  11.0 42.4 %collective-permute-start.2 = (bf16[128,2432]{1,0:T(8,128)(2,1)}, bf16[128,2432]{1,0:T(8,128)(2,1)S(1)}, u32[]{:S(2)}, u32[]{:S(2)}) collective-permute-start(bf16[128,2432]{1,0:T(8,128)(2,1)} %get-tuple-element.54), channel_id=1, source_target_pairs={{0,12},{4,8},{8,4},{12,0},{16,28},{20,24},{24,20},{28,16},{1,13},{... | collective-permute-start | bytes 1867784 | tf_op jit(solution)/shard_map/ppermute | solution.py:35
  13.0 27.3 %collective-permute-start.3 = (bf16[176,512]{1,0:T(8,128)(2,1)}, bf16[176,512]{1,0:T(8,128)(2,1)S(1)}, u32[]{:S(2)}, u32[]{:S(2)}) collective-permute-start(bf16[176,512]{1,0:T(8,128)(2,1)} %get-tuple-element.55), channel_id=1, source_target_pairs={{0,4},{4,8},{8,12},{12,16},{16,20},{20,24},{24,28},{1,5},{5,9},{9,... | collective-permute-start | bytes 540680 | tf_op jit(solution)/shard_map/ppermute | solution.py:30
  16.8 28.8 %collective-permute-start.4 = (bf16[176,512]{1,0:T(8,128)(2,1)}, bf16[176,512]{1,0:T(8,128)(2,1)S(1)}, u32[]{:S(2)}, u32[]{:S(2)}) collective-permute-start(bf16[176,512]{1,0:T(8,128)(2,1)} %get-tuple-element.56), channel_id=1, source_target_pairs={{0,8},{4,12},{8,16},{12,20},{16,24},{20,28},{1,9},{5,13},{9,17},{1... | collective-permute-start | bytes 540680 | tf_op jit(solution)/shard_map/ppermute | solution.py:30
  40.3 14.0 %copy-start.3 = (bf16[176,512]{1,0:T(8,128)(2,1)}, bf16[176,512]{1,0:T(8,128)(2,1)S(1)}, u32[]{:S(2)}) copy-start(bf16[176,512]{1,0:T(8,128)(2,1)S(1)} %collective-permute-done.3.refs_6_.refs_7_) | copy-start | bytes 540676
  40.3 10.6 %collective-permute-start.5 = (bf16[176,512]{1,0:T(8,128)(2,1)}, bf16[176,512]{1,0:T(8,128)(2,1)S(1)}, u32[]{:S(2)}, u32[]{:S(2)}) collective-permute-start(bf16[176,512]{1,0:T(8,128)(2,1)} %get-tuple-element.57), channel_id=1, source_target_pairs={{0,12},{4,16},{8,20},{12,24},{16,28},{1,13},{5,17},{9,21},{13,25},... | collective-permute-start | bytes 540680 | tf_op jit(solution)/shard_map/ppermute | solution.py:30
  45.6 8.7 %copy-start.4 = (bf16[176,512]{1,0:T(8,128)(2,1)}, bf16[176,512]{1,0:T(8,128)(2,1)S(1)}, u32[]{:S(2)}) copy-start(bf16[176,512]{1,0:T(8,128)(2,1)S(1)} %collective-permute-done.4.refs_7_.refs_6_) | copy-start | bytes 540676
  45.6 7.8 %collective-permute-start.6 = (bf16[176,512]{1,0:T(8,128)(2,1)}, bf16[176,512]{1,0:T(8,128)(2,1)S(1)}, u32[]{:S(2)}, u32[]{:S(2)}) collective-permute-start(bf16[176,512]{1,0:T(8,128)(2,1)} %get-tuple-element.58), channel_id=1, source_target_pairs={{0,16},{4,20},{8,24},{12,28},{1,17},{5,21},{9,25},{13,29},{2,18},{... | collective-permute-start | bytes 540680 | tf_op jit(solution)/shard_map/ppermute | solution.py:30
  50.9 3.4 %copy-start.5 = (bf16[176,512]{1,0:T(8,128)(2,1)}, bf16[176,512]{1,0:T(8,128)(2,1)S(1)}, u32[]{:S(2)}) copy-start(bf16[176,512]{1,0:T(8,128)(2,1)S(1)} %collective-permute-done.5.refs_8_.refs_5_) | copy-start | bytes 540676
  53.4 0.9 copy-start
  53.4 1.1 copy-start.1
  53.4 1.3 copy-start.2
  65.0 9.4 %collective-permute-start.7 = (bf16[8,128,128]{2,1,0:T(8,128)(2,1)}, bf16[8,128,128]{2,1,0:T(8,128)(2,1)S(1)}, u32[]{:S(2)}, u32[]{:S(2)}) collective-permute-start(bf16[8,128,128]{2,1,0:T(8,128)(2,1)} %get-tuple-element.59), channel_id=1, source_target_pairs={{0,16},{4,20},{8,24},{12,28},{1,17},{5,21},{9,25},{13,29},{2,18},{... | collective-permute-start | bytes 786440 | tf_op jit(solution)/shard_map/ppermute | solution.py:30
  70.2 9.4 %collective-permute-start.8 = (bf16[8,128,128]{2,1,0:T(8,128)(2,1)}, bf16[8,128,128]{2,1,0:T(8,128)(2,1)S(1)}, u32[]{:S(2)}, u32[]{:S(2)}) collective-permute-start(bf16[8,128,128]{2,1,0:T(8,128)(2,1)} %get-tuple-element.60), channel_id=1, source_target_pairs={{16,0},{20,4},{24,8},{28,12},{17,1},{21,5},{25,9},{29,13},{18,2},{... | collective-permute-start | bytes 786440 | tf_op jit(solution)/shard_map/ppermute | solution.py:30
  74.3 5.2 %copy-start.12 = (bf16[8,128,128]{2,1,0:T(8,128)(2,1)}, bf16[8,128,128]{2,1,0:T(8,128)(2,1)S(1)}, u32[]{:S(2)}) copy-start(bf16[8,128,128]{2,1,0:T(8,128)(2,1)S(1)} %collective-permute-done.7.refs_15_) | copy-start | bytes 786436
  106.8 14.0 %collective-permute-start.9 = (f32[224,128]{1,0:T(8,128)}, f32[224,128]{1,0:T(8,128)S(1)}, u32[]{:S(2)}, u32[]{:S(2)}) collective-permute-start(f32[224,128]{1,0:T(8,128)} %get-tuple-element.62), channel_id=1, source_target_pairs={{0,4},{4,0},{8,12},{12,8},{16,20},{20,16},{24,28},{28,24},{1,5},{5... | collective-permute-start | bytes 344072 | tf_op jit(solution)/shard_map/ppermute | solution.py:35
  110.1 26.8 %collective-permute-start.10 = (f32[224,128]{1,0:T(8,128)}, f32[224,128]{1,0:T(8,128)S(1)}, u32[]{:S(2)}, u32[]{:S(2)}) collective-permute-start(f32[224,128]{1,0:T(8,128)} %get-tuple-element.63), channel_id=1, source_target_pairs={{0,8},{4,12},{8,0},{12,4},{16,24},{20,28},{24,16},{28,20},{1,9},{5... | collective-permute-start | bytes 344072 | tf_op jit(solution)/shard_map/ppermute | solution.py:35
  117.9 20.4 %collective-permute-start.11 = (f32[224,128]{1,0:T(8,128)}, f32[224,128]{1,0:T(8,128)S(1)}, u32[]{:S(2)}, u32[]{:S(2)}) collective-permute-start(f32[224,128]{1,0:T(8,128)} %get-tuple-element.64), channel_id=1, source_target_pairs={{0,12},{4,8},{8,4},{12,0},{16,28},{20,24},{24,20},{28,16},{1,13},{... | collective-permute-start | bytes 344072 | tf_op jit(solution)/shard_map/ppermute | solution.py:35
  117.9 24.0 %collective-permute-start.19 = (bf16[128,256]{1,0:T(8,128)(2,1)}, bf16[128,256]{1,0:T(8,128)(2,1)S(1)}, u32[]{:S(2)}, u32[]{:S(2)}) collective-permute-start(bf16[128,256]{1,0:T(8,128)(2,1)} %get-tuple-element.75), channel_id=1, source_target_pairs={{0,12},{4,8},{8,4},{12,0},{16,28},{20,24},{24,20},{28,16},{1,13},{... | collective-permute-start | bytes 196616 | tf_op jit(solution)/shard_map/ppermute | solution.py:35
  120.9 22.4 %collective-permute-start.18 = (bf16[128,256]{1,0:T(8,128)(2,1)}, bf16[128,256]{1,0:T(8,128)(2,1)S(1)}, u32[]{:S(2)}, u32[]{:S(2)}) collective-permute-start(bf16[128,256]{1,0:T(8,128)(2,1)} %get-tuple-element.74), channel_id=1, source_target_pairs={{0,8},{4,12},{8,0},{12,4},{16,24},{20,28},{24,16},{28,20},{1,9},{5... | collective-permute-start | bytes 196616 | tf_op jit(solution)/shard_map/ppermute | solution.py:35
  120.9 16.0 %copy-start.16 = (f32[224,128]{1,0:T(8,128)}, f32[224,128]{1,0:T(8,128)S(1)}, u32[]{:S(2)}) copy-start(f32[224,128]{1,0:T(8,128)S(1)} %collective-permute-done.9.refs_2_) | copy-start | bytes 344068
  120.9 23.7 %collective-permute-start.17 = (bf16[128,256]{1,0:T(8,128)(2,1)}, bf16[128,256]{1,0:T(8,128)(2,1)S(1)}, u32[]{:S(2)}, u32[]{:S(2)}) collective-permute-start(bf16[128,256]{1,0:T(8,128)(2,1)} %get-tuple-element.73), channel_id=1, source_target_pairs={{0,4},{4,0},{8,12},{12,8},{16,20},{20,16},{24,28},{28,24},{1,5},{5... | collective-permute-start | bytes 196616 | tf_op jit(solution)/shard_map/ppermute | solution.py:35
  136.9 2.8 %copy-start.17 = (f32[224,128]{1,0:T(8,128)}, f32[224,128]{1,0:T(8,128)S(1)}, u32[]{:S(2)}) copy-start(f32[224,128]{1,0:T(8,128)S(1)} %collective-permute-done.10.refs_3_) | copy-start | bytes 344068
  136.9 5.0 %copy-start.27 = (bf16[128,512]{1,0:T(8,128)(2,1)S(1)}, bf16[128,512]{1,0:T(8,128)(2,1)}, u32[]{:S(2)}) copy-start(bf16[128,512]{1,0:T(8,128)(2,1)} %get-tuple-element.85) | copy-start | bytes 393220
  136.9 6.3 %copy-start.26 = (bf16[128,512]{1,0:T(8,128)(2,1)S(1)}, bf16[128,512]{1,0:T(8,128)(2,1)}, u32[]{:S(2)}) copy-start(bf16[128,512]{1,0:T(8,128)(2,1)} %get-tuple-element.84) | copy-start | bytes 393220
  136.9 30.2 %collective-permute-start.26 = (bf16[128,512]{1,0:T(8,128)(2,1)}, bf16[128,512]{1,0:T(8,128)(2,1)S(1)}, u32[]{:S(2)}, u32[]{:S(2)}) collective-permute-start(bf16[128,512]{1,0:T(8,128)(2,1)} %get-tuple-element.87), channel_id=1, source_target_pairs={{16,0},{20,4},{24,8},{28,12},{17,1},{21,5},{25,9},{29,13},{18,2},{... | collective-permute-start | bytes 393224 | tf_op jit(solution)/shard_map/ppermute | solution.py:30
  138.4 1.3 copy-start.18
  138.4 36.7 %collective-permute-start.25 = (bf16[128,512]{1,0:T(8,128)(2,1)}, bf16[128,512]{1,0:T(8,128)(2,1)S(1)}, u32[]{:S(2)}, u32[]{:S(2)}) collective-permute-start(bf16[128,512]{1,0:T(8,128)(2,1)} %get-tuple-element.86), channel_id=1, source_target_pairs={{12,0},{16,4},{20,8},{24,12},{28,16},{13,1},{17,5},{21,9},{25,13},... | collective-permute-start | bytes 393224 | tf_op jit(solution)/shard_map/ppermute | solution.py:30
  139.7 6.3 %copy-start.20 = (bf16[128,256]{1,0:T(8,128)(2,1)S(1)}, bf16[128,256]{1,0:T(8,128)(2,1)}, u32[]{:S(2)}) copy-start(bf16[128,256]{1,0:T(8,128)(2,1)} %get-tuple-element.72) | copy-start | bytes 196612
  139.7 28.0 %copy-start.25 = (bf16[128,2048]{1,0:T(8,128)(2,1)S(1)}, bf16[128,2048]{1,0:T(8,128)(2,1)}, u32[]{:S(2)}) copy-start(bf16[128,2048]{1,0:T(8,128)(2,1)} %get-tuple-element.69) | copy-start | bytes 1572868
  141.9 33.2 %collective-permute-start.24 = (bf16[128,512]{1,0:T(8,128)(2,1)S(1)}, bf16[128,512]{1,0:T(8,128)(2,1)S(1)}, u32[]{:S(2)}, u32[]{:S(2)}) collective-permute-start(bf16[128,512]{1,0:T(8,128)(2,1)S(1)} %copy-done.27), channel_id=1, source_target_pairs={{8,0},{12,4},{16,8},{20,12},{24,16},{28,20},{9,1},{13,5},{17,9},{2... | collective-permute-start | bytes 393224 | tf_op jit(solution)/shard_map/ppermute | solution.py:30
  143.3 32.0 %collective-permute-start.23 = (bf16[128,512]{1,0:T(8,128)(2,1)S(1)}, bf16[128,512]{1,0:T(8,128)(2,1)S(1)}, u32[]{:S(2)}, u32[]{:S(2)}) collective-permute-start(bf16[128,512]{1,0:T(8,128)(2,1)S(1)} %copy-done.26), channel_id=1, source_target_pairs={{4,0},{8,4},{12,8},{16,12},{20,16},{24,20},{28,24},{5,1},{9,5},{13... | collective-permute-start | bytes 393224 | tf_op jit(solution)/shard_map/ppermute | solution.py:30
  144.6 8.2 %collective-permute-start.12 = (f32[8,4352]{1,0:T(8,128)}, f32[8,4352]{1,0:T(8,128)S(1)}, u32[]{:S(2)}, u32[]{:S(2)}) collective-permute-start(f32[8,4352]{1,0:T(8,128)} %get-tuple-element.65), channel_id=1, source_target_pairs={{4,0},{8,4},{12,8},{16,12},{20,16},{24,20},{28,24},{5,1},{9,5},{13... | collective-permute-start | bytes 417800 | tf_op jit(solution)/shard_map/ppermute | solution.py:30
  146.1 6.6 %copy-start.15 = (f32[8,4544]{1,0:T(8,128)S(1)}, f32[8,4544]{1,0:T(8,128)}, u32[]{:S(2)}) copy-start(f32[8,4544]{1,0:T(8,128)} %get-tuple-element.66) | copy-start | bytes 436228
  146.1 29.0 %copy-start.24 = (bf16[128,2048]{1,0:T(8,128)(2,1)S(1)}, bf16[128,2048]{1,0:T(8,128)(2,1)}, u32[]{:S(2)}) copy-start(bf16[128,2048]{1,0:T(8,128)(2,1)} %get-tuple-element.70) | copy-start | bytes 1572868
  152.7 14.4 %copy-start.14 = (f32[8,4352]{1,0:T(8,128)}, f32[8,4352]{1,0:T(8,128)S(1)}, u32[]{:S(2)}) copy-start(f32[8,4352]{1,0:T(8,128)S(1)} %collective-permute-done.12.refs_3_) | copy-start | bytes 417796
  152.7 13.6 %collective-permute-start.13 = (f32[8,4544]{1,0:T(8,128)S(1)}, f32[8,4544]{1,0:T(8,128)S(1)}, u32[]{:S(2)}, u32[]{:S(2)}) collective-permute-start(f32[8,4544]{1,0:T(8,128)S(1)} %copy-done.15), channel_id=1, source_target_pairs={{0,16},{4,20},{8,24},{12,28},{16,0},{20,4},{24,8},{28,12},{1,17},{... | collective-permute-start | bytes 436232 | tf_op jit(solution)/shard_map/ppermute | solution.py:35
  166.4 8.9 %copy-start.11 = (f32[128,512]{1,0:T(8,128)S(1)}, f32[128,512]{1,0:T(8,128)}, u32[]{:S(2)}) copy-start(f32[128,512]{1,0:T(8,128)} %get-tuple-element.83) | copy-start | bytes 786436
  166.4 19.7 %collective-permute-start.14 = (bf16[128,2048]{1,0:T(8,128)(2,1)}, bf16[128,2048]{1,0:T(8,128)(2,1)S(1)}, u32[]{:S(2)}, u32[]{:S(2)}) collective-permute-start(bf16[128,2048]{1,0:T(8,128)(2,1)} %get-tuple-element.68), channel_id=1, source_target_pairs={{0,4},{4,0},{8,12},{12,8},{16,20},{20,16},{24,28},{28,24},{1,5},{5... | collective-permute-start | bytes 1572872 | tf_op jit(solution)/shard_map/ppermute | solution.py:35
  167.8 18.3 %collective-permute-start.15 = (bf16[128,2048]{1,0:T(8,128)(2,1)S(1)}, bf16[128,2048]{1,0:T(8,128)(2,1)S(1)}, u32[]{:S(2)}, u32[]{:S(2)}) collective-permute-start(bf16[128,2048]{1,0:T(8,128)(2,1)S(1)} %copy-done.25), channel_id=1, source_target_pairs={{0,8},{4,12},{8,0},{12,4},{16,24},{20,28},{24,16},{28,20},{1,9},{5... | collective-permute-start | bytes 1572872 | tf_op jit(solution)/shard_map/ppermute | solution.py:35
  175.2 15.3 %collective-permute-start.16 = (bf16[128,2048]{1,0:T(8,128)(2,1)S(1)}, bf16[128,2048]{1,0:T(8,128)(2,1)S(1)}, u32[]{:S(2)}, u32[]{:S(2)}) collective-permute-start(bf16[128,2048]{1,0:T(8,128)(2,1)S(1)} %copy-done.24), channel_id=1, source_target_pairs={{0,12},{4,8},{8,4},{12,0},{16,28},{20,24},{24,20},{28,16},{1,13},{... | collective-permute-start | bytes 1572872 | tf_op jit(solution)/shard_map/ppermute | solution.py:35
  175.2 6.0 %collective-permute-start.22 = (f32[136,256]{1,0:T(8,128)S(1)}, f32[136,256]{1,0:T(8,128)S(1)}, u32[]{:S(2)}, u32[]{:S(2)}) collective-permute-start(f32[136,256]{1,0:T(8,128)S(1)} %pad_maximum_fusion), channel_id=1, source_target_pairs={{0,3},{1,2},{2,1},{3,0},{4,7},{5,6},{6,5},{7,4},{8,11},{9,10},{10,... | collective-permute-start | bytes 417800 | tf_op jit(solution)/shard_map/ppermute | solution.py:35
  175.4 6.7 %copy-start.19 = (f32[128,64]{1,0:T(8,128)S(1)}, f32[128,64]{1,0:T(8,128)}, u32[]{:S(2)}) copy-start(f32[128,64]{1,0:T(8,128)} %get-tuple-element.90) | copy-start | bytes 98308
  175.4 8.8 %collective-permute-start.21 = (f32[136,256]{1,0:T(8,128)S(1)}, f32[136,256]{1,0:T(8,128)S(1)}, u32[]{:S(2)}, u32[]{:S(2)}) collective-permute-start(f32[136,256]{1,0:T(8,128)S(1)} %pad_maximum_fusion), channel_id=1, source_target_pairs={{0,2},{1,3},{2,0},{3,1},{4,6},{5,7},{6,4},{7,5},{8,10},{9,11},{10,... | collective-permute-start | bytes 417800 | tf_op jit(solution)/shard_map/ppermute | solution.py:35
  181.1 3.1 %collective-permute-start.20 = (f32[136,256]{1,0:T(8,128)S(1)}, f32[136,256]{1,0:T(8,128)S(1)}, u32[]{:S(2)}, u32[]{:S(2)}) collective-permute-start(f32[136,256]{1,0:T(8,128)S(1)} %pad_maximum_fusion), channel_id=1, source_target_pairs={{0,1},{1,0},{2,3},{3,2},{4,5},{5,4},{6,7},{7,6},{8,9},{9,8},{10,11... | collective-permute-start | bytes 417800 | tf_op jit(solution)/shard_map/ppermute | solution.py:35
  186.0 4.4 %copy-start.8 = (bf16[128,2048]{1,0:T(8,128)(2,1)}, bf16[128,2048]{1,0:T(8,128)(2,1)S(1)}, u32[]{:S(2)}) copy-start(bf16[128,2048]{1,0:T(8,128)(2,1)S(1)} %collective-permute-done.14.refs_6_) | copy-start | bytes 1572868
  186.0 4.4 %copy-start.9 = (bf16[128,2048]{1,0:T(8,128)(2,1)}, bf16[128,2048]{1,0:T(8,128)(2,1)S(1)}, u32[]{:S(2)}) copy-start(bf16[128,2048]{1,0:T(8,128)(2,1)S(1)} %collective-permute-done.15.refs_7_) | copy-start | bytes 1572868
  (7 other events, 5.0 us)

commit v3 on v2

--- a/solution.py
+++ b/solution.py
@@ -149,33 +149,36 @@
 
 
 def pack_kernel(n, heads, idx_ref, x_ref, z_ref, d_ref, raw_ref, step_ref, *outs):
-    width = heads * MP
+    half = heads * MP // 2
     me = idx_ref[0]
     lane = iota((x_ref.shape[0], 128), 1)
     for m in range(n):
         dest = me ^ m
-        lanes = pl.ds(pl.multiple_of(dest * width, 128), width)
-        z = z_ref[:, lanes].astype(F32)
-        grad = d_ref[:, lanes].astype(F32) * z * jax.nn.sigmoid(z)
-        outs[m][:, :width] = x_ref[:, lanes]
-        outs[m][:, width : 2 * width] = grad.astype(BF16)
-        outs[m][:, 2 * width : 2 * width + 256] = raw_ref[...]
+        for side in range(2):
+            out = outs[side * n + m]
+            lanes = pl.ds(pl.multiple_of((2 * dest + side) * half, 128), half)
+            z = z_ref[:, lanes].astype(F32)
+            grad = d_ref[:, lanes].astype(F32) * z * jax.nn.sigmoid(z)
+            out[:, :half] = x_ref[:, lanes]
+            out[:, half : 2 * half] = grad.astype(BF16)
+        outs[m][:, 2 * half : 2 * half + 256] = raw_ref[...]
         logit = pltpu.roll(step_ref[...], (128 - dest * heads) % 128, 1)
         high = logit.astype(BF16).astype(F32)
         middle = (logit - high).astype(BF16).astype(F32)
         rest = logit - high - middle
         parts = jnp.where(lane < heads, high, pltpu.roll(middle, heads, 1))
         parts = jnp.where(lane < 2 * heads, parts, pltpu.roll(rest, 2 * heads, 1))
-        outs[m][:, 2 * width + 256 :] = parts.astype(BF16)
+        outs[m][:, 2 * half + 256 :] = parts.astype(BF16)
 
 
 def pack_call(n, heads, idx, mixer_x, gate_z, d_mixer, raw, steps):
     rows = mixer_x.shape[0]
     return pl.pallas_call(
         lambda *refs: pack_kernel(n, heads, *refs),
-        out_shape=[jax.ShapeDtypeStruct((rows, 2 * heads * MP + 384), BF16)] * n,
+        out_shape=[jax.ShapeDtypeStruct((rows, heads * MP + 384), BF16)] * n
+        + [jax.ShapeDtypeStruct((rows, heads * MP), BF16)] * n,
         in_specs=[smem()] + [vmem()] * 5,
-        out_specs=[vmem()] * n,
+        out_specs=[vmem()] * (2 * n),
         compiler_params=params(),
         name="pack",
     )(idx, mixer_x, gate_z, d_mixer, raw, steps)
@@ -268,22 +271,21 @@
 
 
 def unpack_kernel(n, hp, idx_ref, z_ref, d_ref, margin_ref, share_ref, *refs):
-    big = refs[:n]
-    gx_ref, gz_ref, taps_ref, bias_ref, heads_ref = refs[n:]
+    gx_ref, gz_ref, taps_ref, bias_ref, heads_ref = refs[2 * n :]
     channels = z_ref.shape[1]
-    width = channels // n
+    width = channels // n // 2
     me = idx_ref[0]
     use = jnp.where(me == n - 1, 1.0, 0.0)
-    for m in range(n):
-        source = me ^ m
-        lanes = pl.ds(pl.multiple_of(source * width, 128), width)
-        gx_ref[: RB - 16, lanes] = big[m][: RB - 16, :width]
-        end = big[m][RB - 16 :, :width].astype(F32)
+    for m in range(2 * n):
+        piece = refs[m]
+        lanes = pl.ds(pl.multiple_of((2 * (me ^ (m % n)) + m // n) * width, 128), width)
+        gx_ref[: RB - 16, lanes] = piece[: RB - 16, :width]
+        end = piece[RB - 16 :, :width].astype(F32)
         end = jnp.concatenate([end[:8], end[8:] + use * margin_ref[:, lanes]], axis=0)
         gx_ref[RB - 16 :, lanes] = end.astype(BF16)
         z = z_ref[:, lanes].astype(F32)
         sig = jax.nn.sigmoid(z)
-        y = big[m][:, width:].astype(F32)
+        y = piece[:, width:].astype(F32)
         gz_ref[:, lanes] = (d_ref[:, lanes].astype(F32) * y * (sig * (1.0 + z * (1.0 - sig)))).astype(BF16)
     taps_ref[...] = share_ref[:KC, :channels]
     bias_ref[...] = share_ref[KC : KC + 1, :channels]
@@ -303,7 +305,7 @@
             jax.ShapeDtypeStruct((1, channels), F32),
             jax.ShapeDtypeStruct((3, n * hp), F32),
         ],
-        in_specs=[smem()] + [vmem()] * (4 + n),
+        in_specs=[smem()] + [vmem()] * (4 + 2 * n),
         out_specs=[vmem()] * 5,
         compiler_params=params(),
         name="unpack",
@@ -315,15 +317,17 @@
 
 
 class Shared:
-    def __init__(self, n, heads, hp, idx_ref, doc_ref, ins, scratch, full):
+    def __init__(self, n, heads, side, idx_ref, doc_ref, ins, scratch, full):
         self.n = n
         self.me = me = idx_ref[0]
         first = (idx_ref[1] - me) * RB
         xd_in = ins[:n]
         tails = ins[n : 2 * n]
-        self.wx_ref, self.bx_ref, wbc_ref, bbc_ref, par_ref = ins[2 * n :]
+        aux = ins[2 * n : 3 * n] if side else xd_in
+        self.wx_ref, self.bx_ref, wbc_ref, bbc_ref, par_ref = ins[-5:]
         self.par_ref = par_ref
-        width = heads * MP
+        self.side = side
+        self.width = width = heads * MP
         self.tail_ref, self.xd_ref, self.raw_ref, self.off_ref, self.xs_ref = scratch[:5]
         self.bb_ref, self.cc_ref, self.bt_ref, self.ct_ref, self.step_ref, self.cum_ref = scratch[5:11]
         if full:
@@ -335,14 +339,14 @@
         self.e_log = e_log = jnp.exp(par_ref[0])
         for m in range(n):
             source = me ^ m
-            self.tail_ref[m, :, : width // 2] = tails[m][RB : RB + 16, :]
-            self.tail_ref[m, :, width // 2 : width] = tails[m][RB + 16 : RB + 32, :]
+            self.tail_ref[m, :, :width] = tails[m][RB + 16 * side : RB + 16 * side + 16, :]
             self.tail_ref[m, :, width:] = tails[m][RB + 32 : RB + 48, :256]
             self.xd_ref[self.rows(source), :] = xd_in[m][:, : 2 * width]
-            raw = xd_in[m][:, 2 * width : 2 * width + 256]
+            raw = aux[m][:, 2 * width : 2 * width + 256]
             self.raw_ref[pl.ds(pl.multiple_of(source * RB + 8, 8), RB), :] = raw.astype(F32)
-            parts = xd_in[m][:, 2 * width + 256 :].astype(F32).T
-            logit = parts[:hp] + parts[hp : 2 * hp] + parts[2 * hp : 3 * hp]
+            parts = aux[m][:, 2 * width + 256 :].astype(F32).T
+            at = side * heads
+            logit = parts[at : at + heads] + parts[at + 2 * heads : at + 3 * heads] + parts[at + 4 * heads : at + 5 * heads]
             logit = logit + par_ref[1]
             step = jnp.maximum(logit, 0.0) + jnp.log1p(jnp.exp(-jnp.abs(logit)))
             self.step_ref[source] = step
@@ -357,8 +361,9 @@
             pos = first + c * RB + sub
             off = pos - doc_start(doc_ref, pos)
             self.off_ref[self.rows(c), :] = off
-            pre_b = self.conv(c, self.raw_ref, slice(0, 128), wbc[:, :128], bbc[:, :128])
-            pre_c = self.conv(c, self.raw_ref, slice(128, 256), wbc[:, 128:], bbc[:, 128:])
+            masks = [off >= j for j in range(KC)]
+            pre_b = self.conv(c, self.raw_ref, slice(0, 128), wbc[:, :128], bbc[:, :128], masks)
+            pre_c = self.conv(c, self.raw_ref, slice(128, 256), wbc[:, 128:], bbc[:, 128:], masks)
             b_in = pre_b * jax.nn.sigmoid(pre_b)
             c_out = pre_c * jax.nn.sigmoid(pre_c)
             self.bt_ref[c] = b_in.T.astype(BF16)
@@ -377,13 +382,16 @@
     def rows(self, c, extra=0):
         return pl.ds(pl.multiple_of(c * RB, RB), RB + extra)
 
-    def conv(self, c, src_ref, lanes, weight, bias):
-        off = self.off_ref[self.rows(c), :]
+    def conv(self, c, src_ref, lanes, weight, bias, masks):
         window = src_ref[self.rows(c, 8), lanes]
         pre = bias + weight[0:1] * window[8:]
         for j in range(1, KC):
-            pre = pre + weight[j : j + 1] * jnp.where(off >= j, window[8 - j : 8 + RB - j], 0.0)
+            pre = pre + weight[j : j + 1] * jnp.where(masks[j], window[8 - j : 8 + RB - j], 0.0)
         return pre
+
+    def masks(self, c):
+        off = self.off_ref[self.rows(c), :]
+        return off, [off >= j for j in range(KC)]
 
     def load(self, u, lanes):
         self.xs_ref[u, :8, :] = self.tail_ref[self.me, :, lanes].astype(F32)[8:]
@@ -402,11 +410,14 @@
         keep = jnp.where(last_off >= RB, jnp.exp(last), 0.0)
         return enter, leave, keep
 
+    def held(self, p):
+        return pl.ds(pl.multiple_of((2 * self.me + self.side) * self.width + p * 128, 128), 128)
+
     def pair_rows(self, ref, c, p):
         return ref[c, pl.ds(2 * p, 1), :], ref[c, pl.ds(2 * p + 1, 1), :]
 
 
-def shared_scratch(n, heads, hp, wide, full):
+def shared_scratch(n, heads, wide, full):
     width = heads * MP
     tokens = n * RB
     found = [
@@ -419,37 +430,37 @@
         pltpu.VMEM((tokens, 128), BF16),
         pltpu.VMEM((n, 128, RB), BF16),
         pltpu.VMEM((n, 128, RB), BF16),
-        pltpu.VMEM((n, hp, 128), F32),
-        pltpu.VMEM((n, hp, 128), F32),
+        pltpu.VMEM((n, heads, 128), F32),
+        pltpu.VMEM((n, heads, 128), F32),
     ]
     if full:
         found += [
             pltpu.VMEM((n, RB, RB), F32),
             pltpu.VMEM((n, RB, RB), F32),
-            pltpu.VMEM((n, hp, 128), F32),
+            pltpu.VMEM((n, heads, 128), F32),
         ]
     return found
 
 
-def totals_kernel(n, heads, hp, wide, idx_ref, doc_ref, *refs):
+def totals_kernel(n, heads, side, wide, idx_ref, doc_ref, *refs):
     pairs = heads * MP // 128
     width = heads * MP
-    ins = refs[: 2 * n + 5]
-    state_ref, grad_ref, keep_ref = refs[2 * n + 5 : 2 * n + 8]
-    sh = Shared(n, heads, hp, idx_ref, doc_ref, ins, refs[2 * n + 8 :], False)
+    at = (2 + side) * n + 5
+    ins = refs[:at]
+    state_ref, grad_ref, keep_ref = refs[at : at + 3]
+    sh = Shared(n, heads, side, idx_ref, doc_ref, ins, refs[at + 3 :], False)
 
     def streams(block, carry):
         ids = [block * wide + u for u in range(wide)]
-        held = [pl.ds(pl.multiple_of(sh.me * width + p * 128, 128), 128) for p in ids]
+        held = [sh.held(p) for p in ids]
         weight = [sh.wx_ref[:, h] for h in held]
         bias = [sh.bx_ref[:, h] for h in held]
         for u in range(wide):
             sh.load(u, pl.ds(pl.multiple_of(ids[u] * 128, 128), 128))
 
-        def one(u, c, state, grads, kept):
+        def one(u, c, off, masks, state, grads, kept):
             p = ids[u]
-            off = sh.off_ref[sh.rows(c), :]
-            pre = sh.conv(c, sh.xs_ref.at[u], slice(None), weight[u], bias[u])
+            pre = sh.conv(c, sh.xs_ref.at[u], slice(None), weight[u], bias[u], masks)
             x = pre * jax.nn.sigmoid(pre)
             row0, row1 = sh.pair_rows(sh.cum_ref, c, p)
             step0, step1 = sh.pair_rows(sh.step_ref, c, p)
@@ -462,7 +473,8 @@
             return state, grads, kept * keep
 
         def chunk(c, held):
-            return tuple(one(u, c, *held[u]) for u in range(wide))
+            off, masks = sh.masks(c)
+            return tuple(one(u, c, off, masks, *held[u]) for u in range(wide))
 
         zero = jnp.zeros((128, 128), F32)
         found = lax.fori_loop(0, n, chunk, tuple((zero, zero, jnp.ones((1, 128), F32)) for _ in range(wide)))
@@ -475,11 +487,11 @@
     lax.fori_loop(0, pairs // wide, streams, 0)
 
 
-def totals_call(n, heads, hp, idx, doc, ins):
+def totals_call(n, heads, side, idx, doc, ins):
     pairs = heads * MP // 128
     wide = 2 - pairs % 2
     return pl.pallas_call(
-        lambda *refs: totals_kernel(n, heads, hp, wide, *refs),
+        lambda *refs: totals_kernel(n, heads, side, wide, *refs),
         out_shape=[
             jax.ShapeDtypeStruct((pairs, 128, 128), BF16),
             jax.ShapeDtypeStruct((pairs, 128, 128), BF16),
@@ -487,29 +499,36 @@
         ],
         in_specs=[smem(), smem()] + [vmem()] * len(ins),
         out_specs=[vmem()] * 3,
-        scratch_shapes=shared_scratch(n, heads, hp, wide, False),
+        scratch_shapes=shared_scratch(n, heads, wide, False),
         compiler_params=params(),
-        name="totals",
     )(idx, doc, *ins)
 
 
-def mixer_kernel(n, heads, hp, wide, idx_ref, doc_ref, *refs):
+def mixer_kernel(n, heads, side, wide, idx_ref, doc_ref, *refs):
     width = heads * MP
     pairs = width // 128
-    ins = refs[: 2 * n + 5]
-    first_ref, later_ref = refs[2 * n + 5 : 2 * n + 7]
-    at = 2 * n + 7
+    all_rows = 2 * heads
+    at = (2 + side) * n + 5
+    ins = refs[:at]
+    first_ref, later_ref = refs[at : at + 2]
+    at = at + 2
+    if side:
+        sums_in = refs[at : at + 3]
+        logit_in, part_in = refs[at + 3 : at + 5]
+        at = at + 5
     big_out = refs[at : at + n]
-    bc_out = refs[at + n : at + 2 * n]
-    edge_out = refs[at + 2 * n : at + 3 * n]
-    at = at + 3 * n
+    at = at + n
+    if side:
+        bc_out = refs[at : at + n]
+        edge_out = refs[at + n : at + 2 * n]
+        dcb_ref, db_ref, dc_ref, og_ref = refs[at + 2 * n : at + 2 * n + 4]
+        at = at + 2 * n + 4
+    else:
+        dcb_ref, db_ref, dc_ref, logit_out, part_out = refs[at : at + 5]
+        at = at + 5
     (
         od_ref,
-        og_ref,
         gp_ref,
-        dcb_ref,
-        db_ref,
-        dc_ref,
         z1_ref,
         z2_ref,
         sin_ref,
@@ -523,35 +542,34 @@
         k_ref,
         acc_ref,
         skip_ref,
-    ) = refs[at : at + 19]
-    sh = Shared(n, heads, hp, idx_ref, doc_ref, ins, refs[at + 19 :], True)
+    ) = refs[at : at + 15]
+    sh = Shared(n, heads, side, idx_ref, doc_ref, ins, refs[at + 15 :], True)
+    hp = heads
     me, lane, sub, low = sh.me, sh.lane, sh.sub, sh.low
-    par_ref, wx_ref, bx_ref, xd_ref, off_ref = sh.par_ref, sh.wx_ref, sh.bx_ref, sh.xd_ref, sh.off_ref
+    par_ref, wx_ref, bx_ref, xd_ref = sh.par_ref, sh.wx_ref, sh.bx_ref, sh.xd_ref
     raw_ref, xs_ref, cum_ref, step_ref = sh.raw_ref, sh.xs_ref, sh.cum_ref, sh.step_ref
     bb_ref, cc_ref, bt_ref, ct_ref = sh.bb_ref, sh.cc_ref, sh.bt_ref, sh.ct_ref
     cb_ref, bias_ref, sg_ref = sh.cb_ref, sh.bias_ref, sh.sg_ref
     wbc, bbc, e_log, conv, rows_of = sh.wbc, sh.bbc, sh.e_log, sh.conv, sh.rows
     tokens = n * RB
-    sums_at = hp + 8 * pairs + 16
+    sums_at = all_rows + 16 * pairs + 16
     zero8 = jnp.zeros((8, 128), F32)
     for c in range(n):
         z1_ref[c] = jnp.zeros((hp, 128), F32)
         z2_ref[c] = jnp.zeros((hp, 128), F32)
-        dcb_ref[c] = jnp.zeros((RB, RB), F32)
-        db_ref[c] = jnp.zeros((RB, 128), F32)
-        dc_ref[c] = jnp.zeros((RB, 128), F32)
+        for held_ref, k in ((dcb_ref, 0), (db_ref, 1), (dc_ref, 2)):
+            held_ref[c] = sums_in[k][c] if side else jnp.zeros((RB, RB), F32)
     skip_ref[...] = jnp.zeros((hp, 128), F32)
     for u in range(wide):
         for j in range(KC - 1):
             gp_ref[u, j, tokens:, :] = zero8
 
-    def conv_back(c, grad, src_ref, lanes, weight, u):
-        off = off_ref[rows_of(c), :]
+    def conv_back(c, grad, src_ref, lanes, weight, u, masks):
         window = src_ref[rows_of(c, 8), lanes]
         back = weight[0:1] * grad
         sums = [by_sublane(grad * window[8:])]
         for j in range(1, KC):
-            held_back = jnp.where(off >= j, grad, 0.0)
+            held_back = jnp.where(masks[j], grad, 0.0)
             sums.append(by_sublane(held_back * window[8 - j : 8 + RB - j]))
             gp_ref[u, j - 1, rows_of(c), :] = held_back
             back = back + weight[j : j + 1] * gp_ref[u, j - 1, rows_of(c, 8), :][j : j + RB]
@@ -574,7 +592,7 @@
         each = range(wide)
         lanes = [pl.ds(pl.multiple_of(p * 128, 128), 128) for p in ids]
         lanes_d = [pl.ds(pl.multiple_of(width + p * 128, 128), 128) for p in ids]
-        held = [pl.ds(pl.multiple_of(me * width + p * 128, 128), 128) for p in ids]
+        held = [sh.held(p) for p in ids]
         weight = [wx_ref[:, h] for h in held]
         bias = [bx_ref[:, h] for h in held]
         skip = [
@@ -587,11 +605,10 @@
         for u in each:
             sh.load(u, lanes[u])
 
-        def forward_one(u, c, state):
+        def forward_one(u, c, off, masks, state):
             p = ids[u]
             rows = rows_of(c)
-            off = off_ref[rows, :]
-            pre = conv(c, xs_ref.at[u], slice(None), weight[u], bias[u])
+            pre = conv(c, xs_ref.at[u], slice(None), weight[u], bias[u], masks)
             x, slope = silu_parts(pre)
             xc_ref[u, rows, :] = x
             ds_ref[u, rows, :] = slope
@@ -637,7 +654,8 @@
             return new_state, added, dot(entered, state_low, NT)
 
         def forward(c, states):
-            found = [forward_one(u, c, states[u]) for u in each]
+            off, masks = sh.masks(c)
+            found = [forward_one(u, c, off, masks, states[u]) for u in each]
             dcb_ref[c] += sum(f[1] for f in found)
             dc_ref[c] += sum(f[2] for f in found)
             return tuple(f[0] for f in found)
@@ -648,7 +666,7 @@
             for j in range(KC + 2):
                 acc_ref[u, j] = zero8
 
-        def backward_one(u, c, later):
+        def backward_one(u, c, masks, later):
             rows = rows_of(c)
             later_low = later.astype(BF16)
             leave = lv_ref[u, rows, :]
@@ -666,7 +684,7 @@
             steps = dot(pick[u], (x * grad_value).astype(BF16), NT)
             grad_b = dot((leave * value).astype(BF16), later_low, NT)
             grad_x = (step * grad_value + skip[u] * grad) * ds_ref[u, rows, :]
-            back, sums = conv_back(c, grad_x, xs_ref.at[u], slice(None), weight[u], u)
+            back, sums = conv_back(c, grad_x, xs_ref.at[u], slice(None), weight[u], u, masks)
             od_ref[rows, lanes[u]] = back.astype(BF16)
             sums.append(by_sublane(grad * x))
             for j in range(KC + 2):
@@ -676,7 +694,8 @@
 
         def backward(k, laters):
             c = n - 1 - k
-            found = [backward_one(u, c, laters[u]) for u in each]
+            _, masks = sh.masks(c)
+            found = [backward_one(u, c, masks, laters[u]) for u in each]
             z1_ref[c] += sum(f[1] for f in found)
             z2_ref[c] += sum(f[2] for f in found)
             db_ref[c] += sum(f[3] for f in found)
@@ -687,14 +706,20 @@
             found = [jnp.sum(acc_ref[u, j], axis=0, keepdims=True) for j in range(KC + 2)]
             skip_ref[...] += pick[u].astype(F32) * found[KC + 1]
             found = found[: KC + 1] + [jnp.zeros((8 - KC - 1, 128), F32)]
-            edge_out[0][pl.ds(pl.multiple_of(sums_at + 8 * ids[u], 8), 8), :] = jnp.concatenate(found, axis=0)
-            edge_out[0][pl.ds(pl.multiple_of(hp + 8 * ids[u], 8), 8), :] = margin_of(weight[u], u)
+            if side:
+                taps_to, taps_at = edge_out[0], sums_at + 8 * (pairs + ids[u])
+                margin_to, margin_at = edge_out[0], all_rows + 8 * (pairs + ids[u])
+            else:
+                taps_to, taps_at = part_out, 8 * (pairs + ids[u])
+                margin_to, margin_at = part_out, 8 * ids[u]
+            taps_to[pl.ds(pl.multiple_of(taps_at, 8), 8), :] = jnp.concatenate(found, axis=0)
+            margin_to[pl.ds(pl.multiple_of(margin_at, 8), 8), :] = margin_of(weight[u], u)
         return carry
 
     lax.fori_loop(0, pairs // wide, streams, 0)
 
-    for side in range(2):
-        lanes = slice(128 * side, 128 * side + 128)
+    for part in range(2 if side else 0):
+        lanes = slice(128 * part, 128 * part + 128)
         weight = wbc[:, lanes]
         bias = bbc[:, lanes]
         for j in range(KC + 1):
@@ -704,12 +729,13 @@
             c = n - 1 - k
             rows = rows_of(c)
             mixed = dcb_ref[c].astype(BF16)
-            if side == 0:
+            if part == 0:
                 grad = db_ref[c] + dot(mixed, cc_ref[rows, :], TN)
             else:
                 grad = dc_ref[c] + dot(mixed, bb_ref[rows, :], NN)
-            pre = conv(c, raw_ref, lanes, weight, bias)
-            back, sums = conv_back(c, grad * silu_parts(pre)[1], raw_ref, lanes, weight, 0)
+            _, masks = sh.masks(c)
+            pre = conv(c, raw_ref, lanes, weight, bias, masks)
+            back, sums = conv_back(c, grad * silu_parts(pre)[1], raw_ref, lanes, weight, 0, masks)
             og_ref[rows, lanes] = back.astype(BF16)
             for j in range(KC + 1):
                 acc_ref[0, j] += sums[j]
@@ -718,9 +744,9 @@
         lax.fori_loop(0, n, finish, 0)
         found = [jnp.sum(acc_ref[0, j], axis=0, keepdims=True) for j in range(KC + 1)]
         found.append(jnp.zeros((8 - KC - 1, 128), F32))
-        at_row = 8 * pairs + 8 * side
+        at_row = 16 * pairs + 8 * part
         edge_out[0][sums_at + at_row : sums_at + at_row + 8, :] = jnp.concatenate(found, axis=0)
-        edge_out[0][hp + at_row : hp + at_row + 8, :] = margin_of(weight, 0)
+        edge_out[0][all_rows + at_row : all_rows + at_row + 8, :] = margin_of(weight, 0)
 
     later_sum = (sub >= lane).astype(F32)
     sum_log = jnp.zeros((hp, 128), F32)
@@ -732,39 +758,54 @@
         logit_grad = step_grad * sg_ref[c]
         sum_log = sum_log - step_ref[c] * e_log * rate_grad
         sum_step = sum_step + logit_grad
-        edge_out[m][:hp, :] = logit_grad
+        if side:
+            edge_out[m][:hp, :] = logit_in[c]
+            edge_out[m][hp:all_rows, :] = logit_grad
+            bc_out[m][...] = og_ref[rows_of(c), :]
+        else:
+            logit_out[c] = logit_grad
         big_out[m][...] = od_ref[rows_of(c), :]
-        bc_out[m][...] = og_ref[rows_of(c), :]
-    at_row = sums_at + 8 * pairs + 16
-    edge_out[0][at_row : at_row + hp, :] = sum_log
-    edge_out[0][at_row + hp : at_row + 2 * hp, :] = sum_step
-    edge_out[0][at_row + 2 * hp : at_row + 3 * hp, :] = skip_ref[...]
-    for m in range(1, n):
-        edge_out[m][hp:, :] = edge_out[0][hp:, :]
-
-
-def mixer_call(n, heads, hp, idx, doc, ins, first, later):
+    if side:
+        edge_out[0][all_rows : all_rows + 8 * pairs, :] = part_in[: 8 * pairs, :]
+        edge_out[0][sums_at : sums_at + 8 * pairs, :] = part_in[8 * pairs : 16 * pairs, :]
+    for k, value in enumerate((sum_log, sum_step, skip_ref[...])):
+        if side:
+            at_row = sums_at + 16 * pairs + 16 + k * all_rows
+            edge_out[0][at_row : at_row + hp, :] = part_in[16 * pairs + k * hp : 16 * pairs + (k + 1) * hp, :]
+            edge_out[0][at_row + hp : at_row + all_rows, :] = value
+        else:
+            part_out[16 * pairs + k * hp : 16 * pairs + (k + 1) * hp, :] = value
+    for m in range(1, n if side else 0):
+        edge_out[m][all_rows:, :] = edge_out[0][all_rows:, :]
+
+
+def mixer_call(n, heads, side, idx, doc, ins, first, later, earlier):
     width = heads * MP
     pairs = width // 128
     wide = 2 - pairs % 2
     tokens = n * RB
-    square = pltpu.VMEM((n, RB, RB), F32)
+    square = jax.ShapeDtypeStruct((n, RB, RB), F32)
     flat = pltpu.VMEM((wide, tokens, 128), F32)
-    per_head = pltpu.VMEM((n, hp, 128), F32)
+    per_head = pltpu.VMEM((n, heads, 128), F32)
+    outs = [jax.ShapeDtypeStruct((RB, 2 * width), BF16)] * n
+    if side:
+        outs += [jax.ShapeDtypeStruct((RB, 256), BF16)] * n
+        outs += [jax.ShapeDtypeStruct((8 * heads + 32 * pairs + 32, 128), F32)] * n
+        sums = [pltpu.VMEM((n, RB, RB), F32)] * 3 + [pltpu.VMEM((tokens, 256), BF16)]
+    else:
+        outs += [square] * 3
+        outs += [jax.ShapeDtypeStruct((n, heads, 128), F32)]
+        outs += [jax.ShapeDtypeStruct((16 * pairs + 3 * heads, 128), F32)]
+        sums = []
     return pl.pallas_call(
-        lambda *refs: mixer_kernel(n, heads, hp, wide, *refs),
-        out_shape=[jax.ShapeDtypeStruct((RB, 2 * width), BF16)] * n
-        + [jax.ShapeDtypeStruct((RB, 256), BF16)] * n
-        + [jax.ShapeDtypeStruct((4 * hp + 16 * pairs + 32, 128), F32)] * n,
-        in_specs=[smem(), smem()] + [vmem()] * (len(ins) + 2),
-        out_specs=[vmem()] * (3 * n),
-        scratch_shapes=[
+        lambda *refs: mixer_kernel(n, heads, side, wide, *refs),
+        out_shape=outs,
+        in_specs=[smem(), smem()] + [vmem()] * (len(ins) + 2 + len(earlier)),
+        out_specs=[vmem()] * len(outs),
+        scratch_shapes=sums
+        + [
             pltpu.VMEM((tokens, 2 * width), BF16),
-            pltpu.VMEM((tokens, 256), BF16),
             pltpu.VMEM((wide, KC - 1, tokens + 8, 128), F32),
-            square,
-            square,
-            square,
             per_head,
             per_head,
             pltpu.VMEM((wide, n + 1, 128, 128), F32),
@@ -777,12 +818,11 @@
             pltpu.VMEM((wide, tokens, 128), BF16),
             pltpu.VMEM((wide, n, 8, 128), F32),
             pltpu.VMEM((wide, KC + 2, 8, 128), F32),
-            pltpu.VMEM((hp, 128), F32),
+            pltpu.VMEM((heads, 128), F32),
         ]
-        + shared_scratch(n, heads, hp, wide, True),
+        + shared_scratch(n, heads, wide, True),
         compiler_params=params(),
-        name="mixer",
-    )(idx, doc, *ins, first, later)
+    )(idx, doc, *ins, first, later, *earlier)
 
 
 def program(
@@ -825,30 +865,38 @@
 
     logits = jnp.pad(dt_raw, ((0, 0), (0, 128 - all_heads)))
     packed = pack_call(group, heads, idx, mixer_x, gate_z, d_mixer, mixer_bc, logits)
-    big = [packed[0]] + [crossed(packed[m], "ctx", m) for m in range(1, group)]
-
+    big = []
+    for side in range(2):
+        piece = packed[side * group : (side + 1) * group]
+        big.append([piece[0]] + [crossed(piece[m], "ctx", m) for m in range(1, group)])
+
+    half = heads // 2
     head_params = jnp.stack([a_log, dt_bias, skip_d])
     head_params = lax.dynamic_slice_in_dim(head_params, inside * heads, heads, 1)
-    head_params = jnp.broadcast_to(head_params[:, :, None], (3, hp, 128))
-    ins = (
-        big
-        + tails
-        + [conv_weight_x, conv_bias_x[None], conv_weight_bc, conv_bias_bc[None], head_params]
-    )
-    state, grad_state, keep = totals_call(group, heads, hp, idx, doc_lengths, ins)
-    back_state, back_keep = grad_state, keep
-    covered = 1
-    while covered < n // group // 2:
-        step_by = covered * group
-        state = (state.astype(F32) + keep[:, :1] * shifted(state, "ctx", step_by).astype(F32)).astype(BF16)
-        back_state = (
-            back_state.astype(F32) + back_keep[:, :1] * shifted(back_state, "ctx", -step_by).astype(F32)
-        ).astype(BF16)
-        keep = keep * shifted(keep, "ctx", step_by)
-        back_keep = back_keep * shifted(back_keep, "ctx", -step_by)
-        covered = 2 * covered
-    first = shifted(state, "ctx", group)
-    later = shifted(back_state, "ctx", -group)
+    head_params = jnp.broadcast_to(head_params[:, :, None], (3, heads, 128))
+    ins = []
+    entering = []
+    for side in range(2):
+        ins.append(
+            big[side]
+            + tails
+            + (big[0] if side else [])
+            + [conv_weight_x, conv_bias_x[None], conv_weight_bc, conv_bias_bc[None]]
+            + [head_params[:, side * half : (side + 1) * half]]
+        )
+        state, back_state, keep = totals_call(group, half, side, idx, doc_lengths, ins[side])
+        back_keep = keep
+        covered = 1
+        while covered < n // group // 2:
+            step_by = covered * group
+            state = (state.astype(F32) + keep[:, :1] * shifted(state, "ctx", step_by).astype(F32)).astype(BF16)
+            back_state = (
+                back_state.astype(F32) + back_keep[:, :1] * shifted(back_state, "ctx", -step_by).astype(F32)
+            ).astype(BF16)
+            keep = keep * shifted(keep, "ctx", step_by)
+            back_keep = back_keep * shifted(back_keep, "ctx", -step_by)
+            covered = 2 * covered
+        entering.append((shifted(state, "ctx", group), shifted(back_state, "ctx", -group)))
 
     attended = attention_call(idx, doc_lengths, att_queries, d_attn, blocks)
     grad_queries = attended[0]
@@ -860,10 +908,12 @@
     grad_keys = grad_kv[:, :kv_width].astype(BF16)
     grad_values = grad_kv[:, kv_width:].astype(BF16)
 
-    results = mixer_call(group, heads, hp, idx, doc_lengths, ins, first, later)
+    first = mixer_call(group, half, 0, idx, doc_lengths, ins[0], *entering[0], [])
+    big = [first[0]] + [crossed(first[m], "ctx", m) for m in range(1, group)]
+    results = mixer_call(group, half, 1, idx, doc_lengths, ins[1], *entering[1], first[group:])
     edges = [results[2 * group]] + [crossed(results[2 * group + m], "ctx", m) for m in range(1, group)]
     bc_parts = [results[group]] + [crossed(results[group + m], "ctx", m) for m in range(1, group)]
-    big = [results[0]] + [crossed(results[m], "ctx", m) for m in range(1, group)]
+    big = big + [results[0]] + [crossed(results[m], "ctx", m) for m in range(1, group)]
 
     grad_logits, margin, share = edges_call(group, hp, pairs, idx, edges)
     margin = shifted(margin, "ctx", -1)

time: 198 us -> 185 us (0.934)
  waiting for transfers between devices: 50.6 us -> 26.9 us
  Pallas kernels: 64.9 us -> 73 us
    ppermute x11 -> x13, waiting for transfers between devices: 37.2 us -> 0.03 us  [shifted(): lax.ppermute(value, axis, [(source, source + steps) for source in range(i...]
    ppermute x16 -> x22, waiting for transfers between devices: 13.5 us -> 26.8 us  [crossed(): lax.ppermute(value, axis, [(source, source ^ mask) for source in range(co...]
    pallas_call x2 -> x4, Pallas kernels: 36.8 us -> 45 us  [the longest x2 31.2 us: mixer_call(): pl.pallas_call(lambda *refs: mixer_kernel(n, heads, side, wide, *refs), o...]
    ppermute x16 -> x22, starting transfers between devices: 39.4 us -> 43.9 us  [crossed(): lax.ppermute(value, axis, [(source, source ^ mask) for source in range(co...]
    ppermute x11 -> x13, starting transfers between devices: 30.3 us -> 27.1 us  [shifted(): lax.ppermute(value, axis, [(source, source + steps) for source in range(i...]
    unnamed x58 -> x92, local copies, waits for them, and re-layouts: 4.86 us -> 5.75 us
  transfers between devices with their start and end apart: 27 -> 35, of which waited for: 9 -> 6; matrix products, arithmetic and copies ran while one was open for 2% -> 3% of each run, Pallas kernels for 10% -> 35%
where the time goes in v3:
time: 185 us
  Pallas kernels  73 us (39%)
  starting transfers between devices  71 us (38%)
  waiting for transfers between devices  26.9 us (15%)
  local copies, waits for them, and re-layouts  11.8 us (6%)
    ppermute x22, starting transfers between devices, crossed(): lax.ppermute(value, axis, [(source, source ^ mask) for source in range(co...  43.9 us
    pallas_call x2, Pallas kernels, mixer_call(): pl.pallas_call(lambda *refs: mixer_kernel(n, heads, side, wide, *refs), o...  31.2 us
    ppermute x13, starting transfers between devices, shifted(): lax.ppermute(value, axis, [(source, source + steps) for source in range(i...  27.1 us
    ppermute x22, waiting for transfers between devices, crossed(): lax.ppermute(value, axis, [(source, source ^ mask) for source in range(co...  26.8 us
    pallas_call x1, Pallas kernels, attention_call(): pl.pallas_call(lambda *refs: attention_kernel(nb - 1, *refs), out_shape=o...  15.5 us
    pallas_call x2, Pallas kernels, totals_call(): pl.pallas_call(lambda *refs: totals_kernel(n, heads, side, wide, *refs),...  13.8 us
    unnamed x92, local copies, waits for them, and re-layouts  5.75 us
    pallas_call x1, Pallas kernels, unpack_call(): pl.pallas_call(lambda *refs: unpack_kernel(n, hp, *refs), out_shape=[jax....  4.66 us
  transfers between devices with their start and end apart: 35, of which 6 were waited for; matrix products, arithmetic and copies ran while one was open for 3% of the time, Pallas kernels for 35%

profile of v3, /device:TPU:0, one launch (start us, length us, event | category | flops | bytes accessed | tf_op | source)
XLA Modules:
  0.0 184.8 jit_solution(16086735781149887832)
XLA Ops:
  0.6 2.0 %keys.1 = (bf16[128,512]{1,0:T(8,128)(2,1)}, bf16[176,512]{1,0:T(8,128)(2,1)}, bf16[176,512]{1,0:T(8,128)(2,1)}, bf16[176,512]{1,0:T(8,128)(2,1)}, bf16[176,512]{1,0:T(8,128)(2,1)}) custom-call(bf16[128,256]{1,0:T(8,128)(2,1)} %refs_0_.1, bf16[128,256]{1,0:T(8,128)(2,1)} %refs_1_.9, bf16[128,4096]{1,0:T(8,128)(2,1)} %refs_2_.5, bf16[128,256]{1,0:T(8,128)(2,1)} %refs_3_.4), custom_call_target="tpu_custom_call" | custom-call | tf_op jit(solution)/shard_map/keys/pallas_call | solution.py:206
  2.6 5.0 %collective-permute-start.3 = (bf16[176,512]{1,0:T(8,128)(2,1)}, bf16[176,512]{1,0:T(8,128)(2,1)S(1)}, u32[]{:S(2)}, u32[]{:S(2)}) collective-permute-start(bf16[176,512]{1,0:T(8,128)(2,1)} %get-tuple-element.70), channel_id=1, source_target_pairs={{0,4},{4,8},{8,12},{12,16},{16,20},{20,24},{24,28},{1,5},{5,9},{9,... | collective-permute-start | bytes 540680 | tf_op jit(solution)/shard_map/ppermute | solution.py:30
  7.6 3.5 %collective-permute-start.4 = (bf16[176,512]{1,0:T(8,128)(2,1)}, bf16[176,512]{1,0:T(8,128)(2,1)S(1)}, u32[]{:S(2)}, u32[]{:S(2)}) collective-permute-start(bf16[176,512]{1,0:T(8,128)(2,1)} %get-tuple-element.71), channel_id=1, source_target_pairs={{0,8},{4,12},{8,16},{12,20},{16,24},{20,28},{1,9},{5,13},{9,17},{1... | collective-permute-start | bytes 540680 | tf_op jit(solution)/shard_map/ppermute | solution.py:30
  11.1 4.5 %collective-permute-start.5 = (bf16[176,512]{1,0:T(8,128)(2,1)}, bf16[176,512]{1,0:T(8,128)(2,1)S(1)}, u32[]{:S(2)}, u32[]{:S(2)}) collective-permute-start(bf16[176,512]{1,0:T(8,128)(2,1)} %get-tuple-element.72), channel_id=1, source_target_pairs={{0,12},{4,16},{8,20},{12,24},{16,28},{1,13},{5,17},{9,21},{13,25},... | collective-permute-start | bytes 540680 | tf_op jit(solution)/shard_map/ppermute | solution.py:30
  16.9 3.7 %pack.1 = (bf16[128,1408]{1,0:T(8,128)(2,1)}, bf16[128,1408]{1,0:T(8,128)(2,1)}, bf16[128,1408]{1,0:T(8,128)(2,1)}, bf16[128,1408]{1,0:T(8,128)(2,1)}, bf16[128,...) custom-call(s32[2]{0:T(128)} %pad_add_fusion.refs_0_, ...), custom_call_target="tpu_custom_call" | custom-call | tf_op jit(solution)/shard_map/pack/pallas_call | solution.py:176
  20.6 1.5 collective-permute-start
  22.1 1.3 collective-permute-start.6
  23.5 1.2 collective-permute-start.7
  24.7 5.3 %collective-permute-start.9 = (bf16[128,1408]{1,0:T(8,128)(2,1)}, bf16[128,1408]{1,0:T(8,128)(2,1)S(1)}, u32[]{:S(2)}, u32[]{:S(2)}) collective-permute-start(bf16[128,1408]{1,0:T(8,128)(2,1)} %get-tuple-element.77), channel_id=1, source_target_pairs={{0,12},{4,8},{8,4},{12,0},{16,28},{20,24},{24,20},{28,16},{1,13},{... | collective-permute-start | bytes 1081352 | tf_op jit(solution)/shard_map/ppermute | solution.py:35
  30.9 2.8 %collective-permute-start.2 = (bf16[128,1024]{1,0:T(8,128)(2,1)}, bf16[128,1024]{1,0:T(8,128)(2,1)S(1)}, u32[]{:S(2)}, u32[]{:S(2)}) collective-permute-start(bf16[128,1024]{1,0:T(8,128)(2,1)} %get-tuple-element.69), channel_id=1, source_target_pairs={{0,12},{4,8},{8,4},{12,0},{16,28},{20,24},{24,20},{28,16},{1,13},{... | collective-permute-start | bytes 786440 | tf_op jit(solution)/shard_map/ppermute | solution.py:35
  33.8 15.8 %collective-permute-done.1.refs_4_ = bf16[128,1024]{1,0:T(8,128)(2,1)S(1)} collective-permute-done((bf16[128,1024]{1,0:T(8,128)(2,1)}, bf16[128,1024]{1,0:T(8,128)(2,1)S(1)}, u32[]{:S(2)}, u32[]{:S(2)}) %collective-permute-start.1) | collective-permute-done | bytes 262176 | tf_op jit(solution)/shard_map/ppermute | solution.py:35
  49.6 3.6 %collective-permute-done.2.refs_5_ = bf16[128,1024]{1,0:T(8,128)(2,1)S(1)} collective-permute-done((bf16[128,1024]{1,0:T(8,128)(2,1)}, bf16[128,1024]{1,0:T(8,128)(2,1)S(1)}, u32[]{:S(2)}, u32[]{:S(2)}) %collective-permute-start.2) | collective-permute-done | bytes 262176 | tf_op jit(solution)/shard_map/ppermute | solution.py:35
  53.3 0.8 broadcast_in_dim.22.refs_18_
  54.3 7.1 %shard_map.272 = (bf16[4,128,128]{2,1,0:T(8,128)(2,1)}, bf16[4,128,128]{2,1,0:T(8,128)(2,1)}, f32[4,8,128]{2,1,0:T(8,128)}) custom-call(s32[2]{0:T(128)} %pad_add_fusion.refs_0_, s32[8]{0:T(128)} %refs_1_.15, bf16[128,1024]{1,0:T(8,128)(2,1)} %get-tuple-element.66.refs_2_, bf16[128,1024]{1,0:T(8,128)(2,1)} %copy-done.7, bf16[128,1024]{1,0:T(8,128)(2,1)} %copy-done.8, ...), custom_call_target="tpu_custom_call" | custom-call | tf_op jit(solution)/shard_map/pallas_call | solution.py:493
  61.3 2.4 %collective-permute-start.10 = (bf16[4,128,128]{2,1,0:T(8,128)(2,1)}, bf16[4,128,128]{2,1,0:T(8,128)(2,1)S(1)}, u32[]{:S(2)}, u32[]{:S(2)}) collective-permute-start(bf16[4,128,128]{2,1,0:T(8,128)(2,1)} %get-tuple-element.78), channel_id=1, source_target_pairs={{0,16},{4,20},{8,24},{12,28},{1,17},{5,21},{9,25},{13,29},{2,18},{... | collective-permute-start | bytes 393224 | tf_op jit(solution)/shard_map/ppermute | solution.py:30
  64.4 6.7 %shard_map.273 = (bf16[4,128,128]{2,1,0:T(8,128)(2,1)}, bf16[4,128,128]{2,1,0:T(8,128)(2,1)}, f32[4,8,128]{2,1,0:T(8,128)}) custom-call(s32[2]{0:T(128)} %pad_add_fusion.refs_0_, s32[8]{0:T(128)} %refs_1_.15, bf16[128,1408]{1,0:T(8,128)(2,1)} %get-tuple-element.74.refs_10_.refs_2_, bf16[128,1408]{1,0:T(8,128)(2,1)} %copy-done, bf16[128,1408]{1,0:T(8,128)(2,1)} %copy-done.1, ...), custom_call_target="tpu_custom_call" | custom-call | tf_op jit(solution)/shard_map/pallas_call | solution.py:493
  71.2 1.3 collective-permute-start.12
  72.5 1.3 collective-permute-start.13
  73.8 1.3 collective-permute-start.11
  75.1 15.5 %attention.1 = (bf16[128,2048]{1,0:T(8,128)(2,1)}, bf16[128,512]{1,0:T(8,128)(2,1)}, bf16[128,512]{1,0:T(8,128)(2,1)}, bf16[128,512]{1,0:T(8,128)(2,1)}, bf16[128,512]{1,0:T(8,128)(2,1)}, /*index=5*/f32[128,512]{1,0:T(8,128)}) custom-call(s32[2]{0:T(128)} %pad_add_fusion.refs_0_, s32[8]{0:T(128)} %refs_1_.15, bf16[128,2048]{1,0:T(8,128)(2,1)} %refs_2_.7, ...), custom_call_target="tpu_custom_call" | custom-call | tf_op jit(solution)/shard_map/attention/pallas_call | solution.py:131
  90.5 1.3 collective-permute-start.34
  91.8 1.3 collective-permute-start.33
  93.2 1.3 collective-permute-start.32
  94.5 1.5 collective-permute-start.31
  96.0 14.4 %shard_map.274 = (bf16[128,1024]{1,0:T(8,128)(2,1)}, bf16[128,1024]{1,0:T(8,128)(2,1)}, bf16[128,1024]{1,0:T(8,128)(2,1)}, bf16[128,1024]{1,0:T(8,128)(2,1)}, f3...) custom-call(s32[2]{0:T(128)} %pad_add_fusion.refs_0_, ...), custom_call_target="tpu_custom_call" | custom-call | tf_op jit(solution)/shard_map/pallas_call | solution.py:800
  111.1 16.8 %shard_map.275 = (bf16[128,1024]{1,0:T(8,128)(2,1)}, bf16[128,1024]{1,0:T(8,128)(2,1)}, bf16[128,1024]{1,0:T(8,128)(2,1)}, bf16[128,1024]{1,0:T(8,128)(2,1)}, bf...) custom-call(s32[2]{0:T(128)} %pad_add_fusion.refs_0_, ...), custom_call_target="tpu_custom_call" | custom-call | tf_op jit(solution)/shard_map/pallas_call | solution.py:800
  127.9 4.7 %collective-permute-start.14 = (f32[224,128]{1,0:T(8,128)}, f32[224,128]{1,0:T(8,128)S(1)}, u32[]{:S(2)}, u32[]{:S(2)}) collective-permute-start(f32[224,128]{1,0:T(8,128)} %get-tuple-element.88), channel_id=1, source_target_pairs={{0,4},{4,0},{8,12},{12,8},{16,20},{20,16},{24,28},{28,24},{1,5},{5... | collective-permute-start | bytes 344072 | tf_op jit(solution)/shard_map/ppermute | solution.py:35
  132.6 4.5 %collective-permute-start.15 = (f32[224,128]{1,0:T(8,128)}, f32[224,128]{1,0:T(8,128)S(1)}, u32[]{:S(2)}, u32[]{:S(2)}) collective-permute-start(f32[224,128]{1,0:T(8,128)} %get-tuple-element.89), channel_id=1, source_target_pairs={{0,8},{4,12},{8,0},{12,4},{16,24},{20,28},{24,16},{28,20},{1,9},{5... | collective-permute-start | bytes 344072 | tf_op jit(solution)/shard_map/ppermute | solution.py:35
  137.2 0.7 copy-done.41
  138.1 1.4 collective-permute-start.19
  139.4 1.5 collective-permute-start.27
  141.0 0.7 collective-permute-start.26
  141.7 3.2 %collective-permute-start.25 = (bf16[128,256]{1,0:T(8,128)(2,1)S(1)}, bf16[128,256]{1,0:T(8,128)(2,1)S(1)}, u32[]{:S(2)}, u32[]{:S(2)}) collective-permute-start(bf16[128,256]{1,0:T(8,128)(2,1)S(1)} %copy-done.42), channel_id=1, source_target_pairs={{0,4},{4,0},{8,12},{12,8},{16,20},{20,16},{24,28},{28,24},{1,5},{5... | collective-permute-start | bytes 196616 | tf_op jit(solution)/shard_map/ppermute | solution.py:35
  146.3 2.2 %edges.1 = (f32[128,64]{1,0:T(8,128)}, f32[8,4352]{1,0:T(8,128)}, f32[8,4544]{1,0:T(8,128)}) custom-call(s32[2]{0:T(128)} %pad_add_fusion.refs_0_, f32[224,128]{1,0:T(8,128)} %get-tuple-element.87.refs_1_, f32[224,128]{1,0:T(8,128)} %copy-done.24, f32[224,128]{1,0:T(8,128)} %copy-done.25, f32[224,128]{1,0:T(8,128)} %copy-done.26), custom_call_target="tpu_custom_call" | custom-call | tf_op jit(solution)/shard_map/edges/pallas_call | solution.py:258
  148.4 1.0 collective-permute-start.21
  149.4 1.3 collective-permute-start.17
  150.7 1.9 %collective-permute-done.25 = bf16[128,256]{1,0:T(8,128)(2,1)S(1)} collective-permute-done((bf16[128,256]{1,0:T(8,128)(2,1)S(1)}, bf16[128,256]{1,0:T(8,128)(2,1)S(1)}, u32[]{:S(2)}, u32[]{:S(2)}) %collective-permute-start.25) | collective-permute-done | bytes 65568 | tf_op jit(solution)/shard_map/ppermute | solution.py:35
  152.6 5.3 %collective-permute-start.18 = (f32[8,4544]{1,0:T(8,128)}, f32[8,4544]{1,0:T(8,128)S(1)}, u32[]{:S(2)}, u32[]{:S(2)}) collective-permute-start(f32[8,4544]{1,0:T(8,128)} %get-tuple-element.92), channel_id=1, source_target_pairs={{0,16},{4,20},{8,24},{12,28},{16,0},{20,4},{24,8},{28,12},{1,17},{... | collective-permute-start | bytes 436232 | tf_op jit(solution)/shard_map/ppermute | solution.py:35
  158.0 0.8 copy-done.27
  158.8 0.7 copy.32
  159.5 3.2 %collective-permute-start.22 = (bf16[128,1024]{1,0:T(8,128)(2,1)S(1)}, bf16[128,1024]{1,0:T(8,128)(2,1)S(1)}, u32[]{:S(2)}, u32[]{:S(2)}) collective-permute-start(bf16[128,1024]{1,0:T(8,128)(2,1)S(1)} %copy-done.37), channel_id=1, source_target_pairs={{0,4},{4,0},{8,12},{12,8},{16,20},{20,16},{24,28},{28,24},{1,5},{5... | collective-permute-start | bytes 786440 | tf_op jit(solution)/shard_map/ppermute | solution.py:35
  162.7 0.8 collective-permute-done.18
  163.5 5.4 %collective-permute-start.23 = (bf16[128,1024]{1,0:T(8,128)(2,1)S(1)}, bf16[128,1024]{1,0:T(8,128)(2,1)S(1)}, u32[]{:S(2)}, u32[]{:S(2)}) collective-permute-start(bf16[128,1024]{1,0:T(8,128)(2,1)S(1)} %copy-done.35), channel_id=1, source_target_pairs={{0,8},{4,12},{8,0},{12,4},{16,24},{20,28},{24,16},{28,20},{1,9},{5... | collective-permute-start | bytes 786440 | tf_op jit(solution)/shard_map/ppermute | solution.py:35
  169.6 1.6 collective-permute-start.29
  171.5 1.8 collective-permute-done.23.refs_11_
  173.2 3.0 %collective-permute-done.24.refs_12_ = bf16[128,1024]{1,0:T(8,128)(2,1)S(1)} collective-permute-done((bf16[128,1024]{1,0:T(8,128)(2,1)S(1)}, bf16[128,1024]{1,0:T(8,128)(2,1)S(1)}, u32[]{:S(2)}, u32[]{:S(2)}) %collective-permute-start.24) | collective-permute-done | bytes 262176 | tf_op jit(solution)/shard_map/ppermute | solution.py:35
  176.9 4.7 %unpack.1 = (bf16[128,4096]{1,0:T(8,128)(2,1)}, bf16[128,4096]{1,0:T(8,128)(2,1)}, f32[4,4096]{1,0:T(4,128)}, f32[1,4096]{1,0:T(1,128)}, f32[3,64]{1,0:T(4,128)}) custom-call(s32[2]{0:T(128)} %pad_add_fusion.refs_0_, bf16[128,4096]{1,0:T(8,128)(2,1)} %refs_1_.14, bf16[128,4096]{1,0:T(8,128)(2,1)} %refs_2_.6, f32[8,4352]{1,0:T(8,128)} %copy-done.18, ...), custom_call_target="tpu_custom_call" | custom-call | tf_op jit(solution)/shard_map/unpack/pallas_call | solution.py:299
  181.6 1.3 slice_bitcast_fusion
  (143 shorter events, 8.9 us)
Async XLA Ops:
  2.6 13.6 %copy-start.29 = (f32[128,64]{0,1:T(8,128)S(1)}, f32[128,64]{0,1:T(8,128)}, u32[]{:S(2)}) copy-start(f32[128,64]{0,1:T(8,128)} %param.19) | copy-start | bytes 98308
  2.6 20.8 %collective-permute-start.3 = (bf16[176,512]{1,0:T(8,128)(2,1)}, bf16[176,512]{1,0:T(8,128)(2,1)S(1)}, u32[]{:S(2)}, u32[]{:S(2)}) collective-permute-start(bf16[176,512]{1,0:T(8,128)(2,1)} %get-tuple-element.70), channel_id=1, source_target_pairs={{0,4},{4,8},{8,12},{12,16},{16,20},{20,24},{24,28},{1,5},{5,9},{9,... | collective-permute-start | bytes 540680 | tf_op jit(solution)/shard_map/ppermute | solution.py:30
  7.6 17.1 %collective-permute-start.4 = (bf16[176,512]{1,0:T(8,128)(2,1)}, bf16[176,512]{1,0:T(8,128)(2,1)S(1)}, u32[]{:S(2)}, u32[]{:S(2)}) collective-permute-start(bf16[176,512]{1,0:T(8,128)(2,1)} %get-tuple-element.71), channel_id=1, source_target_pairs={{0,8},{4,12},{8,16},{12,20},{16,24},{20,28},{1,9},{5,13},{9,17},{1... | collective-permute-start | bytes 540680 | tf_op jit(solution)/shard_map/ppermute | solution.py:30
  11.1 13.6 %collective-permute-start.5 = (bf16[176,512]{1,0:T(8,128)(2,1)}, bf16[176,512]{1,0:T(8,128)(2,1)S(1)}, u32[]{:S(2)}, u32[]{:S(2)}) collective-permute-start(bf16[176,512]{1,0:T(8,128)(2,1)} %get-tuple-element.72), channel_id=1, source_target_pairs={{0,12},{4,16},{8,20},{12,24},{16,28},{1,13},{5,17},{9,21},{13,25},... | collective-permute-start | bytes 540680 | tf_op jit(solution)/shard_map/ppermute | solution.py:30
  20.6 10.2 %collective-permute-start = (bf16[128,1024]{1,0:T(8,128)(2,1)}, bf16[128,1024]{1,0:T(8,128)(2,1)S(1)}, u32[]{:S(2)}, u32[]{:S(2)}) collective-permute-start(bf16[128,1024]{1,0:T(8,128)(2,1)} %get-tuple-element.67), channel_id=1, source_target_pairs={{0,4},{4,0},{8,12},{12,8},{16,20},{20,16},{24,28},{28,24},{1,5},{5... | collective-permute-start | bytes 786440 | tf_op jit(solution)/shard_map/ppermute | solution.py:35
  22.1 8.6 %collective-permute-start.6 = (bf16[176,512]{1,0:T(8,128)(2,1)S(1)}, bf16[176,512]{1,0:T(8,128)(2,1)S(1)}, u32[]{:S(2)}, u32[]{:S(2)}) collective-permute-start(bf16[176,512]{1,0:T(8,128)(2,1)S(1)} %copy-done.39), channel_id=1, source_target_pairs={{0,16},{4,20},{8,24},{12,28},{1,17},{5,21},{9,25},{13,29},{2,18},{... | collective-permute-start | bytes 540680 | tf_op jit(solution)/shard_map/ppermute | solution.py:30
  23.4 30.6 %copy-start.3 = (bf16[176,512]{1,0:T(8,128)(2,1)}, bf16[176,512]{1,0:T(8,128)(2,1)S(1)}, u32[]{:S(2)}) copy-start(bf16[176,512]{1,0:T(8,128)(2,1)S(1)} %collective-permute-done.3.refs_6_.refs_7_) | copy-start | bytes 540676
  23.5 29.8 %collective-permute-start.7 = (bf16[128,1408]{1,0:T(8,128)(2,1)}, bf16[128,1408]{1,0:T(8,128)(2,1)S(1)}, u32[]{:S(2)}, u32[]{:S(2)}) collective-permute-start(bf16[128,1408]{1,0:T(8,128)(2,1)} %get-tuple-element.75), channel_id=1, source_target_pairs={{0,4},{4,0},{8,12},{12,8},{16,20},{20,16},{24,28},{28,24},{1,5},{5... | collective-permute-start | bytes 1081352 | tf_op jit(solution)/shard_map/ppermute | solution.py:35
  24.7 29.3 %copy-start.4 = (bf16[176,512]{1,0:T(8,128)(2,1)}, bf16[176,512]{1,0:T(8,128)(2,1)S(1)}, u32[]{:S(2)}) copy-start(bf16[176,512]{1,0:T(8,128)(2,1)S(1)} %collective-permute-done.4.refs_7_.refs_6_) | copy-start | bytes 540676
  24.7 28.5 %collective-permute-start.8 = (bf16[128,1408]{1,0:T(8,128)(2,1)}, bf16[128,1408]{1,0:T(8,128)(2,1)S(1)}, u32[]{:S(2)}, u32[]{:S(2)}) collective-permute-start(bf16[128,1408]{1,0:T(8,128)(2,1)} %get-tuple-element.76), channel_id=1, source_target_pairs={{0,8},{4,12},{8,0},{12,4},{16,24},{20,28},{24,16},{28,20},{1,9},{5... | collective-permute-start | bytes 1081352 | tf_op jit(solution)/shard_map/ppermute | solution.py:35
  24.7 29.3 %copy-start.5 = (bf16[176,512]{1,0:T(8,128)(2,1)}, bf16[176,512]{1,0:T(8,128)(2,1)S(1)}, u32[]{:S(2)}) copy-start(bf16[176,512]{1,0:T(8,128)(2,1)S(1)} %collective-permute-done.5.refs_8_.refs_5_) | copy-start | bytes 540676
  24.7 28.5 %collective-permute-start.9 = (bf16[128,1408]{1,0:T(8,128)(2,1)}, bf16[128,1408]{1,0:T(8,128)(2,1)S(1)}, u32[]{:S(2)}, u32[]{:S(2)}) collective-permute-start(bf16[128,1408]{1,0:T(8,128)(2,1)} %get-tuple-element.77), channel_id=1, source_target_pairs={{0,12},{4,8},{8,4},{12,0},{16,28},{20,24},{24,20},{28,16},{1,13},{... | collective-permute-start | bytes 1081352 | tf_op jit(solution)/shard_map/ppermute | solution.py:35
  30.8 23.3 %copy-start.6 = (bf16[176,512]{1,0:T(8,128)(2,1)}, bf16[176,512]{1,0:T(8,128)(2,1)S(1)}, u32[]{:S(2)}) copy-start(bf16[176,512]{1,0:T(8,128)(2,1)S(1)} %collective-permute-done.6.refs_9_.refs_4_) | copy-start | bytes 540676
  30.8 18.8 %collective-permute-start.1 = (bf16[128,1024]{1,0:T(8,128)(2,1)}, bf16[128,1024]{1,0:T(8,128)(2,1)S(1)}, u32[]{:S(2)}, u32[]{:S(2)}) collective-permute-start(bf16[128,1024]{1,0:T(8,128)(2,1)} %get-tuple-element.68), channel_id=1, source_target_pairs={{0,8},{4,12},{8,0},{12,4},{16,24},{20,28},{24,16},{28,20},{1,9},{5... | collective-permute-start | bytes 786440 | tf_op jit(solution)/shard_map/ppermute | solution.py:35
  30.9 23.2 %copy-start.7 = (bf16[128,1024]{1,0:T(8,128)(2,1)}, bf16[128,1024]{1,0:T(8,128)(2,1)S(1)}, u32[]{:S(2)}) copy-start(bf16[128,1024]{1,0:T(8,128)(2,1)S(1)} %collective-permute-done.refs_3_) | copy-start | bytes 786436
  30.9 22.3 %collective-permute-start.2 = (bf16[128,1024]{1,0:T(8,128)(2,1)}, bf16[128,1024]{1,0:T(8,128)(2,1)S(1)}, u32[]{:S(2)}, u32[]{:S(2)}) collective-permute-start(bf16[128,1024]{1,0:T(8,128)(2,1)} %get-tuple-element.69), channel_id=1, source_target_pairs={{0,12},{4,8},{8,4},{12,0},{16,28},{20,24},{24,20},{28,16},{1,13},{... | collective-permute-start | bytes 786440 | tf_op jit(solution)/shard_map/ppermute | solution.py:35
  61.3 30.5 %collective-permute-start.10 = (bf16[4,128,128]{2,1,0:T(8,128)(2,1)}, bf16[4,128,128]{2,1,0:T(8,128)(2,1)S(1)}, u32[]{:S(2)}, u32[]{:S(2)}) collective-permute-start(bf16[4,128,128]{2,1,0:T(8,128)(2,1)} %get-tuple-element.78), channel_id=1, source_target_pairs={{0,16},{4,20},{8,24},{12,28},{1,17},{5,21},{9,25},{13,29},{2,18},{... | collective-permute-start | bytes 393224 | tf_op jit(solution)/shard_map/ppermute | solution.py:30
  71.2 22.0 %collective-permute-start.12 = (bf16[4,128,128]{2,1,0:T(8,128)(2,1)}, bf16[4,128,128]{2,1,0:T(8,128)(2,1)S(1)}, u32[]{:S(2)}, u32[]{:S(2)}) collective-permute-start(bf16[4,128,128]{2,1,0:T(8,128)(2,1)} %get-tuple-element.80), channel_id=1, source_target_pairs={{0,16},{4,20},{8,24},{12,28},{1,17},{5,21},{9,25},{13,29},{2,18},{... | collective-permute-start | bytes 393224 | tf_op jit(solution)/shard_map/ppermute | solution.py:30
  72.5 22.0 %collective-permute-start.13 = (bf16[4,128,128]{2,1,0:T(8,128)(2,1)}, bf16[4,128,128]{2,1,0:T(8,128)(2,1)S(1)}, u32[]{:S(2)}, u32[]{:S(2)}) collective-permute-start(bf16[4,128,128]{2,1,0:T(8,128)(2,1)} %get-tuple-element.81), channel_id=1, source_target_pairs={{16,0},{20,4},{24,8},{28,12},{17,1},{21,5},{25,9},{29,13},{18,2},{... | collective-permute-start | bytes 393224 | tf_op jit(solution)/shard_map/ppermute | solution.py:30
  73.8 36.7 %collective-permute-start.11 = (bf16[4,128,128]{2,1,0:T(8,128)(2,1)S(1)}, bf16[4,128,128]{2,1,0:T(8,128)(2,1)S(1)}, u32[]{:S(2)}, u32[]{:S(2)}) collective-permute-start(bf16[4,128,128]{2,1,0:T(8,128)(2,1)S(1)} %copy-done.40), channel_id=1, source_target_pairs={{16,0},{20,4},{24,8},{28,12},{17,1},{21,5},{25,9},{29,13},{18,2},{... | collective-permute-start | bytes 393224 | tf_op jit(solution)/shard_map/ppermute | solution.py:30
  90.5 42.0 %collective-permute-start.34 = (bf16[128,512]{1,0:T(8,128)(2,1)}, bf16[128,512]{1,0:T(8,128)(2,1)S(1)}, u32[]{:S(2)}, u32[]{:S(2)}) collective-permute-start(bf16[128,512]{1,0:T(8,128)(2,1)} %get-tuple-element.117), channel_id=1, source_target_pairs={{16,0},{20,4},{24,8},{28,12},{17,1},{21,5},{25,9},{29,13},{18,2},{... | collective-permute-start | bytes 393224 | tf_op jit(solution)/shard_map/ppermute | solution.py:30
  91.8 18.6 %copy-start.20 = (bf16[4,128,128]{2,1,0:T(8,128)(2,1)}, bf16[4,128,128]{2,1,0:T(8,128)(2,1)S(1)}, u32[]{:S(2)}) copy-start(bf16[4,128,128]{2,1,0:T(8,128)(2,1)S(1)} %collective-permute-done.10.refs_19_) | copy-start | bytes 393220
  91.8 45.2 %collective-permute-start.33 = (bf16[128,512]{1,0:T(8,128)(2,1)}, bf16[128,512]{1,0:T(8,128)(2,1)S(1)}, u32[]{:S(2)}, u32[]{:S(2)}) collective-permute-start(bf16[128,512]{1,0:T(8,128)(2,1)} %get-tuple-element.116), channel_id=1, source_target_pairs={{12,0},{16,4},{20,8},{24,12},{28,16},{13,1},{17,5},{21,9},{25,13},... | collective-permute-start | bytes 393224 | tf_op jit(solution)/shard_map/ppermute | solution.py:30
  93.2 43.9 %collective-permute-start.32 = (bf16[128,512]{1,0:T(8,128)(2,1)}, bf16[128,512]{1,0:T(8,128)(2,1)S(1)}, u32[]{:S(2)}, u32[]{:S(2)}) collective-permute-start(bf16[128,512]{1,0:T(8,128)(2,1)} %get-tuple-element.115), channel_id=1, source_target_pairs={{8,0},{12,4},{16,8},{20,12},{24,16},{28,20},{9,1},{13,5},{17,9},{2... | collective-permute-start | bytes 393224 | tf_op jit(solution)/shard_map/ppermute | solution.py:30
  94.5 42.5 %collective-permute-start.31 = (bf16[128,512]{1,0:T(8,128)(2,1)}, bf16[128,512]{1,0:T(8,128)(2,1)S(1)}, u32[]{:S(2)}, u32[]{:S(2)}) collective-permute-start(bf16[128,512]{1,0:T(8,128)(2,1)} %get-tuple-element.114), channel_id=1, source_target_pairs={{4,0},{8,4},{12,8},{16,12},{20,16},{24,20},{28,24},{5,1},{9,5},{13... | collective-permute-start | bytes 393224 | tf_op jit(solution)/shard_map/ppermute | solution.py:30
  111.1 25.9 %copy-start.13 = (f32[128,512]{1,0:T(8,128)S(1)}, f32[128,512]{1,0:T(8,128)}, u32[]{:S(2)}) copy-start(f32[128,512]{1,0:T(8,128)} %get-tuple-element.113) | copy-start | bytes 786436
  127.9 13.1 %collective-permute-start.14 = (f32[224,128]{1,0:T(8,128)}, f32[224,128]{1,0:T(8,128)S(1)}, u32[]{:S(2)}, u32[]{:S(2)}) collective-permute-start(f32[224,128]{1,0:T(8,128)} %get-tuple-element.88), channel_id=1, source_target_pairs={{0,4},{4,0},{8,12},{12,8},{16,20},{20,16},{24,28},{28,24},{1,5},{5... | collective-permute-start | bytes 344072 | tf_op jit(solution)/shard_map/ppermute | solution.py:35
  132.6 9.2 %collective-permute-start.15 = (f32[224,128]{1,0:T(8,128)}, f32[224,128]{1,0:T(8,128)S(1)}, u32[]{:S(2)}, u32[]{:S(2)}) collective-permute-start(f32[224,128]{1,0:T(8,128)} %get-tuple-element.89), channel_id=1, source_target_pairs={{0,8},{4,12},{8,0},{12,4},{16,24},{20,28},{24,16},{28,20},{1,9},{5... | collective-permute-start | bytes 344072 | tf_op jit(solution)/shard_map/ppermute | solution.py:35
  137.1 22.4 %copy-start.37 = (bf16[128,1024]{1,0:T(8,128)(2,1)S(1)}, bf16[128,1024]{1,0:T(8,128)(2,1)}, u32[]{:S(2)}) copy-start(bf16[128,1024]{1,0:T(8,128)(2,1)} %get-tuple-element.98) | copy-start | bytes 786436
  137.9 7.7 %collective-permute-start.16 = (f32[224,128]{1,0:T(8,128)S(1)}, f32[224,128]{1,0:T(8,128)S(1)}, u32[]{:S(2)}, u32[]{:S(2)}) collective-permute-start(f32[224,128]{1,0:T(8,128)S(1)} %copy-done.41), channel_id=1, source_target_pairs={{0,12},{4,8},{8,4},{12,0},{16,28},{20,24},{24,20},{28,16},{1,13},{... | collective-permute-start | bytes 344072 | tf_op jit(solution)/shard_map/ppermute | solution.py:35
  138.1 30.8 %collective-permute-start.19 = (bf16[128,1024]{1,0:T(8,128)(2,1)S(1)}, bf16[128,1024]{1,0:T(8,128)(2,1)S(1)}, u32[]{:S(2)}, u32[]{:S(2)}) collective-permute-start(bf16[128,1024]{1,0:T(8,128)(2,1)S(1)} %copy-done.38), channel_id=1, source_target_pairs={{0,4},{4,0},{8,12},{12,8},{16,20},{20,16},{24,28},{28,24},{1,5},{5... | collective-permute-start | bytes 786440 | tf_op jit(solution)/shard_map/ppermute | solution.py:35
  139.4 9.0 %collective-permute-start.27 = (bf16[128,256]{1,0:T(8,128)(2,1)S(1)}, bf16[128,256]{1,0:T(8,128)(2,1)S(1)}, u32[]{:S(2)}, u32[]{:S(2)}) collective-permute-start(bf16[128,256]{1,0:T(8,128)(2,1)S(1)} %copy-done.44), channel_id=1, source_target_pairs={{0,12},{4,8},{8,4},{12,0},{16,28},{20,24},{24,20},{28,16},{1,13},{... | collective-permute-start | bytes 196616 | tf_op jit(solution)/shard_map/ppermute | solution.py:35
  141.0 8.5 %collective-permute-start.26 = (bf16[128,256]{1,0:T(8,128)(2,1)S(1)}, bf16[128,256]{1,0:T(8,128)(2,1)S(1)}, u32[]{:S(2)}, u32[]{:S(2)}) collective-permute-start(bf16[128,256]{1,0:T(8,128)(2,1)S(1)} %copy-done.43), channel_id=1, source_target_pairs={{0,8},{4,12},{8,0},{12,4},{16,24},{20,28},{24,16},{28,20},{1,9},{5... | collective-permute-start | bytes 196616 | tf_op jit(solution)/shard_map/ppermute | solution.py:35
  141.7 10.9 %collective-permute-start.25 = (bf16[128,256]{1,0:T(8,128)(2,1)S(1)}, bf16[128,256]{1,0:T(8,128)(2,1)S(1)}, u32[]{:S(2)}, u32[]{:S(2)}) collective-permute-start(bf16[128,256]{1,0:T(8,128)(2,1)S(1)} %copy-done.42), channel_id=1, source_target_pairs={{0,4},{4,0},{8,12},{12,8},{16,20},{20,16},{24,28},{28,24},{1,5},{5... | collective-permute-start | bytes 196616 | tf_op jit(solution)/shard_map/ppermute | solution.py:35
  145.6 24.0 %collective-permute-start.20 = (bf16[128,1024]{1,0:T(8,128)(2,1)S(1)}, bf16[128,1024]{1,0:T(8,128)(2,1)S(1)}, u32[]{:S(2)}, u32[]{:S(2)}) collective-permute-start(bf16[128,1024]{1,0:T(8,128)(2,1)S(1)} %copy-done.36), channel_id=1, source_target_pairs={{0,8},{4,12},{8,0},{12,4},{16,24},{20,28},{24,16},{28,20},{1,9},{5... | collective-permute-start | bytes 786440 | tf_op jit(solution)/shard_map/ppermute | solution.py:35
  146.3 11.6 %copy-start.28 = (bf16[128,256]{1,0:T(8,128)(2,1)S(1)}, bf16[128,256]{1,0:T(8,128)(2,1)}, u32[]{:S(2)}) copy-start(bf16[128,256]{1,0:T(8,128)(2,1)} %get-tuple-element.102) | copy-start | bytes 196612
  146.3 17.3 %copy-start.35 = (bf16[128,1024]{1,0:T(8,128)(2,1)S(1)}, bf16[128,1024]{1,0:T(8,128)(2,1)}, u32[]{:S(2)}) copy-start(bf16[128,1024]{1,0:T(8,128)(2,1)} %get-tuple-element.99) | copy-start | bytes 786436
  148.4 21.2 %collective-permute-start.21 = (bf16[128,1024]{1,0:T(8,128)(2,1)S(1)}, bf16[128,1024]{1,0:T(8,128)(2,1)S(1)}, u32[]{:S(2)}, u32[]{:S(2)}) collective-permute-start(bf16[128,1024]{1,0:T(8,128)(2,1)S(1)} %copy-done.33), channel_id=1, source_target_pairs={{0,12},{4,8},{8,4},{12,0},{16,28},{20,24},{24,20},{28,16},{1,13},{... | collective-permute-start | bytes 786440 | tf_op jit(solution)/shard_map/ppermute | solution.py:35
  149.4 10.1 %collective-permute-start.17 = (f32[8,4352]{1,0:T(8,128)}, f32[8,4352]{1,0:T(8,128)S(1)}, u32[]{:S(2)}, u32[]{:S(2)}) collective-permute-start(f32[8,4352]{1,0:T(8,128)} %get-tuple-element.91), channel_id=1, source_target_pairs={{4,0},{8,4},{12,8},{16,12},{20,16},{24,20},{28,24},{5,1},{9,5},{13... | collective-permute-start | bytes 417800 | tf_op jit(solution)/shard_map/ppermute | solution.py:30
  152.6 10.9 %collective-permute-start.18 = (f32[8,4544]{1,0:T(8,128)}, f32[8,4544]{1,0:T(8,128)S(1)}, u32[]{:S(2)}, u32[]{:S(2)}) collective-permute-start(f32[8,4544]{1,0:T(8,128)} %get-tuple-element.92), channel_id=1, source_target_pairs={{0,16},{4,20},{8,24},{12,28},{16,0},{20,4},{24,8},{28,12},{1,17},{... | collective-permute-start | bytes 436232 | tf_op jit(solution)/shard_map/ppermute | solution.py:35
  157.9 11.0 %copy-start.34 = (bf16[128,1024]{1,0:T(8,128)(2,1)S(1)}, bf16[128,1024]{1,0:T(8,128)(2,1)}, u32[]{:S(2)}) copy-start(bf16[128,1024]{1,0:T(8,128)(2,1)} %get-tuple-element.100) | copy-start | bytes 786436
  157.9 11.0 %copy-start.19 = (f32[8,4544]{1,0:T(8,128)S(1)}, f32[8,4544]{1,0:T(8,128)}, u32[]{:S(2)}) copy-start(f32[8,4544]{1,0:T(8,128)} %get-tuple-element.92) | copy-start | bytes 436228
  159.5 11.7 %collective-permute-start.22 = (bf16[128,1024]{1,0:T(8,128)(2,1)S(1)}, bf16[128,1024]{1,0:T(8,128)(2,1)S(1)}, u32[]{:S(2)}, u32[]{:S(2)}) collective-permute-start(bf16[128,1024]{1,0:T(8,128)(2,1)S(1)} %copy-done.37), channel_id=1, source_target_pairs={{0,4},{4,0},{8,12},{12,8},{16,20},{20,16},{24,28},{28,24},{1,5},{5... | collective-permute-start | bytes 786440 | tf_op jit(solution)/shard_map/ppermute | solution.py:35
  163.5 9.7 %collective-permute-start.23 = (bf16[128,1024]{1,0:T(8,128)(2,1)S(1)}, bf16[128,1024]{1,0:T(8,128)(2,1)S(1)}, u32[]{:S(2)}, u32[]{:S(2)}) collective-permute-start(bf16[128,1024]{1,0:T(8,128)(2,1)S(1)} %copy-done.35), channel_id=1, source_target_pairs={{0,8},{4,12},{8,0},{12,4},{16,24},{20,28},{24,16},{28,20},{1,9},{5... | collective-permute-start | bytes 786440 | tf_op jit(solution)/shard_map/ppermute | solution.py:35
  168.9 7.3 %collective-permute-start.24 = (bf16[128,1024]{1,0:T(8,128)(2,1)S(1)}, bf16[128,1024]{1,0:T(8,128)(2,1)S(1)}, u32[]{:S(2)}, u32[]{:S(2)}) collective-permute-start(bf16[128,1024]{1,0:T(8,128)(2,1)S(1)} %copy-done.34), channel_id=1, source_target_pairs={{0,12},{4,8},{8,4},{12,0},{16,28},{20,24},{24,20},{28,16},{1,13},{... | collective-permute-start | bytes 786440 | tf_op jit(solution)/shard_map/ppermute | solution.py:35
  169.6 13.3 %collective-permute-start.30 = (f32[136,256]{1,0:T(8,128)S(1)}, f32[136,256]{1,0:T(8,128)S(1)}, u32[]{:S(2)}, u32[]{:S(2)}) collective-permute-start(f32[136,256]{1,0:T(8,128)S(1)} %pad_maximum_fusion), channel_id=1, source_target_pairs={{0,3},{1,2},{2,1},{3,0},{4,7},{5,6},{6,5},{7,4},{8,11},{9,10},{10,... | collective-permute-start | bytes 417800 | tf_op jit(solution)/shard_map/ppermute | solution.py:35
  169.6 13.3 %collective-permute-start.29 = (f32[136,256]{1,0:T(8,128)S(1)}, f32[136,256]{1,0:T(8,128)S(1)}, u32[]{:S(2)}, u32[]{:S(2)}) collective-permute-start(f32[136,256]{1,0:T(8,128)S(1)} %pad_maximum_fusion), channel_id=1, source_target_pairs={{0,2},{1,3},{2,0},{3,1},{4,6},{5,7},{6,4},{7,5},{8,10},{9,11},{10,... | collective-permute-start | bytes 417800 | tf_op jit(solution)/shard_map/ppermute | solution.py:35
  171.2 11.7 %collective-permute-start.28 = (f32[136,256]{1,0:T(8,128)S(1)}, f32[136,256]{1,0:T(8,128)S(1)}, u32[]{:S(2)}, u32[]{:S(2)}) collective-permute-start(f32[136,256]{1,0:T(8,128)S(1)} %pad_maximum_fusion), channel_id=1, source_target_pairs={{0,1},{1,0},{2,3},{3,2},{4,5},{5,4},{6,7},{7,6},{8,9},{9,8},{10,11... | collective-permute-start | bytes 417800 | tf_op jit(solution)/shard_map/ppermute | solution.py:35
  (32 other events, 103.2 us)
